TPU v7x, 128 devices: a whole 4x4x4 slice. The times are simulated.
128 devices in a mesh: seq: 16 (over x, y_hi, core), filt: 8 (over y_lo, z).
Axes of the slice: x: 4, y: 4 (y_hi: 2, y_lo: 2; y = y_hi * 2 + y_lo), z: 4, core: 2. Of those that a mesh axis runs over, the one named last changes fastest.
Arguments:
- tokens: bfloat16 [43008, 1024], P('seq', 'filt'), may hold values from -6 to 6
- conv_weight: bfloat16 [2, 3, 1024, 1024], P(None, None, None, 'filt'), may hold values from -0.109375 to 0.109375
- conv_bias: float32 [2, 1024], P(None, 'filt'), may hold values from -3 to 3
- mix_weight: bfloat16 [2, 1024, 1024], P(None, None, 'filt'), may hold values from -0.1875 to 0.1875
- mix_bias: float32 [2, 1024], P(None, 'filt'), may hold values from -3 to 3
- norm_gain: float32 [2, 1024], replicated, may hold values from 0.1 to 1.9
Outputs:
- layer_output: bfloat16 [43008, 1024], P('seq', 'filt')
All inputs are finite; a program needn't handle non-finite values.
Results may differ from a plain program's by a relative error of at most 0.014.
Values may be sent and summed in bfloat16 or wider, within the bound.
No kernel may reach another device: no remote copies, remote signals or barrier semaphores. Data moves between devices by JAX's collectives and lax.ppermute only.
A program may use at most 64 MiB of HBM per device.

v0:
```python
import jax
import jax.numpy as jnp
from jax import lax
from jax.sharding import PartitionSpec as P

LAYERS = 2


def passed_along(block, axis, distance):
    devices = range(lax.axis_size(axis))
    route = [(i - distance, i) for i in devices if i - distance in devices]
    return lax.ppermute(block, axis, route)


def normalize(values, gain_row):
    widened = values.astype(jnp.float32)
    scale = lax.rsqrt(jnp.mean(widened * widened, axis=-1, keepdims=True) + 1e-06)
    return (widened * scale * gain_row).astype(jnp.bfloat16)


def product(left, right):
    return jnp.dot(left, right, preferred_element_type=jnp.float32)


def per_device(tokens, conv_weight, conv_bias, mix_weight, mix_bias, norm_gain):
    current = tokens
    for block_index in range(LAYERS):
        stride = 2**block_index
        conv_local = conv_weight[block_index]
        mix_local = mix_weight[block_index]
        gathered = lax.all_gather(current, "filt", axis=1, tiled=True)
        normed = normalize(gathered, norm_gain[block_index])
        hidden = product(normed, conv_local[1])
        earlier = passed_along(normed, "seq", stride)
        following = passed_along(normed, "seq", -stride)
        hidden = hidden + product(earlier, conv_local[0]) + product(following, conv_local[2])
        hidden = hidden + conv_bias[block_index]
        activated = jax.nn.gelu(hidden, approximate=False).astype(jnp.bfloat16)
        mixed = product(lax.all_gather(activated, "filt", axis=1, tiled=True), mix_local)
        current = (current.astype(jnp.float32) + mixed + mix_bias[block_index]).astype(jnp.bfloat16)
    return current


def solution(mesh):
    in_specs = (
        P("seq", "filt"),
        P(None, None, None, "filt"),
        P(None, "filt"),
        P(None, None, "filt"),
        P(None, "filt"),
        P(),
    )
    out_specs = P("seq", "filt")
    return jax.shard_map(
        per_device, mesh=mesh, in_specs=in_specs, out_specs=out_specs, check_vma=False
    )
```

profile of v0, /device:TPU:1, one launch (start us, length us, event | category | flops | bytes accessed | tf_op | source)
XLA Modules:
  0.0 702.7 jit_solution(6063370070618525827)
XLA Ops:
  6.5 0.0 all-gather.5.cloned.1.call-start
  6.5 0.7 all-gather.5.cloned.1.call-update
  7.3 0.0 all-gather.7.cloned.1.call-start
  7.3 0.8 fusion.50
  8.1 72.7 %all-gather.5.cloned.1.call-done = bf16[2688,1024]{1,0:T(8,128)(2,1)} async-done(((bf16[2688,128]{1,0:T(8,128)(2,1)}), bf16[2688,1024]{1,0:T(8,128)(2,1)}) %all-gather.5.cloned.1.call-update) | async-done | bytes 5505040 | tf_op jit(solution)/shard_map/all_gather | solution.py:31
  80.8 0.0 copy-start
  80.8 3.9 fusion
  84.7 0.3 copy-done
  85.0 0.0 copy-start.5
  85.0 0.0 copy-start.2
  85.0 1.3 fusion.2
  86.3 7.9 %collective-permute-start = (bf16[2688,1024]{1,0:T(8,128)(2,1)S(1)}, bf16[2688,1024]{1,0:T(8,128)(2,1)S(1)}, u32[]{:S(2)}, u32[]{:S(2)}) collective-permute-start(bf16[2688,1024]{1,0:T(8,128)(2,1)S(1)} %fusion.2), channel_id=1, source_target_pairs={{0,8},{8,16},{16,24},{24,32},{32,40},{40,48},{48,56},{56,64},{64,7... | collective-permute-start | bytes 16515080 | tf_op jit(solution)/shard_map/ppermute | solution.py:12
  94.2 1.9 collective-permute-start.1
  96.1 0.0 copy-done.5
  96.1 0.0 copy-done.2
  96.1 1.6 fusion.40
  97.8 114.9 %collective-permute-done = bf16[2688,1024]{1,0:T(8,128)(2,1)S(1)} collective-permute-done((bf16[2688,1024]{1,0:T(8,128)(2,1)S(1)}, bf16[2688,1024]{1,0:T(8,128)(2,1)S(1)}, u32[]{:S(2)}, u32[]{:S(2)}) %collective-permute-start) | collective-permute-done | bytes 5505056 | tf_op jit(solution)/shard_map/ppermute | solution.py:12
  212.6 1.6 convolution_add_fusion.5
  214.2 0.0 collective-permute-done.1
  214.3 0.0 copy-start.6
  214.3 0.0 copy-start.3
  214.3 0.0 copy-start.7
  214.3 5.1 fusion.14
  219.4 0.0 all-gather.7.cloned.1.call-update
  219.4 0.0 all-gather.9.cloned.1.call-start
  219.5 0.0 copy-done.6
  219.5 70.5 %all-gather.7.cloned.1.call-done = bf16[2688,1024]{1,0:T(8,128)(2,1)} async-done(((bf16[2688,128]{1,0:T(8,128)(2,1)}), bf16[2688,1024]{1,0:T(8,128)(2,1)}) %all-gather.7.cloned.1.call-update) | async-done | bytes 5505040 | tf_op jit(solution)/shard_map/all_gather | solution.py:39
  290.0 0.0 copy-done.3
  290.0 0.0 copy-done.7
  290.0 5.0 fusion.11
  295.1 0.0 all-gather.9.cloned.1.call-update
  295.1 0.2 all-gather.11.cloned.1.call-start
  295.3 72.3 %all-gather.9.cloned.1.call-done = bf16[2688,1024]{1,0:T(8,128)(2,1)} async-done(((bf16[2688,128]{1,0:T(8,128)(2,1)}), bf16[2688,1024]{1,0:T(8,128)(2,1)}) %all-gather.9.cloned.1.call-update) | async-done | bytes 5505040 | tf_op jit(solution)/shard_map/all_gather | solution.py:31
  367.7 3.9 fusion.3
  371.5 0.3 copy-done.1
  371.8 1.3 fusion.5
  373.2 4.6 collective-permute-start.2
  377.7 1.3 collective-permute-start.3
  379.0 1.6 fusion.35
  380.6 229.0 %collective-permute-done.2 = bf16[2688,1024]{1,0:T(8,128)(2,1)S(1)} collective-permute-done((bf16[2688,1024]{1,0:T(8,128)(2,1)S(1)}, bf16[2688,1024]{1,0:T(8,128)(2,1)S(1)}, u32[]{:S(2)}, u32[]{:S(2)}) %collective-permute-start.2) | collective-permute-done | bytes 5505056 | tf_op jit(solution)/shard_map/ppermute | solution.py:12
  609.7 1.7 convolution_add_fusion.2
  611.4 0.0 collective-permute-done.3
  611.4 0.0 copy-start.4
  611.4 5.1 fusion.17
  616.5 0.0 all-gather.11.cloned.1.call-update
  616.5 74.6 %all-gather.11.cloned.1.call-done = bf16[2688,1024]{1,0:T(8,128)(2,1)} async-done(((bf16[2688,128]{1,0:T(8,128)(2,1)}), bf16[2688,1024]{1,0:T(8,128)(2,1)}) %all-gather.11.cloned.1.call-update) | async-done | bytes 5505040 | tf_op jit(solution)/shard_map/all_gather | solution.py:39
  691.1 0.0 copy-done.4
  691.1 5.0 fusion.10
  (5 shorter events, 0.0 us)
Async XLA Ops:
  6.5 74.3 %all-gather.5.cloned.1.call-start = ((), (), s32[]{:S(2)}) async-start(), calls=%async_computation | async-start | bytes 6193152 | tf_op jit(solution)/shard_map/all_gather | solution.py:31
  7.3 282.8 %all-gather.7.cloned.1.call-start = ((), (), s32[]{:S(2)}) async-start(), calls=%async_computation.1 | async-start | bytes 6193152 | tf_op jit(solution)/shard_map/all_gather | solution.py:39
  80.8 4.2 copy-start
  85.0 11.1 %copy-start.5 = (f32[2,128]{1,0:T(2,128)S(1)}, f32[2,128]{1,0:T(2,128)}, u32[]{:S(2)}) copy-start(f32[2,128]{1,0:T(2,128)} %param.8) | copy-start | bytes 3076
  85.0 11.2 %copy-start.2 = (bf16[2,3,1024,128]{3,2,1,0:T(8,128)(2,1)S(1)}, bf16[2,3,1024,128]{3,2,1,0:T(8,128)(2,1)}, u32[]{:S(2)}) copy-start(bf16[2,3,1024,128]{3,2,1,0:T(8,128)(2,1)} %param.7) | copy-start | bytes 4718596
  86.3 126.4 %collective-permute-start = (bf16[2688,1024]{1,0:T(8,128)(2,1)S(1)}, bf16[2688,1024]{1,0:T(8,128)(2,1)S(1)}, u32[]{:S(2)}, u32[]{:S(2)}) collective-permute-start(bf16[2688,1024]{1,0:T(8,128)(2,1)S(1)} %fusion.2), channel_id=1, source_target_pairs={{0,8},{8,16},{16,24},{24,32},{32,40},{40,48},{48,56},{56,64},{64,7... | collective-permute-start | bytes 16515080 | tf_op jit(solution)/shard_map/ppermute | solution.py:12
  94.2 120.1 %collective-permute-start.1 = (bf16[2688,1024]{1,0:T(8,128)(2,1)S(1)}, bf16[2688,1024]{1,0:T(8,128)(2,1)S(1)}, u32[]{:S(2)}, u32[]{:S(2)}) collective-permute-start(bf16[2688,1024]{1,0:T(8,128)(2,1)S(1)} %fusion.2), channel_id=1, source_target_pairs={{8,0},{16,8},{24,16},{32,24},{40,32},{48,40},{56,48},{64,56},{72,6... | collective-permute-start | bytes 16515080 | tf_op jit(solution)/shard_map/ppermute | solution.py:12
  214.3 5.2 copy-start.6
  214.3 75.8 %copy-start.3 = (bf16[2688,128]{1,0:T(8,128)(2,1)S(1)}, bf16[2688,128]{1,0:T(8,128)(2,1)}, u32[]{:S(2)}) copy-start(bf16[2688,128]{1,0:T(8,128)(2,1)} %param.6) | copy-start | bytes 2064388
  214.3 75.7 %copy-start.7 = (bf16[2,1024,128]{2,1,0:T(8,128)(2,1)S(1)}, bf16[2,1024,128]{2,1,0:T(8,128)(2,1)}, u32[]{:S(2)}) copy-start(bf16[2,1024,128]{2,1,0:T(8,128)(2,1)} %param.9) | copy-start | bytes 1572868
  219.4 148.2 %all-gather.9.cloned.1.call-start = ((), (), s32[]{:S(2)}) async-start(), calls=%async_computation.2 | async-start | bytes 6193152 | tf_op jit(solution)/shard_map/all_gather | solution.py:31
  295.1 396.0 %all-gather.11.cloned.1.call-start = ((), (), s32[]{:S(2)}) async-start(), calls=%async_computation.3 | async-start | bytes 6193152 | tf_op jit(solution)/shard_map/all_gather | solution.py:39
  367.7 4.2 copy-start.1
  373.2 236.5 %collective-permute-start.2 = (bf16[2688,1024]{1,0:T(8,128)(2,1)S(1)}, bf16[2688,1024]{1,0:T(8,128)(2,1)S(1)}, u32[]{:S(2)}, u32[]{:S(2)}) collective-permute-start(bf16[2688,1024]{1,0:T(8,128)(2,1)S(1)} %fusion.5), channel_id=1, source_target_pairs={{0,16},{8,24},{16,32},{24,40},{32,48},{40,56},{48,64},{56,72},{64,... | collective-permute-start | bytes 16515080 | tf_op jit(solution)/shard_map/ppermute | solution.py:12
  377.7 233.6 %collective-permute-start.3 = (bf16[2688,1024]{1,0:T(8,128)(2,1)S(1)}, bf16[2688,1024]{1,0:T(8,128)(2,1)S(1)}, u32[]{:S(2)}, u32[]{:S(2)}) collective-permute-start(bf16[2688,1024]{1,0:T(8,128)(2,1)S(1)} %fusion.5), channel_id=1, source_target_pairs={{16,0},{24,8},{32,16},{40,24},{48,32},{56,40},{64,48},{72,56},{80,... | collective-permute-start | bytes 16515080 | tf_op jit(solution)/shard_map/ppermute | solution.py:12
  611.4 79.8 %copy-start.4 = (bf16[2688,128]{1,0:T(8,128)(2,1)S(1)}, bf16[2688,128]{1,0:T(8,128)(2,1)}, u32[]{:S(2)}) copy-start(bf16[2688,128]{1,0:T(8,128)(2,1)} %fusion.11) | copy-start | bytes 2064388
Sparse Core Ops, SparseCore 0:
  8.9 71.8 all-gather.4
  219.6 70.4 all-gather.6
  295.2 72.4 all-gather.8
  616.6 74.4 all-gather.10
where the time goes:
time: 706 us; the launch traced here: 703 us
  waiting for transfers between devices  635 us (90%)
  matrix products  26.8 us (4%)
  starting transfers between devices  16 us (2%)
  between operations  13.3 us (2%)
  other arithmetic  10.4 us (1%)
    ppermute x4, waiting for transfers between devices, passed_along(): return lax.ppermute(block, axis, route)  344 us
    all_gather x2, waiting for transfers between devices, per_device(): lax.all_gather(activated, 'filt', axis=1, tiled=True)  145 us
    all_gather x2, waiting for transfers between devices, per_device(): gathered = lax.all_gather(current, 'filt', axis=1, tiled=True)  145 us
    dot_general x8, matrix products, product(): return jnp.dot(left, right, preferred_element_type=jnp.float32)  26.8 us
    ppermute x4, starting transfers between devices, passed_along(): return lax.ppermute(block, axis, route)  15.7 us
  transfers between devices with their start and end apart: 8, of which 6 were waited for; matrix products, arithmetic and copies ran while one was open for 1% of the time, Pallas kernels for 0%

commit v1 on v0

v1 whole, which is shorter than its diff:
```python
import functools

import jax
import jax.numpy as jnp
from jax import lax
from jax.experimental import pallas as pl
from jax.experimental.pallas import tpu as pltpu
from jax.sharding import PartitionSpec as P

LAYERS = 2
C = 1024
BLOCKS = 16
LANES = 128
SHARDS = 8
RES = 24
ROWS = BLOCKS * RES
EXTRA = 16
AXES = ("seq", "filt")


def coords(i):
    z, i = i % 4, i // 4
    yl, i = i % 2, i // 2
    c, i = i % 2, i // 2
    yh, x = i % 2, i // 2
    return x, yh * 2 + yl, z, c


def linear(x, y, z, c):
    x, y, z = x % 4, y % 4, z % 4
    return (((x * 2 + y // 2) * 2 + c) * 2 + y % 2) * 4 + z


def route(step):
    return [(i, linear(*step(*coords(i)))) for i in range(128)]


Z_AWAY = route(lambda x, y, z, c: (x, y, z + 1 - 2 * c, c))
Z_BACK = route(lambda x, y, z, c: (x, y, z - 1 + 2 * c, c))
Y_SIDE = route(lambda x, y, z, c: (x, y + 1 - 2 * c, z, c))
SWAP = route(lambda x, y, z, c: (x, y, z, 1 - c))


def send(block, path):
    return lax.ppermute(block, AXES, path)


def three_parts(v):
    hi = v.astype(jnp.bfloat16).astype(jnp.float32)
    mid = (v - hi).astype(jnp.bfloat16).astype(jnp.float32)
    lo = v - hi - mid
    return [hi, mid, lo]


def prepare_kernel(where_ref, tokens_ref, conv_ref, mix_ref, conv_bias_ref, mix_bias_ref, padded_ref, *rest):
    own, (zeros, bias, sems) = rest[:LAYERS], rest[LAYERS:]
    core = where_ref[0]
    length = tokens_ref.shape[0]
    moves = [(tokens_ref, padded_ref.at[pl.ds(0, length)])]
    for layer in range(LAYERS):
        moves.append((conv_ref.at[layer, 2 * core], own[layer].at[pl.ds(0, C)]))
    copies = [pltpu.make_async_copy(a, b, sems.at[i]) for i, (a, b) in enumerate(moves)]
    for copy in copies:
        copy.start()
    for layer in range(LAYERS):
        second = own[layer].at[pl.ds(C, C)]

        @pl.when(core == 0)
        def _(layer=layer, second=second):
            pltpu.make_async_copy(conv_ref.at[layer, 1], second, sems.at[5 + layer]).start()

        @pl.when(core == 1)
        def _(layer=layer, second=second):
            pltpu.make_async_copy(mix_ref.at[layer], second, sems.at[5 + layer]).start()

    zeros[...] = jnp.zeros_like(zeros)
    for layer in range(LAYERS):
        rows = three_parts(conv_bias_ref[layer:layer + 1, :]) + three_parts(mix_bias_ref[layer:layer + 1, :])
        rows.append(jnp.zeros((EXTRA - 6, LANES), jnp.float32))
        bias[layer] = jnp.concatenate(rows, axis=0).astype(jnp.bfloat16)
    late = [(zeros, padded_ref.at[pl.ds(length, 128 * RES - length)])]
    for layer in range(LAYERS):
        late.append((bias.at[layer], own[layer].at[pl.ds(2 * C, EXTRA)]))
    more = [pltpu.make_async_copy(a, b, sems.at[7 + i]) for i, (a, b) in enumerate(late)]
    for copy in more:
        copy.start()
    for copy in copies + more:
        copy.wait()
    for layer in range(LAYERS):
        pltpu.make_async_copy(mix_ref.at[layer], own[layer].at[pl.ds(C, C)], sems.at[5 + layer]).wait()


def prepare(where, tokens, conv, mix, conv_bias, mix_bias):
    anywhere = pl.BlockSpec(memory_space=pl.ANY)
    hbm = pl.BlockSpec(memory_space=pltpu.HBM)
    vmem = pl.BlockSpec(memory_space=pltpu.VMEM)
    half = jax.ShapeDtypeStruct((2 * C + EXTRA, LANES), jnp.bfloat16)
    return pl.pallas_call(
        prepare_kernel,
        out_shape=[jax.ShapeDtypeStruct((128 * RES, LANES), jnp.bfloat16)] + [half] * LAYERS,
        in_specs=[pl.BlockSpec(memory_space=pltpu.SMEM), hbm, hbm, hbm, vmem, vmem],
        out_specs=[anywhere] * (1 + LAYERS),
        scratch_shapes=[
            pltpu.VMEM((128 * RES - tokens.shape[0], LANES), jnp.bfloat16),
            pltpu.VMEM((LAYERS, EXTRA, LANES), jnp.bfloat16),
            pltpu.SemaphoreType.DMA((7 + 1 + LAYERS,)),
        ],
        compiler_params=pltpu.CompilerParams(vmem_limit_bytes=4 * 2**20),
        cost_estimate=pl.CostEstimate(flops=0, bytes_accessed=4 * 2**20, transcendentals=0),
        name="prepare",
    )(where, tokens, conv, mix, conv_bias, mix_bias)


def layer_kernel(layer, first, last, where_ref, x_ref, gain_ref, conv_ref, mix_ref, own_ref, *rest):
    mine, other = rest[:7], rest[7:14]
    out_ref = rest[14]
    w, bias, x, n, act, sems, bias_sems = rest[15:]
    core = where_ref[0]

    def strip(k):
        return pl.ds(k * LANES, LANES)

    def home(k):
        return pl.ds(pl.multiple_of(where_ref[1 + k] * LANES, LANES), LANES)

    for k in range(SHARDS):
        moves = []
        if k == 0:
            for t in range(3):
                moves.append((conv_ref.at[layer, t], t))
            moves.append((mix_ref.at[layer], 3))
            extra = own_ref
        else:
            for src, base in ((mine[k - 1], 2 * core), (other[k - 1], 2 - 2 * core)):
                for h in range(2):
                    moves.append((src.at[pl.ds(h * C, C)], base + h))
            extra = mine[k - 1]
        for src, t in moves:
            pltpu.make_async_copy(src, w.at[t, :, strip(k)], sems.at[t, k]).start()
        pltpu.make_async_copy(extra.at[pl.ds(2 * C, EXTRA)], bias.at[:, strip(k)], bias_sems.at[k]).start()

    def ready(t, k):
        pltpu.make_async_copy(mix_ref.at[layer], w.at[t, :, strip(k)], sems.at[t, k]).wait()

    if first:
        for b in range(BLOCKS):
            for f in range(SHARDS):
                x[b * RES:(b + 1) * RES, f * LANES:(f + 1) * LANES] = x_ref[b * SHARDS + f].astype(jnp.float32)
    else:
        x[...] = x_ref[...].astype(jnp.float32)
    wide = x[...]
    scale = lax.rsqrt(jnp.mean(wide * wide, axis=-1, keepdims=True) + 1e-06)
    n[...] = (wide * scale * gain_ref[layer:layer + 1, :]).astype(jnp.bfloat16)

    shift = RES * 2**layer
    width = 2 * LANES

    def bias_row(start, cols):
        parts = bias[:, cols].astype(jnp.float32)
        return parts[start:start + 1] + parts[start + 1:start + 2] + parts[start + 2:start + 3]

    for j in range(SHARDS // 2):
        cols = slice(j * width, (j + 1) * width)
        for k in (2 * j, 2 * j + 1):
            for t in range(3):
                ready(t, k)
            pltpu.make_async_copy(own_ref.at[pl.ds(2 * C, EXTRA)], bias.at[:, strip(k)], bias_sems.at[k]).wait()
        hidden = jnp.dot(n[...], w[1, :, cols], preferred_element_type=jnp.float32) + bias_row(0, cols)
        edge = jnp.zeros((shift, width), jnp.float32)
        earlier = jnp.dot(n[...], w[0, :, cols], preferred_element_type=jnp.float32)
        hidden = hidden + jnp.concatenate([edge, earlier[:ROWS - shift]], axis=0)
        later = jnp.dot(n[...], w[2, :, cols], preferred_element_type=jnp.float32)
        hidden = hidden + jnp.concatenate([later[shift:], edge], axis=0)
        done = (hidden * (1.0 + lax.erf(hidden * 0.7071067811865476)) * 0.5).astype(jnp.bfloat16)
        for h in range(2):
            act[:, home(2 * j + h)] = done[:, h * LANES:(h + 1) * LANES]

    for j in range(SHARDS // 2):
        cols = slice(j * width, (j + 1) * width)
        for k in (2 * j, 2 * j + 1):
            ready(3, k)
        mixed = jnp.dot(act[...], w[3, :, cols], preferred_element_type=jnp.float32) + bias_row(3, cols)
        for h in range(2):
            k = 2 * j + h
            total = (x[:, home(k)] + mixed[:, h * LANES:(h + 1) * LANES]).astype(jnp.bfloat16)
            if last:
                f = where_ref[1 + k]
                for b in range(BLOCKS):
                    out_ref[b * SHARDS + f] = total[b * RES:(b + 1) * RES]
            else:
                out_ref[:, home(k)] = total


def run_layer(layer, where, x, gain, conv, mix, own, mine, other):
    first, last = layer == 0, layer == LAYERS - 1
    anywhere = pl.BlockSpec(memory_space=pl.ANY)
    hbm = pl.BlockSpec(memory_space=pltpu.HBM)
    vmem = pl.BlockSpec(memory_space=pltpu.VMEM)
    out = (BLOCKS * SHARDS, RES, LANES) if last else (ROWS, C)
    return pl.pallas_call(
        functools.partial(layer_kernel, layer, first, last),
        out_shape=jax.ShapeDtypeStruct(out, jnp.bfloat16),
        in_specs=[pl.BlockSpec(memory_space=pltpu.SMEM), vmem, vmem, hbm, hbm] + [anywhere] * 15,
        out_specs=vmem,
        scratch_shapes=[
            pltpu.VMEM((4, C, C), jnp.bfloat16),
            pltpu.VMEM((EXTRA, C), jnp.bfloat16),
            pltpu.VMEM((ROWS, C), jnp.float32),
            pltpu.VMEM((ROWS, C), jnp.bfloat16),
            pltpu.VMEM((ROWS, C), jnp.bfloat16),
            pltpu.SemaphoreType.DMA((4, SHARDS)),
            pltpu.SemaphoreType.DMA((SHARDS,)),
        ],
        compiler_params=pltpu.CompilerParams(vmem_limit_bytes=20 * 2**20),
        cost_estimate=pl.CostEstimate(flops=8 * ROWS * C * C, bytes_accessed=9 * 2**20, transcendentals=ROWS * C),
        name=f"layer{layer}",
    )(where, x, gain, conv, mix, own, *mine, *other)


def per_device(tokens, conv_weight, conv_bias, mix_weight, mix_bias, norm_gain):
    seq, filt = lax.axis_index("seq"), lax.axis_index("filt")
    core = seq & 1
    z, yl = filt & 3, filt >> 2
    zs = [z, (z - 1 + 2 * core) & 3, (z + 1 - 2 * core) & 3, (z + 2) & 3]
    shards = [yl * 4 + v for v in zs] + [(1 - yl) * 4 + v for v in zs]
    where = jnp.stack([core] + shards).astype(jnp.int32)

    padded, *owns = prepare(where, tokens, conv_weight, mix_weight, conv_bias, mix_bias)
    x = lax.all_to_all(padded.reshape(128, RES, LANES), AXES, split_axis=0, concat_axis=0, tiled=True)

    gathered = []
    for layer in range(LAYERS):
        own = owns[layer]
        if layer > 0:
            own, x, near, far = lax.optimization_barrier((own, x, near, far))
            gathered[0][1][0], gathered[0][1][1] = near, far
        near = send(own, Z_AWAY)
        far = send(own, Z_BACK)
        beyond = send(near, Z_AWAY)
        same = [own, near, far, beyond]
        cross = [send(v, Y_SIDE) for v in same]
        mine = same[1:] + cross
        other_core = [send(v, SWAP) for v in mine]
        gathered.append((own, mine, other_core))

    for layer in range(LAYERS):
        own, mine, other = gathered[layer]
        order = [1, 0, 2, 3, 5, 4, 6]
        x = run_layer(layer, where, x, norm_gain, conv_weight, mix_weight, own, mine, [other[i] for i in order])
    y = lax.all_to_all(x, AXES, split_axis=0, concat_axis=0, tiled=True)
    return y.reshape(128 * RES, LANES)[:tokens.shape[0]]


def solution(mesh):
    in_specs = (
        P("seq", "filt"),
        P(None, None, None, "filt"),
        P(None, "filt"),
        P(None, None, "filt"),
        P(None, "filt"),
        P(),
    )
    out_specs = P("seq", "filt")
    return jax.shard_map(
        per_device, mesh=mesh, in_specs=in_specs, out_specs=out_specs, check_vma=False
    )
```

time: 706 us -> 129 us (0.18)
  waiting for transfers between devices: 635 us -> 17.4 us
  starting transfers between devices: 16 us -> 62.7 us
  matrix products: 26.8 us -> 0 us
  Pallas kernels: 0 us -> 22.4 us
  blocking collectives: 0 us -> 20.4 us
  between operations: 13.3 us -> 0.11 us
  other arithmetic: 10.4 us -> 0 us
    ppermute x4 -> x28, waiting for transfers between devices: 344 us -> 8.65 us  [send(): return lax.ppermute(block, AXES, path)]
    all_gather x4 -> x0, waiting for transfers between devices: 290 us -> none  [the longest x2 145 us: per_device(): lax.all_gather(activated, 'filt', axis=1, tiled=True)]
    ppermute x4 -> x28, starting transfers between devices: 15.7 us -> 55.2 us  [send(): return lax.ppermute(block, AXES, path)]
    dot_general x8 -> x0, matrix products: 26.8 us -> none  [product(): return jnp.dot(left, right, preferred_element_type=jnp.float32)]
    pallas_call x0 -> x3, Pallas kernels: none -> 22.4 us  [the longest x2 20.7 us: run_layer(): pl.pallas_call(functools.partial(layer_kernel, layer, first, last), out_s...]
    all_to_all x0 -> x1, blocking collectives: none -> 20.4 us  [per_device(): y = lax.all_to_all(x, AXES, split_axis=0, concat_axis=0, tiled=True)]
    all_to_all x0 -> x1, waiting for transfers between devices: none -> 8.77 us  [per_device(): lax.all_to_all(padded.reshape(128, RES, LANES), AXES, split_axis=0, conca...]
    reduce_sum x2 -> x0, other arithmetic: 7.71 us -> none  [normalize(): jnp.mean(widened * widened, axis=-1, keepdims=True) + 1e-06]
  transfers between devices with their start and end apart: 8 -> 29, of which waited for: 6 -> 7; matrix products, arithmetic and copies ran while one was open for 1% -> 0% of each run, Pallas kernels for 0% -> 7%
where the time goes in v1:
time: 129 us
  starting transfers between devices  62.7 us (49%)
  Pallas kernels  22.4 us (17%)
  blocking collectives  20.4 us (16%)
  waiting for transfers between devices  17.4 us (13%)
  local copies, waits for them, and re-layouts  5.92 us (5%)
    ppermute x28, starting transfers between devices, send(): return lax.ppermute(block, AXES, path)  55.2 us
    pallas_call x2, Pallas kernels, run_layer(): pl.pallas_call(functools.partial(layer_kernel, layer, first, last), out_s...  20.7 us
    all_to_all x1, blocking collectives, per_device(): y = lax.all_to_all(x, AXES, split_axis=0, concat_axis=0, tiled=True)  20.4 us
    all_to_all x1, waiting for transfers between devices, per_device(): lax.all_to_all(padded.reshape(128, RES, LANES), AXES, split_axis=0, conca...  8.77 us
    ppermute x28, waiting for transfers between devices, send(): return lax.ppermute(block, AXES, path)  8.65 us
    all_to_all x1, starting transfers between devices, per_device(): lax.all_to_all(padded.reshape(128, RES, LANES), AXES, split_axis=0, conca...  7.48 us
    unnamed x16, local copies, waits for them, and re-layouts  4.92 us
  transfers between devices with their start and end apart: 29, of which 7 were waited for; matrix products, arithmetic and copies ran while one was open for 0% of the time, Pallas kernels for 7%

profile of v1, /device:TPU:1, one launch (start us, length us, event | category | flops | bytes accessed | tf_op | source)
XLA Modules:
  0.0 129.0 jit_solution(12817352116608422323)
XLA Ops:
  0.0 0.1 stack.39.where_ref
  0.1 1.4 %copy-done = bf16[2,3,1024,128]{3,2,1,0:T(8,128)(2,1)S(1)} copy-done((bf16[2,3,1024,128]{3,2,1,0:T(8,128)(2,1)S(1)}, bf16[2,3,1024,128]{3,2,1,0:T(8,128)(2,1)}, u32[]{:S(2)}) %copy-start) | copy-done | bytes 1572888
  1.5 1.1 copy-done.2
  2.6 1.0 copy-done.3
  3.6 0.7 copy-done.5
  4.3 0.7 copy-done.6
  5.0 1.7 %prepare.1 = (bf16[3072,128]{1,0:T(8,128)(2,1)}, bf16[2064,128]{1,0:T(8,128)(2,1)}, bf16[2064,128]{1,0:T(8,128)(2,1)S(1)}) custom-call(s32[9]{0:T(128)S(1)} %stack.39.where_ref, bf16[2688,128]{1,0:T(8,128)(2,1)S(1)} %copy-done.2, bf16[2,3,1024,128]{3,2,1,0:T(8,128)(2,1)S(1)} %copy-done, bf16[2,1024,128]{2,1,0:T(8,128)(2,1)S(1)} %copy-done.3, ...), custom_call_target="tpu_custom_call" | custom-call | bytes 4194304 | tf_op jit(solution)/shard_map/prepare/pallas_call | solution.py:98
  6.7 4.7 %collective-permute-start = (bf16[2064,128]{1,0:T(8,128)(2,1)}, bf16[2064,128]{1,0:T(8,128)(2,1)}, u32[]{:S(2)}, u32[]{:S(2)}) collective-permute-start(bf16[2064,128]{1,0:T(8,128)(2,1)} %get-tuple-element.14.own_ref), channel_id=1, source_target_pairs={{0,1},{1,2},{2,3},{3,0},{4,5},{5,6},{6,7},{7,4},{8,11},{9,8},{10,9... | collective-permute-start | bytes 1585160 | tf_op jit(solution)/shard_map/ppermute | solution.py:45
  11.3 0.0 collective-permute-start.1
  11.3 2.7 %collective-permute-start.3 = (bf16[2064,128]{1,0:T(8,128)(2,1)}, bf16[2064,128]{1,0:T(8,128)(2,1)}, u32[]{:S(2)}, u32[]{:S(2)}) collective-permute-start(bf16[2064,128]{1,0:T(8,128)(2,1)} %get-tuple-element.14.own_ref), channel_id=1, source_target_pairs={{0,4},{1,5},{2,6},{3,7},{4,16},{5,17},{6,18},{7,19},{8,28},{9,29},... | collective-permute-start | bytes 1585160 | tf_op jit(solution)/shard_map/ppermute | solution.py:45
  14.1 7.5 %all-to-all-start = ((bf16[128,24,128]{2,1,0:T(8,128)(2,1)}), bf16[128,24,128]{2,1,0:T(8,128)(2,1)S(1)}, u32[]{:S(2)}, u32[]{:S(2)}) async-start(bf16[128,24,128]{2,1,0:T(8,128)(2,1)} %bitcast.9), calls=%async_computation | async-start | bytes 1572864 | tf_op jit(solution)/shard_map/all_to_all | solution.py:229
  21.6 0.7 collective-permute-done.rest_0_
  22.2 3.4 %collective-permute-start.2 = (bf16[2064,128]{1,0:T(8,128)(2,1)}, bf16[2064,128]{1,0:T(8,128)(2,1)}, u32[]{:S(2)}, u32[]{:S(2)}) collective-permute-start(bf16[2064,128]{1,0:T(8,128)(2,1)} %collective-permute-done.rest_0_), channel_id=1, source_target_pairs={{0,1},{1,2},{2,3},{3,0},{4,5},{5,6},{6,7},{7,4},{8,11},{9,8},{10,9... | collective-permute-start | bytes 1585160 | tf_op jit(solution)/shard_map/ppermute | solution.py:45
  25.7 2.9 %collective-permute-start.4 = (bf16[2064,128]{1,0:T(8,128)(2,1)}, bf16[2064,128]{1,0:T(8,128)(2,1)}, u32[]{:S(2)}, u32[]{:S(2)}) collective-permute-start(bf16[2064,128]{1,0:T(8,128)(2,1)} %collective-permute-done.rest_0_), channel_id=1, source_target_pairs={{0,4},{1,5},{2,6},{3,7},{4,16},{5,17},{6,18},{7,19},{8,28},{9,29},... | collective-permute-start | bytes 1585160 | tf_op jit(solution)/shard_map/ppermute | solution.py:45
  28.6 0.0 collective-permute-done.1.rest_1_
  28.6 0.6 collective-permute-start.5
  29.1 0.5 collective-permute-start.7
  29.7 8.8 %all-to-all-done.x_ref = bf16[128,24,128]{2,1,0:T(8,128)(2,1)S(1)} async-done(((bf16[128,24,128]{2,1,0:T(8,128)(2,1)}), bf16[128,24,128]{2,1,0:T(8,128)(2,1)S(1)}, u32[]{:S(2)}, u32[]{:S(2)}) %all-to-all-start) | async-done | bytes 786464 | tf_op jit(solution)/shard_map/all_to_all | solution.py:229
  38.4 0.3 collective-permute-done.2.rest_2_
  38.8 2.5 %collective-permute-start.10 = (bf16[2064,128]{1,0:T(8,128)(2,1)}, bf16[2064,128]{1,0:T(8,128)(2,1)S(1)}, u32[]{:S(2)}, u32[]{:S(2)}) collective-permute-start(bf16[2064,128]{1,0:T(8,128)(2,1)} %collective-permute-done.3.rest_3_), channel_id=1, source_target_pairs={{0,8},{1,9},{2,10},{3,11},{4,12},{5,13},{6,14},{7,15},{8,0},{9,1},... | collective-permute-start | bytes 1585160 | tf_op jit(solution)/shard_map/ppermute | solution.py:45
  41.2 0.0 collective-permute-done.4.rest_4_
  41.2 0.4 collective-permute-start.14
  41.6 2.1 %collective-permute-done.5.rest_5_ = bf16[2064,128]{1,0:T(8,128)(2,1)} collective-permute-done((bf16[2064,128]{1,0:T(8,128)(2,1)}, bf16[2064,128]{1,0:T(8,128)(2,1)}, u32[]{:S(2)}, u32[]{:S(2)}) %collective-permute-start.5) | collective-permute-done | bytes 528416 | tf_op jit(solution)/shard_map/ppermute | solution.py:45
  43.7 1.0 collective-permute-start.15
  44.8 2.2 %collective-permute-start.17 = (bf16[2064,128]{1,0:T(8,128)(2,1)S(1)}, bf16[2064,128]{1,0:T(8,128)(2,1)S(1)}, u32[]{:S(2)}, u32[]{:S(2)}) collective-permute-start(bf16[2064,128]{1,0:T(8,128)(2,1)S(1)} %get-tuple-element.18.own_ref), channel_id=1, source_target_pairs={{0,4},{1,5},{2,6},{3,7},{4,16},{5,17},{6,18},{7,19},{8,28},{9,29},... | collective-permute-start | bytes 1585160 | tf_op jit(solution)/shard_map/ppermute | solution.py:45
  47.0 0.7 collective-permute-start.6
  47.6 1.9 %collective-permute-start.9 = (bf16[2064,128]{1,0:T(8,128)(2,1)}, bf16[2064,128]{1,0:T(8,128)(2,1)S(1)}, u32[]{:S(2)}, u32[]{:S(2)}) collective-permute-start(bf16[2064,128]{1,0:T(8,128)(2,1)} %collective-permute-done.2.rest_2_), channel_id=1, source_target_pairs={{0,8},{1,9},{2,10},{3,11},{4,12},{5,13},{6,14},{7,15},{8,0},{9,1},... | collective-permute-start | bytes 1585160 | tf_op jit(solution)/shard_map/ppermute | solution.py:45
  49.5 1.1 collective-permute-done.14.rest_0_
  50.6 4.5 %collective-permute-start.12 = (bf16[2064,128]{1,0:T(8,128)(2,1)}, bf16[2064,128]{1,0:T(8,128)(2,1)S(1)}, u32[]{:S(2)}, u32[]{:S(2)}) collective-permute-start(bf16[2064,128]{1,0:T(8,128)(2,1)} %collective-permute-done.4.rest_4_), channel_id=1, source_target_pairs={{0,8},{1,9},{2,10},{3,11},{4,12},{5,13},{6,14},{7,15},{8,0},{9,1},... | collective-permute-start | bytes 1585160 | tf_op jit(solution)/shard_map/ppermute | solution.py:45
  55.1 1.8 %collective-permute-done.15.rest_1_ = bf16[2064,128]{1,0:T(8,128)(2,1)S(1)} collective-permute-done((bf16[2064,128]{1,0:T(8,128)(2,1)S(1)}, bf16[2064,128]{1,0:T(8,128)(2,1)S(1)}, u32[]{:S(2)}, u32[]{:S(2)}) %collective-permute-start.15) | collective-permute-done | bytes 528416 | tf_op jit(solution)/shard_map/ppermute | solution.py:45
  56.9 2.2 %collective-permute-start.16 = (bf16[2064,128]{1,0:T(8,128)(2,1)S(1)}, bf16[2064,128]{1,0:T(8,128)(2,1)S(1)}, u32[]{:S(2)}, u32[]{:S(2)}) collective-permute-start(bf16[2064,128]{1,0:T(8,128)(2,1)S(1)} %collective-permute-done.14.rest_0_), channel_id=1, source_target_pairs={{0,1},{1,2},{2,3},{3,0},{4,5},{5,6},{6,7},{7,4},{8,11},{9,8},{10,9... | collective-permute-start | bytes 1585160 | tf_op jit(solution)/shard_map/ppermute | solution.py:45
  59.2 2.8 %collective-permute-start.19 = (bf16[2064,128]{1,0:T(8,128)(2,1)S(1)}, bf16[2064,128]{1,0:T(8,128)(2,1)S(1)}, u32[]{:S(2)}, u32[]{:S(2)}) collective-permute-start(bf16[2064,128]{1,0:T(8,128)(2,1)S(1)} %collective-permute-done.15.rest_1_), channel_id=1, source_target_pairs={{0,4},{1,5},{2,6},{3,7},{4,16},{5,17},{6,18},{7,19},{8,28},{9,29},... | collective-permute-start | bytes 1585160 | tf_op jit(solution)/shard_map/ppermute | solution.py:45
  61.9 0.0 collective-permute-start.18
  62.0 3.3 %collective-permute-start.21 = (bf16[2064,128]{1,0:T(8,128)(2,1)S(1)}, bf16[2064,128]{1,0:T(8,128)(2,1)S(1)}, u32[]{:S(2)}, u32[]{:S(2)}) collective-permute-start(bf16[2064,128]{1,0:T(8,128)(2,1)S(1)} %collective-permute-done.15.rest_1_), channel_id=1, source_target_pairs={{0,8},{1,9},{2,10},{3,11},{4,12},{5,13},{6,14},{7,15},{8,0},{9,1},... | collective-permute-start | bytes 1585160 | tf_op jit(solution)/shard_map/ppermute | solution.py:45
  65.2 0.1 collective-permute-start.22
  65.3 0.0 collective-permute-done.16.rest_2_
  65.3 4.5 %collective-permute-start.13 = (bf16[2064,128]{1,0:T(8,128)(2,1)S(1)}, bf16[2064,128]{1,0:T(8,128)(2,1)S(1)}, u32[]{:S(2)}, u32[]{:S(2)}) collective-permute-start(bf16[2064,128]{1,0:T(8,128)(2,1)S(1)} %collective-permute-done.6.rest_6_), channel_id=1, source_target_pairs={{0,8},{1,9},{2,10},{3,11},{4,12},{5,13},{6,14},{7,15},{8,0},{9,1},... | collective-permute-start | bytes 1585160 | tf_op jit(solution)/shard_map/ppermute | solution.py:45
  69.9 1.3 %collective-permute-start.20 = (bf16[2064,128]{1,0:T(8,128)(2,1)S(1)}, bf16[2064,128]{1,0:T(8,128)(2,1)S(1)}, u32[]{:S(2)}, u32[]{:S(2)}) collective-permute-start(bf16[2064,128]{1,0:T(8,128)(2,1)S(1)} %collective-permute-done.16.rest_2_), channel_id=1, source_target_pairs={{0,4},{1,5},{2,6},{3,7},{4,16},{5,17},{6,18},{7,19},{8,28},{9,29},... | collective-permute-start | bytes 1585160 | tf_op jit(solution)/shard_map/ppermute | solution.py:45
  71.2 2.5 %collective-permute-done.18.rest_4_ = bf16[2064,128]{1,0:T(8,128)(2,1)S(1)} collective-permute-done((bf16[2064,128]{1,0:T(8,128)(2,1)S(1)}, bf16[2064,128]{1,0:T(8,128)(2,1)S(1)}, u32[]{:S(2)}, u32[]{:S(2)}) %collective-permute-start.18) | collective-permute-done | bytes 528416 | tf_op jit(solution)/shard_map/ppermute | solution.py:45
  73.8 7.4 %collective-permute-start.24 = (bf16[2064,128]{1,0:T(8,128)(2,1)S(1)}, bf16[2064,128]{1,0:T(8,128)(2,1)S(1)}, u32[]{:S(2)}, u32[]{:S(2)}) collective-permute-start(bf16[2064,128]{1,0:T(8,128)(2,1)S(1)} %collective-permute-done.17.rest_3_), channel_id=1, source_target_pairs={{0,8},{1,9},{2,10},{3,11},{4,12},{5,13},{6,14},{7,15},{8,0},{9,1},... | collective-permute-start | bytes 1585160 | tf_op jit(solution)/shard_map/ppermute | solution.py:45
  81.2 0.0 collective-permute-start.23
  81.2 0.5 collective-permute-start.25
  81.7 0.1 collective-permute-start.26
  81.8 5.1 %collective-permute-start.27 = (bf16[2064,128]{1,0:T(8,128)(2,1)S(1)}, bf16[2064,128]{1,0:T(8,128)(2,1)S(1)}, u32[]{:S(2)}, u32[]{:S(2)}) collective-permute-start(bf16[2064,128]{1,0:T(8,128)(2,1)S(1)} %collective-permute-done.20.rest_6_), channel_id=1, source_target_pairs={{0,8},{1,9},{2,10},{3,11},{4,12},{5,13},{6,14},{7,15},{8,0},{9,1},... | collective-permute-start | bytes 1585160 | tf_op jit(solution)/shard_map/ppermute | solution.py:45
  86.9 9.2 %layer0.1.x_ref = bf16[384,1024]{1,0:T(8,128)(2,1)S(1)} custom-call(s32[9]{0:T(128)S(1)} %stack.39.where_ref, bf16[128,24,128]{2,1,0:T(8,128)(2,1)S(1)} %all-to-all-done.x_ref, f32[2,1024]{1,0:T(2,128)S(1)} %copy-done.7, bf16[2,3,1024,128]{3,2,1,0:T(8,128)(2,1)S(1)} %copy-done.1, bf16[2,1024,128]{2,1,0:T(8,128)(2,1)S(1)} %copy-done.4, ...), custom_call_target="tpu_custom_call" | custom-call | flops 3221225472 | bytes 9437184 | tf_op jit(solution)/shard_map/layer0/pallas_call | solution.py:200
  96.1 11.6 %layer1.1 = bf16[128,24,128]{2,1,0:T(8,128)(2,1)S(1)} custom-call(s32[9]{0:T(128)S(1)} %stack.39.where_ref, bf16[384,1024]{1,0:T(8,128)(2,1)S(1)} %layer0.1.x_ref, f32[2,1024]{1,0:T(2,128)S(1)} %copy-done.7, bf16[2,3,1024,128]{3,2,1,0:T(8,128)(2,1)S(1)} %copy-done.1, bf16[2,1024,128]{2,1,0:T(8,128)(2,1)S(1)} %copy-done.4, ...), custom_call_target="tpu_custom_call" | custom-call | flops 3221225472 | bytes 9437184 | tf_op jit(solution)/shard_map/layer1/pallas_call | solution.py:200
  107.7 20.4 %all_to_all.10 = bf16[128,24,128]{2,1,0:T(8,128)(2,1)S(1)} all-to-all(bf16[128,24,128]{2,1,0:T(8,128)(2,1)S(1)} %layer1.1), channel_id=1, replica_groups=mesh['seq'=16,'filt'=8] {'seq','filt'}, dimensions={0} | all-to-all | bytes 1572864 | tf_op jit(solution)/shard_map/all_to_all | solution.py:250
  128.1 0.9 slice.8
  (32 shorter events, 0.1 us)
Async XLA Ops:
  0.1 1.4 %copy-start = (bf16[2,3,1024,128]{3,2,1,0:T(8,128)(2,1)S(1)}, bf16[2,3,1024,128]{3,2,1,0:T(8,128)(2,1)}, u32[]{:S(2)}) copy-start(bf16[2,3,1024,128]{3,2,1,0:T(8,128)(2,1)} %conv_ref.5) | copy-start | bytes 4718596
  1.5 1.1 copy-start.2
  2.6 1.0 copy-start.3
  3.6 0.7 copy-start.5
  4.3 0.7 copy-start.6
  5.0 81.9 %copy-start.1 = (bf16[2,3,1024,128]{3,2,1,0:T(8,128)(2,1)S(1)}, bf16[2,3,1024,128]{3,2,1,0:T(8,128)(2,1)}, u32[]{:S(2)}) copy-start(bf16[2,3,1024,128]{3,2,1,0:T(8,128)(2,1)} %conv_ref.5) | copy-start | bytes 4718596
  5.0 81.9 %copy-start.4 = (bf16[2,1024,128]{2,1,0:T(8,128)(2,1)S(1)}, bf16[2,1024,128]{2,1,0:T(8,128)(2,1)}, u32[]{:S(2)}) copy-start(bf16[2,1024,128]{2,1,0:T(8,128)(2,1)} %mix_ref.5) | copy-start | bytes 1572868
  5.0 81.9 %copy-start.7 = (f32[2,1024]{1,0:T(2,128)S(1)}, f32[2,1024]{1,0:T(2,128)}, u32[]{:S(2)}) copy-start(f32[2,1024]{1,0:T(2,128)} %gain_ref.3) | copy-start | bytes 24580
  6.7 15.6 %collective-permute-start = (bf16[2064,128]{1,0:T(8,128)(2,1)}, bf16[2064,128]{1,0:T(8,128)(2,1)}, u32[]{:S(2)}, u32[]{:S(2)}) collective-permute-start(bf16[2064,128]{1,0:T(8,128)(2,1)} %get-tuple-element.14.own_ref), channel_id=1, source_target_pairs={{0,1},{1,2},{2,3},{3,0},{4,5},{5,6},{6,7},{7,4},{8,11},{9,8},{10,9... | collective-permute-start | bytes 1585160 | tf_op jit(solution)/shard_map/ppermute | solution.py:45
  11.3 17.2 %collective-permute-start.1 = (bf16[2064,128]{1,0:T(8,128)(2,1)}, bf16[2064,128]{1,0:T(8,128)(2,1)}, u32[]{:S(2)}, u32[]{:S(2)}) collective-permute-start(bf16[2064,128]{1,0:T(8,128)(2,1)} %get-tuple-element.14.own_ref), channel_id=1, source_target_pairs={{0,3},{1,0},{2,1},{3,2},{4,7},{5,4},{6,5},{7,6},{8,9},{9,10},{10,1... | collective-permute-start | bytes 1585160 | tf_op jit(solution)/shard_map/ppermute | solution.py:45
  11.3 17.8 %collective-permute-start.3 = (bf16[2064,128]{1,0:T(8,128)(2,1)}, bf16[2064,128]{1,0:T(8,128)(2,1)}, u32[]{:S(2)}, u32[]{:S(2)}) collective-permute-start(bf16[2064,128]{1,0:T(8,128)(2,1)} %get-tuple-element.14.own_ref), channel_id=1, source_target_pairs={{0,4},{1,5},{2,6},{3,7},{4,16},{5,17},{6,18},{7,19},{8,28},{9,29},... | collective-permute-start | bytes 1585160 | tf_op jit(solution)/shard_map/ppermute | solution.py:45
  14.1 24.3 %all-to-all-start = ((bf16[128,24,128]{2,1,0:T(8,128)(2,1)}), bf16[128,24,128]{2,1,0:T(8,128)(2,1)S(1)}, u32[]{:S(2)}, u32[]{:S(2)}) async-start(bf16[128,24,128]{2,1,0:T(8,128)(2,1)} %bitcast.9), calls=%async_computation | async-start | bytes 1572864 | tf_op jit(solution)/shard_map/all_to_all | solution.py:229
  22.2 16.5 %collective-permute-start.2 = (bf16[2064,128]{1,0:T(8,128)(2,1)}, bf16[2064,128]{1,0:T(8,128)(2,1)}, u32[]{:S(2)}, u32[]{:S(2)}) collective-permute-start(bf16[2064,128]{1,0:T(8,128)(2,1)} %collective-permute-done.rest_0_), channel_id=1, source_target_pairs={{0,1},{1,2},{2,3},{3,0},{4,5},{5,6},{6,7},{7,4},{8,11},{9,8},{10,9... | collective-permute-start | bytes 1585160 | tf_op jit(solution)/shard_map/ppermute | solution.py:45
  25.7 15.6 %collective-permute-start.4 = (bf16[2064,128]{1,0:T(8,128)(2,1)}, bf16[2064,128]{1,0:T(8,128)(2,1)}, u32[]{:S(2)}, u32[]{:S(2)}) collective-permute-start(bf16[2064,128]{1,0:T(8,128)(2,1)} %collective-permute-done.rest_0_), channel_id=1, source_target_pairs={{0,4},{1,5},{2,6},{3,7},{4,16},{5,17},{6,18},{7,19},{8,28},{9,29},... | collective-permute-start | bytes 1585160 | tf_op jit(solution)/shard_map/ppermute | solution.py:45
  28.6 15.1 %collective-permute-start.5 = (bf16[2064,128]{1,0:T(8,128)(2,1)}, bf16[2064,128]{1,0:T(8,128)(2,1)}, u32[]{:S(2)}, u32[]{:S(2)}) collective-permute-start(bf16[2064,128]{1,0:T(8,128)(2,1)} %collective-permute-done.1.rest_1_), channel_id=1, source_target_pairs={{0,4},{1,5},{2,6},{3,7},{4,16},{5,17},{6,18},{7,19},{8,28},{9,29},... | collective-permute-start | bytes 1585160 | tf_op jit(solution)/shard_map/ppermute | solution.py:45
  29.1 15.6 %collective-permute-start.8 = (bf16[2064,128]{1,0:T(8,128)(2,1)}, bf16[2064,128]{1,0:T(8,128)(2,1)}, u32[]{:S(2)}, u32[]{:S(2)}) collective-permute-start(bf16[2064,128]{1,0:T(8,128)(2,1)} %collective-permute-done.rest_0_), channel_id=1, source_target_pairs={{0,8},{1,9},{2,10},{3,11},{4,12},{5,13},{6,14},{7,15},{8,0},{9,1},... | collective-permute-start | bytes 1585160 | tf_op jit(solution)/shard_map/ppermute | solution.py:45
  29.1 17.8 %collective-permute-start.7 = (bf16[2064,128]{1,0:T(8,128)(2,1)}, bf16[2064,128]{1,0:T(8,128)(2,1)}, u32[]{:S(2)}, u32[]{:S(2)}) collective-permute-start(bf16[2064,128]{1,0:T(8,128)(2,1)} %collective-permute-done.1.rest_1_), channel_id=1, source_target_pairs={{0,8},{1,9},{2,10},{3,11},{4,12},{5,13},{6,14},{7,15},{8,0},{9,1},... | collective-permute-start | bytes 1585160 | tf_op jit(solution)/shard_map/ppermute | solution.py:45
  38.8 8.9 %collective-permute-start.10 = (bf16[2064,128]{1,0:T(8,128)(2,1)}, bf16[2064,128]{1,0:T(8,128)(2,1)S(1)}, u32[]{:S(2)}, u32[]{:S(2)}) collective-permute-start(bf16[2064,128]{1,0:T(8,128)(2,1)} %collective-permute-done.3.rest_3_), channel_id=1, source_target_pairs={{0,8},{1,9},{2,10},{3,11},{4,12},{5,13},{6,14},{7,15},{8,0},{9,1},... | collective-permute-start | bytes 1585160 | tf_op jit(solution)/shard_map/ppermute | solution.py:45
  41.2 9.4 %collective-permute-start.14 = (bf16[2064,128]{1,0:T(8,128)(2,1)S(1)}, bf16[2064,128]{1,0:T(8,128)(2,1)S(1)}, u32[]{:S(2)}, u32[]{:S(2)}) collective-permute-start(bf16[2064,128]{1,0:T(8,128)(2,1)S(1)} %get-tuple-element.18.own_ref), channel_id=1, source_target_pairs={{0,1},{1,2},{2,3},{3,0},{4,5},{5,6},{6,7},{7,4},{8,11},{9,8},{10,9... | collective-permute-start | bytes 1585160 | tf_op jit(solution)/shard_map/ppermute | solution.py:45
  43.7 13.2 %collective-permute-start.15 = (bf16[2064,128]{1,0:T(8,128)(2,1)S(1)}, bf16[2064,128]{1,0:T(8,128)(2,1)S(1)}, u32[]{:S(2)}, u32[]{:S(2)}) collective-permute-start(bf16[2064,128]{1,0:T(8,128)(2,1)S(1)} %get-tuple-element.18.own_ref), channel_id=1, source_target_pairs={{0,3},{1,0},{2,1},{3,2},{4,7},{5,4},{6,5},{7,6},{8,9},{9,10},{10,1... | collective-permute-start | bytes 1585160 | tf_op jit(solution)/shard_map/ppermute | solution.py:45
  44.8 12.2 %collective-permute-start.17 = (bf16[2064,128]{1,0:T(8,128)(2,1)S(1)}, bf16[2064,128]{1,0:T(8,128)(2,1)S(1)}, u32[]{:S(2)}, u32[]{:S(2)}) collective-permute-start(bf16[2064,128]{1,0:T(8,128)(2,1)S(1)} %get-tuple-element.18.own_ref), channel_id=1, source_target_pairs={{0,4},{1,5},{2,6},{3,7},{4,16},{5,17},{6,18},{7,19},{8,28},{9,29},... | collective-permute-start | bytes 1585160 | tf_op jit(solution)/shard_map/ppermute | solution.py:45
  47.0 12.2 %collective-permute-start.6 = (bf16[2064,128]{1,0:T(8,128)(2,1)}, bf16[2064,128]{1,0:T(8,128)(2,1)S(1)}, u32[]{:S(2)}, u32[]{:S(2)}) collective-permute-start(bf16[2064,128]{1,0:T(8,128)(2,1)} %collective-permute-done.2.rest_2_), channel_id=1, source_target_pairs={{0,4},{1,5},{2,6},{3,7},{4,16},{5,17},{6,18},{7,19},{8,28},{9,29},... | collective-permute-start | bytes 1585160 | tf_op jit(solution)/shard_map/ppermute | solution.py:45
  47.6 14.3 %collective-permute-start.9 = (bf16[2064,128]{1,0:T(8,128)(2,1)}, bf16[2064,128]{1,0:T(8,128)(2,1)S(1)}, u32[]{:S(2)}, u32[]{:S(2)}) collective-permute-start(bf16[2064,128]{1,0:T(8,128)(2,1)} %collective-permute-done.2.rest_2_), channel_id=1, source_target_pairs={{0,8},{1,9},{2,10},{3,11},{4,12},{5,13},{6,14},{7,15},{8,0},{9,1},... | collective-permute-start | bytes 1585160 | tf_op jit(solution)/shard_map/ppermute | solution.py:45
  50.6 11.3 %collective-permute-start.12 = (bf16[2064,128]{1,0:T(8,128)(2,1)}, bf16[2064,128]{1,0:T(8,128)(2,1)S(1)}, u32[]{:S(2)}, u32[]{:S(2)}) collective-permute-start(bf16[2064,128]{1,0:T(8,128)(2,1)} %collective-permute-done.4.rest_4_), channel_id=1, source_target_pairs={{0,8},{1,9},{2,10},{3,11},{4,12},{5,13},{6,14},{7,15},{8,0},{9,1},... | collective-permute-start | bytes 1585160 | tf_op jit(solution)/shard_map/ppermute | solution.py:45
  56.9 8.3 %collective-permute-start.11 = (bf16[2064,128]{1,0:T(8,128)(2,1)}, bf16[2064,128]{1,0:T(8,128)(2,1)S(1)}, u32[]{:S(2)}, u32[]{:S(2)}) collective-permute-start(bf16[2064,128]{1,0:T(8,128)(2,1)} %collective-permute-done.5.rest_5_), channel_id=1, source_target_pairs={{0,8},{1,9},{2,10},{3,11},{4,12},{5,13},{6,14},{7,15},{8,0},{9,1},... | collective-permute-start | bytes 1585160 | tf_op jit(solution)/shard_map/ppermute | solution.py:45
  56.9 8.4 %collective-permute-start.16 = (bf16[2064,128]{1,0:T(8,128)(2,1)S(1)}, bf16[2064,128]{1,0:T(8,128)(2,1)S(1)}, u32[]{:S(2)}, u32[]{:S(2)}) collective-permute-start(bf16[2064,128]{1,0:T(8,128)(2,1)S(1)} %collective-permute-done.14.rest_0_), channel_id=1, source_target_pairs={{0,1},{1,2},{2,3},{3,0},{4,5},{5,6},{6,7},{7,4},{8,11},{9,8},{10,9... | collective-permute-start | bytes 1585160 | tf_op jit(solution)/shard_map/ppermute | solution.py:45
  59.2 10.7 %collective-permute-start.19 = (bf16[2064,128]{1,0:T(8,128)(2,1)S(1)}, bf16[2064,128]{1,0:T(8,128)(2,1)S(1)}, u32[]{:S(2)}, u32[]{:S(2)}) collective-permute-start(bf16[2064,128]{1,0:T(8,128)(2,1)S(1)} %collective-permute-done.15.rest_1_), channel_id=1, source_target_pairs={{0,4},{1,5},{2,6},{3,7},{4,16},{5,17},{6,18},{7,19},{8,28},{9,29},... | collective-permute-start | bytes 1585160 | tf_op jit(solution)/shard_map/ppermute | solution.py:45
  61.9 11.8 %collective-permute-start.18 = (bf16[2064,128]{1,0:T(8,128)(2,1)S(1)}, bf16[2064,128]{1,0:T(8,128)(2,1)S(1)}, u32[]{:S(2)}, u32[]{:S(2)}) collective-permute-start(bf16[2064,128]{1,0:T(8,128)(2,1)S(1)} %collective-permute-done.14.rest_0_), channel_id=1, source_target_pairs={{0,4},{1,5},{2,6},{3,7},{4,16},{5,17},{6,18},{7,19},{8,28},{9,29},... | collective-permute-start | bytes 1585160 | tf_op jit(solution)/shard_map/ppermute | solution.py:45
  62.0 19.2 %collective-permute-start.21 = (bf16[2064,128]{1,0:T(8,128)(2,1)S(1)}, bf16[2064,128]{1,0:T(8,128)(2,1)S(1)}, u32[]{:S(2)}, u32[]{:S(2)}) collective-permute-start(bf16[2064,128]{1,0:T(8,128)(2,1)S(1)} %collective-permute-done.15.rest_1_), channel_id=1, source_target_pairs={{0,8},{1,9},{2,10},{3,11},{4,12},{5,13},{6,14},{7,15},{8,0},{9,1},... | collective-permute-start | bytes 1585160 | tf_op jit(solution)/shard_map/ppermute | solution.py:45
  65.2 16.0 %collective-permute-start.22 = (bf16[2064,128]{1,0:T(8,128)(2,1)S(1)}, bf16[2064,128]{1,0:T(8,128)(2,1)S(1)}, u32[]{:S(2)}, u32[]{:S(2)}) collective-permute-start(bf16[2064,128]{1,0:T(8,128)(2,1)S(1)} %collective-permute-done.14.rest_0_), channel_id=1, source_target_pairs={{0,8},{1,9},{2,10},{3,11},{4,12},{5,13},{6,14},{7,15},{8,0},{9,1},... | collective-permute-start | bytes 1585160 | tf_op jit(solution)/shard_map/ppermute | solution.py:45
  65.3 16.4 %collective-permute-start.13 = (bf16[2064,128]{1,0:T(8,128)(2,1)S(1)}, bf16[2064,128]{1,0:T(8,128)(2,1)S(1)}, u32[]{:S(2)}, u32[]{:S(2)}) collective-permute-start(bf16[2064,128]{1,0:T(8,128)(2,1)S(1)} %collective-permute-done.6.rest_6_), channel_id=1, source_target_pairs={{0,8},{1,9},{2,10},{3,11},{4,12},{5,13},{6,14},{7,15},{8,0},{9,1},... | collective-permute-start | bytes 1585160 | tf_op jit(solution)/shard_map/ppermute | solution.py:45
  69.9 11.9 %collective-permute-start.20 = (bf16[2064,128]{1,0:T(8,128)(2,1)S(1)}, bf16[2064,128]{1,0:T(8,128)(2,1)S(1)}, u32[]{:S(2)}, u32[]{:S(2)}) collective-permute-start(bf16[2064,128]{1,0:T(8,128)(2,1)S(1)} %collective-permute-done.16.rest_2_), channel_id=1, source_target_pairs={{0,4},{1,5},{2,6},{3,7},{4,16},{5,17},{6,18},{7,19},{8,28},{9,29},... | collective-permute-start | bytes 1585160 | tf_op jit(solution)/shard_map/ppermute | solution.py:45
  73.8 22.3 %collective-permute-start.24 = (bf16[2064,128]{1,0:T(8,128)(2,1)S(1)}, bf16[2064,128]{1,0:T(8,128)(2,1)S(1)}, u32[]{:S(2)}, u32[]{:S(2)}) collective-permute-start(bf16[2064,128]{1,0:T(8,128)(2,1)S(1)} %collective-permute-done.17.rest_3_), channel_id=1, source_target_pairs={{0,8},{1,9},{2,10},{3,11},{4,12},{5,13},{6,14},{7,15},{8,0},{9,1},... | collective-permute-start | bytes 1585160 | tf_op jit(solution)/shard_map/ppermute | solution.py:45
  81.2 14.9 %collective-permute-start.23 = (bf16[2064,128]{1,0:T(8,128)(2,1)S(1)}, bf16[2064,128]{1,0:T(8,128)(2,1)S(1)}, u32[]{:S(2)}, u32[]{:S(2)}) collective-permute-start(bf16[2064,128]{1,0:T(8,128)(2,1)S(1)} %collective-permute-done.16.rest_2_), channel_id=1, source_target_pairs={{0,8},{1,9},{2,10},{3,11},{4,12},{5,13},{6,14},{7,15},{8,0},{9,1},... | collective-permute-start | bytes 1585160 | tf_op jit(solution)/shard_map/ppermute | solution.py:45
  81.2 14.9 %collective-permute-start.25 = (bf16[2064,128]{1,0:T(8,128)(2,1)S(1)}, bf16[2064,128]{1,0:T(8,128)(2,1)S(1)}, u32[]{:S(2)}, u32[]{:S(2)}) collective-permute-start(bf16[2064,128]{1,0:T(8,128)(2,1)S(1)} %collective-permute-done.19.rest_5_), channel_id=1, source_target_pairs={{0,8},{1,9},{2,10},{3,11},{4,12},{5,13},{6,14},{7,15},{8,0},{9,1},... | collective-permute-start | bytes 1585160 | tf_op jit(solution)/shard_map/ppermute | solution.py:45
  81.7 14.4 %collective-permute-start.26 = (bf16[2064,128]{1,0:T(8,128)(2,1)S(1)}, bf16[2064,128]{1,0:T(8,128)(2,1)S(1)}, u32[]{:S(2)}, u32[]{:S(2)}) collective-permute-start(bf16[2064,128]{1,0:T(8,128)(2,1)S(1)} %collective-permute-done.18.rest_4_), channel_id=1, source_target_pairs={{0,8},{1,9},{2,10},{3,11},{4,12},{5,13},{6,14},{7,15},{8,0},{9,1},... | collective-permute-start | bytes 1585160 | tf_op jit(solution)/shard_map/ppermute | solution.py:45
  81.8 14.3 %collective-permute-start.27 = (bf16[2064,128]{1,0:T(8,128)(2,1)S(1)}, bf16[2064,128]{1,0:T(8,128)(2,1)S(1)}, u32[]{:S(2)}, u32[]{:S(2)}) collective-permute-start(bf16[2064,128]{1,0:T(8,128)(2,1)S(1)} %collective-permute-done.20.rest_6_), channel_id=1, source_target_pairs={{0,8},{1,9},{2,10},{3,11},{4,12},{5,13},{6,14},{7,15},{8,0},{9,1},... | collective-permute-start | bytes 1585160 | tf_op jit(solution)/shard_map/ppermute | solution.py:45

commit v2 on v0

v2 whole, which is shorter than its diff:
```python
import functools

import jax
import jax.numpy as jnp
from jax import lax
from jax.experimental import pallas as pl
from jax.experimental.pallas import tpu as pltpu
from jax.sharding import PartitionSpec as P

LAYERS = 2
C = 1024
BLOCKS = 16
LANES = 128
SHARDS = 8
RES = 24
ROWS = BLOCKS * RES
EXTRA = 16
QUARTER = C // 4
PART = C + EXTRA
AXES = ("seq", "filt")


def coords(i):
    z, i = i % 4, i // 4
    yl, i = i % 2, i // 2
    c, i = i % 2, i // 2
    yh, x = i % 2, i // 2
    return x, yh * 2 + yl, z, c


def linear(x, y, z, c):
    x, y, z = x % 4, y % 4, z % 4
    return (((x * 2 + y // 2) * 2 + c) * 2 + y % 2) * 4 + z


def route(step):
    return [(i, linear(*step(*coords(i)))) for i in range(128)]


Z_AWAY = route(lambda x, y, z, c: (x, y, z + 1 - 2 * c, c))
Z_BACK = route(lambda x, y, z, c: (x, y, z - 1 + 2 * c, c))
Y_SIDE = route(lambda x, y, z, c: (x, y + 1 - 2 * c, z, c))
X_SIDE = route(lambda x, y, z, c: (x + 1 - 2 * c, y, z, c))
SWAP = route(lambda x, y, z, c: (x, y, z, 1 - c))


def send(block, path):
    return lax.ppermute(block, AXES, path)


def three_parts(v):
    hi = v.astype(jnp.bfloat16).astype(jnp.float32)
    mid = (v - hi).astype(jnp.bfloat16).astype(jnp.float32)
    lo = v - hi - mid
    return [hi, mid, lo]


def prepare_kernel(where_ref, tokens_ref, conv_ref, mix_ref, conv_bias_ref, mix_bias_ref, padded_ref, first_ref, second_ref, zeros, bias, sems):
    length = tokens_ref.shape[0]
    moves = [(tokens_ref, padded_ref.at[pl.ds(0, length)])]
    for i, part in enumerate((first_ref, second_ref)):
        rows = pl.ds(pl.multiple_of(where_ref[i] * QUARTER, QUARTER), QUARTER)
        for layer in range(LAYERS):
            for t in range(4):
                source = conv_ref.at[layer, t, rows] if t < 3 else mix_ref.at[layer, rows]
                moves.append((source, part.at[pl.ds(layer * PART + t * QUARTER, QUARTER)]))
    copies = [pltpu.make_async_copy(a, b, sems.at[i]) for i, (a, b) in enumerate(moves)]
    for copy in copies:
        copy.start()
    zeros[...] = jnp.zeros_like(zeros)
    for layer in range(LAYERS):
        rows = three_parts(conv_bias_ref[layer:layer + 1, :]) + three_parts(mix_bias_ref[layer:layer + 1, :])
        rows.append(jnp.zeros((EXTRA - 6, LANES), jnp.float32))
        bias[layer] = jnp.concatenate(rows, axis=0).astype(jnp.bfloat16)
    late = [(zeros, padded_ref.at[pl.ds(length, 128 * RES - length)])]
    for part in (first_ref, second_ref):
        for layer in range(LAYERS):
            late.append((bias.at[layer], part.at[pl.ds(layer * PART + C, EXTRA)]))
    more = [pltpu.make_async_copy(a, b, sems.at[len(moves) + i]) for i, (a, b) in enumerate(late)]
    for copy in more:
        copy.start()
    for copy in copies + more:
        copy.wait()


def prepare(where, tokens, conv, mix, conv_bias, mix_bias):
    anywhere = pl.BlockSpec(memory_space=pl.ANY)
    vmem = pl.BlockSpec(memory_space=pltpu.VMEM)
    part = jax.ShapeDtypeStruct((LAYERS * PART, LANES), jnp.bfloat16)
    return pl.pallas_call(
        prepare_kernel,
        out_shape=[jax.ShapeDtypeStruct((128 * RES, LANES), jnp.bfloat16), part, part],
        in_specs=[pl.BlockSpec(memory_space=pltpu.SMEM), anywhere, anywhere, anywhere, vmem, vmem],
        out_specs=[anywhere] * 3,
        scratch_shapes=[
            pltpu.VMEM((128 * RES - tokens.shape[0], LANES), jnp.bfloat16),
            pltpu.VMEM((LAYERS, EXTRA, LANES), jnp.bfloat16),
            pltpu.SemaphoreType.DMA((2 + 12 * LAYERS,)),
        ],
        compiler_params=pltpu.CompilerParams(vmem_limit_bytes=60 * 2**20),
        cost_estimate=pl.CostEstimate(flops=0, bytes_accessed=4 * 2**20, transcendentals=0),
        name="prepare",
    )(where, tokens, conv, mix, conv_bias, mix_bias)


def blocks_kernel(where_ref, x_ref, gain_ref, conv_ref, mix_ref, own_ref, *rest):
    parts = rest[:4 * (SHARDS - 1)]
    out_ref, w, mine, bias, x, normed, n, act, mixing, sems, mine_sems, bias_sems = rest[4 * (SHARDS - 1):]
    width = 2 * LANES

    def quarter(i):
        return pl.ds(pl.multiple_of(where_ref[i] * QUARTER, QUARTER), QUARTER)

    def home(k):
        return pl.ds(pl.multiple_of(where_ref[4 + k] * LANES, LANES), LANES)

    arriving = []
    for layer in range(LAYERS):
        layer_rows = pl.ds(layer * PART, PART)
        for k in range(SHARDS):
            if k == 0:
                moves = [
                    (conv_ref.at[layer], mine.at[layer, pl.ds(0, 3)], mine_sems.at[layer, 0]),
                    (mix_ref.at[layer], mine.at[layer, 3], mine_sems.at[layer, 1]),
                    (own_ref.at[pl.ds(layer * PART + C, EXTRA)], bias.at[layer], bias_sems.at[layer]),
                ]
            else:
                moves = []
                for i in range(4):
                    p = 4 * (k - 1) + i
                    moves.append((parts[p].at[layer_rows], w.at[p, layer_rows], sems.at[layer, p]))
            copies = [pltpu.make_async_copy(*move) for move in moves]
            for copy in copies:
                copy.start()
            arriving.append(copies)

    for b in range(BLOCKS):
        for f in range(SHARDS):
            x[b * RES:(b + 1) * RES, f * LANES:(f + 1) * LANES] = x_ref[b * SHARDS + f].astype(jnp.float32)

    for layer in range(LAYERS):
        base = layer * PART
        wide = x[...]
        scale = lax.rsqrt(jnp.mean(wide * wide, axis=-1, keepdims=True) + 1e-06)
        normed[...] = wide * scale * gain_ref[layer:layer + 1, :]
        shift = RES * 2**layer
        edge = jnp.zeros((shift, QUARTER), jnp.float32)
        for i in range(4):
            here = normed[:, quarter(i)]
            earlier = jnp.concatenate([edge, here[:ROWS - shift]], axis=0)
            later = jnp.concatenate([here[shift:], edge], axis=0)
            for t, rows in enumerate((earlier, here, later)):
                start = (3 * i + t) * QUARTER
                n[:, start:start + QUARTER] = rows.astype(jnp.bfloat16)

        def conv_column(k):
            if k == 0:
                return jnp.concatenate([mine[layer, t, quarter(i), :] for i in range(4) for t in range(3)], axis=0)
            return jnp.concatenate([w[4 * (k - 1) + i, base:base + 3 * QUARTER, :] for i in range(4)], axis=0)

        def mix_column(k):
            if k == 0:
                return jnp.concatenate([mine[layer, 3, quarter(i), :] for i in range(4)], axis=0)
            return jnp.concatenate([w[4 * (k - 1) + i, base + 3 * QUARTER:base + C, :] for i in range(4)], axis=0)

        def bias_row(k, start):
            rows = bias[layer] if k == 0 else w[4 * (k - 1), base + C:base + PART, :]
            rows = rows.astype(jnp.float32)
            return rows[start:start + 1] + rows[start + 1:start + 2] + rows[start + 2:start + 3]

        for j in range(SHARDS // 2):
            pair = (2 * j, 2 * j + 1)
            for k in pair:
                for copy in arriving[layer * SHARDS + k]:
                    copy.wait()
            taps = jnp.concatenate([conv_column(k) for k in pair], axis=1)
            hidden = jnp.dot(n[...], taps, preferred_element_type=jnp.float32)
            hidden = hidden + jnp.concatenate([bias_row(k, 0) for k in pair], axis=1)
            done = (hidden * (1.0 + lax.erf(hidden * 0.7071067811865476)) * 0.5).astype(jnp.bfloat16)
            for h, k in enumerate(pair):
                act[:, home(k)] = done[:, h * LANES:(h + 1) * LANES]

        for i in range(4):
            mixing[:, i * QUARTER:(i + 1) * QUARTER] = act[:, quarter(i)]

        for j in range(SHARDS // 2):
            pair = (2 * j, 2 * j + 1)
            mixed = jnp.dot(mixing[...], jnp.concatenate([mix_column(k) for k in pair], axis=1), preferred_element_type=jnp.float32)
            mixed = mixed + jnp.concatenate([bias_row(k, 3) for k in pair], axis=1)
            for h, k in enumerate(pair):
                total = x[:, home(k)] + mixed[:, h * LANES:(h + 1) * LANES]
                if layer == LAYERS - 1:
                    f = where_ref[4 + k]
                    for b in range(BLOCKS):
                        out_ref[b * SHARDS + f] = total[b * RES:(b + 1) * RES].astype(jnp.bfloat16)
                else:
                    x[:, home(k)] = total.astype(jnp.bfloat16).astype(jnp.float32)


def run_blocks(where, x, gain, conv, mix, own, parts):
    vmem = pl.BlockSpec(memory_space=pltpu.VMEM)
    anywhere = pl.BlockSpec(memory_space=pl.ANY)
    return pl.pallas_call(
        blocks_kernel,
        out_shape=jax.ShapeDtypeStruct((BLOCKS * SHARDS, RES, LANES), jnp.bfloat16),
        in_specs=[pl.BlockSpec(memory_space=pltpu.SMEM), vmem, vmem] + [anywhere] * (3 + len(parts)),
        out_specs=vmem,
        scratch_shapes=[
            pltpu.VMEM((len(parts), LAYERS * PART, LANES), jnp.bfloat16),
            pltpu.VMEM((LAYERS, 4, C, LANES), jnp.bfloat16),
            pltpu.VMEM((LAYERS, EXTRA, LANES), jnp.bfloat16),
            pltpu.VMEM((ROWS, C), jnp.float32),
            pltpu.VMEM((ROWS, C), jnp.float32),
            pltpu.VMEM((ROWS, 3 * C), jnp.bfloat16),
            pltpu.VMEM((ROWS, C), jnp.bfloat16),
            pltpu.VMEM((ROWS, C), jnp.bfloat16),
            pltpu.SemaphoreType.DMA((LAYERS, len(parts))),
            pltpu.SemaphoreType.DMA((LAYERS, 2)),
            pltpu.SemaphoreType.DMA((LAYERS,)),
        ],
        compiler_params=pltpu.CompilerParams(vmem_limit_bytes=32 * 2**20),
        cost_estimate=pl.CostEstimate(flops=16 * ROWS * C * C, bytes_accessed=18 * 2**20, transcendentals=2 * ROWS * C),
        name="blocks",
    )(where, x, gain, conv, mix, own, *parts)


def per_device(tokens, conv_weight, conv_bias, mix_weight, mix_bias, norm_gain):
    seq, filt = lax.axis_index("seq"), lax.axis_index("filt")
    core, parity = seq & 1, (seq >> 2) & 1
    z, yl = filt & 3, filt >> 2
    quarters = [2 * core + parity, 2 * core + 1 - parity, 2 - 2 * core + parity, 3 - 2 * core - parity]
    zs = [z, (z - 1 + 2 * core) & 3, (z + 1 - 2 * core) & 3, (z + 2) & 3]
    shards = [yl * 4 + v for v in zs] + [(1 - yl) * 4 + v for v in zs]
    where = jnp.stack(quarters + shards).astype(jnp.int32)

    padded, own, own2 = prepare(where, tokens, conv_weight, mix_weight, conv_bias, mix_bias)
    near, far = send(own, Z_AWAY), send(own, Z_BACK)
    cross = send(own, Y_SIDE)
    x = lax.all_to_all(padded.reshape(128, RES, LANES), AXES, split_axis=0, concat_axis=0, tiled=True)
    own2, x = lax.optimization_barrier((own2, x))
    near2, far2 = send(own2, Z_AWAY), send(own2, Z_BACK)
    cross2 = send(own2, Y_SIDE)
    beyond = send(near, Z_AWAY)
    cross_near, cross_far = send(near, Y_SIDE), send(far, Y_SIDE)
    beyond2 = send(beyond, X_SIDE)
    cross_beyond = send(beyond, Y_SIDE)
    cross_near2, cross_far2, cross_beyond2 = [send(v, X_SIDE) for v in (cross_near, cross_far, cross_beyond)]
    mine = [
        (near, near2), (far, far2), (beyond, beyond2),
        (cross, cross2), (cross_near, cross_near2), (cross_far, cross_far2), (cross_beyond, cross_beyond2),
    ]
    swapped = [[send(v, SWAP) for v in pair] for pair in mine]
    parts = []
    for k, i in enumerate([1, 0, 2, 3, 5, 4, 6]):
        parts += list(mine[k]) + swapped[i]
    x = run_blocks(where, x, norm_gain, conv_weight, mix_weight, own, parts)
    y = lax.all_to_all(x, AXES, split_axis=0, concat_axis=0, tiled=True)
    return y.reshape(128 * RES, LANES)[:tokens.shape[0]]


def solution(mesh):
    in_specs = (
        P("seq", "filt"),
        P(None, None, None, "filt"),
        P(None, "filt"),
        P(None, None, "filt"),
        P(None, "filt"),
        P(),
    )
    out_specs = P("seq", "filt")
    return jax.shard_map(
        per_device, mesh=mesh, in_specs=in_specs, out_specs=out_specs, check_vma=False
    )
```

time: 706 us -> 176 us (0.25)
  waiting for transfers between devices: 635 us -> 10.6 us
  Pallas kernels: 0 us -> 71.4 us
  starting transfers between devices: 16 us -> 67.3 us
  matrix products: 26.8 us -> 0 us
  blocking collectives: 0 us -> 24.6 us
  between operations: 13.3 us -> 0.1 us
  other arithmetic: 10.4 us -> 0 us
    ppermute x4 -> x28, waiting for transfers between devices: 344 us -> 10.5 us  [send(): return lax.ppermute(block, AXES, path)]
    all_gather x4 -> x0, waiting for transfers between devices: 290 us -> none  [the longest x2 145 us: per_device(): lax.all_gather(activated, 'filt', axis=1, tiled=True)]
    pallas_call x0 -> x2, Pallas kernels: none -> 71.4 us  [the longest x1 54.8 us: prepare(): pl.pallas_call(prepare_kernel, out_shape=[jax.ShapeDtypeStruct((128 * RES...]
    ppermute x4 -> x28, starting transfers between devices: 15.7 us -> 58.6 us  [send(): return lax.ppermute(block, AXES, path)]
    dot_general x8 -> x0, matrix products: 26.8 us -> none  [product(): return jnp.dot(left, right, preferred_element_type=jnp.float32)]
    all_to_all x0 -> x1, blocking collectives: none -> 24.6 us  [per_device(): y = lax.all_to_all(x, AXES, split_axis=0, concat_axis=0, tiled=True)]
    all_to_all x0 -> x1, starting transfers between devices: none -> 8.69 us  [per_device(): lax.all_to_all(padded.reshape(128, RES, LANES), AXES, split_axis=0, conca...]
    reduce_sum x2 -> x0, other arithmetic: 7.71 us -> none  [normalize(): jnp.mean(widened * widened, axis=-1, keepdims=True) + 1e-06]
  transfers between devices with their start and end apart: 8 -> 29, of which waited for: 6 -> 7; matrix products, arithmetic and copies ran while one was open for 1% -> 0% of each run, Pallas kernels for 0% -> 0%
where the time goes in v2:
time: 176 us
  Pallas kernels  71.4 us (41%)
  starting transfers between devices  67.3 us (38%)
  blocking collectives  24.6 us (14%)
  waiting for transfers between devices  10.6 us (6%)
    ppermute x28, starting transfers between devices, send(): return lax.ppermute(block, AXES, path)  58.6 us
    pallas_call x1, Pallas kernels, prepare(): pl.pallas_call(prepare_kernel, out_shape=[jax.ShapeDtypeStruct((128 * RES...  54.8 us
    all_to_all x1, blocking collectives, per_device(): y = lax.all_to_all(x, AXES, split_axis=0, concat_axis=0, tiled=True)  24.6 us
    pallas_call x1, Pallas kernels, run_blocks(): pl.pallas_call(blocks_kernel, out_shape=jax.ShapeDtypeStruct((BLOCKS * SH...  16.6 us
    ppermute x28, waiting for transfers between devices, send(): return lax.ppermute(block, AXES, path)  10.5 us
    all_to_all x1, starting transfers between devices, per_device(): lax.all_to_all(padded.reshape(128, RES, LANES), AXES, split_axis=0, conca...  8.69 us
  transfers between devices with their start and end apart: 29, of which 7 were waited for; matrix products, arithmetic and copies ran while one was open for 0% of the time, Pallas kernels for 0%

profile of v2, /device:TPU:1, one launch (start us, length us, event | category | flops | bytes accessed | tf_op | source)
XLA Modules:
  0.0 175.6 jit_solution(8185613959226211695)
XLA Ops:
  0.0 0.7 stack.51.where_ref
  0.7 54.8 %prepare.1 = (bf16[3072,128]{1,0:T(8,128)(2,1)}, bf16[2080,128]{1,0:T(8,128)(2,1)}, bf16[2080,128]{1,0:T(8,128)(2,1)}) custom-call(s32[12]{0:T(128)} %stack.51.where_ref, bf16[2688,128]{1,0:T(8,128)(2,1)} %tokens_ref.1, bf16[2,3,1024,128]{3,2,1,0:T(8,128)(2,1)} %conv_ref.3, bf16[2,1024,128]{2,1,0:T(8,128)(2,1)} %mix_ref.3, f32[2,128]{1,0:T(2,128)} %conv_bias_ref.1, ...), custom_call_target="tpu_custom_call" | custom-call | bytes 4194304 | tf_op jit(solution)/shard_map/prepare/pallas_call | solution.py:90
  55.5 0.0 copy-start.3
  55.5 3.6 %collective-permute-start.12 = (bf16[2080,128]{1,0:T(8,128)(2,1)}, bf16[2080,128]{1,0:T(8,128)(2,1)}, u32[]{:S(2)}, u32[]{:S(2)}) collective-permute-start(bf16[2080,128]{1,0:T(8,128)(2,1)} %get-tuple-element.13.own_ref), channel_id=1, source_target_pairs={{0,4},{1,5},{2,6},{3,7},{4,16},{5,17},{6,18},{7,19},{8,28},{9,29},... | collective-permute-start | bytes 1597448 | tf_op jit(solution)/shard_map/ppermute | solution.py:48
  59.1 1.6 collective-permute-start.2
  60.8 2.1 %collective-permute-start = (bf16[2080,128]{1,0:T(8,128)(2,1)}, bf16[2080,128]{1,0:T(8,128)(2,1)}, u32[]{:S(2)}, u32[]{:S(2)}) collective-permute-start(bf16[2080,128]{1,0:T(8,128)(2,1)} %get-tuple-element.13.own_ref), channel_id=1, source_target_pairs={{0,1},{1,2},{2,3},{3,0},{4,5},{5,6},{6,7},{7,4},{8,11},{9,8},{10,9... | collective-permute-start | bytes 1597448 | tf_op jit(solution)/shard_map/ppermute | solution.py:48
  62.9 8.7 %all-to-all-start = ((bf16[128,24,128]{2,1,0:T(8,128)(2,1)}), bf16[128,24,128]{2,1,0:T(8,128)(2,1)S(1)}, u32[]{:S(2)}, u32[]{:S(2)}) async-start(bf16[128,24,128]{2,1,0:T(8,128)(2,1)} %bitcast.14), calls=%async_computation | async-start | bytes 1572864 | tf_op jit(solution)/shard_map/all_to_all | solution.py:239
  71.6 0.0 collective-permute-done.12.rest_12_
  71.6 1.1 collective-permute-start.14
  72.8 0.2 collective-permute-done.2.rest_4_
  72.9 1.8 %collective-permute-start.18 = (bf16[2080,128]{1,0:T(8,128)(2,1)}, bf16[2080,128]{1,0:T(8,128)(2,1)}, u32[]{:S(2)}, u32[]{:S(2)}) collective-permute-start(bf16[2080,128]{1,0:T(8,128)(2,1)} %collective-permute-done.2.rest_4_), channel_id=1, source_target_pairs={{0,4},{1,5},{2,6},{3,7},{4,16},{5,17},{6,18},{7,19},{8,28},{9,29},... | collective-permute-start | bytes 1597448 | tf_op jit(solution)/shard_map/ppermute | solution.py:48
  74.7 6.8 %collective-permute-start.3 = (bf16[2080,128]{1,0:T(8,128)(2,1)}, bf16[2080,128]{1,0:T(8,128)(2,1)}, u32[]{:S(2)}, u32[]{:S(2)}) collective-permute-start(bf16[2080,128]{1,0:T(8,128)(2,1)} %collective-permute-done.2.rest_4_), channel_id=1, source_target_pairs={{0,8},{1,9},{2,10},{3,11},{4,12},{5,13},{6,14},{7,15},{8,0},{9,1},... | collective-permute-start | bytes 1597448 | tf_op jit(solution)/shard_map/ppermute | solution.py:48
  81.5 0.0 collective-permute-done.rest_0_
  81.5 3.0 %collective-permute-start.16 = (bf16[2080,128]{1,0:T(8,128)(2,1)}, bf16[2080,128]{1,0:T(8,128)(2,1)}, u32[]{:S(2)}, u32[]{:S(2)}) collective-permute-start(bf16[2080,128]{1,0:T(8,128)(2,1)} %collective-permute-done.rest_0_), channel_id=1, source_target_pairs={{0,4},{1,5},{2,6},{3,7},{4,16},{5,17},{6,18},{7,19},{8,28},{9,29},... | collective-permute-start | bytes 1597448 | tf_op jit(solution)/shard_map/ppermute | solution.py:48
  84.5 3.8 %collective-permute-start.8 = (bf16[2080,128]{1,0:T(8,128)(2,1)}, bf16[2080,128]{1,0:T(8,128)(2,1)}, u32[]{:S(2)}, u32[]{:S(2)}) collective-permute-start(bf16[2080,128]{1,0:T(8,128)(2,1)} %collective-permute-done.rest_0_), channel_id=1, source_target_pairs={{0,1},{1,2},{2,3},{3,0},{4,5},{5,6},{6,7},{7,4},{8,11},{9,8},{10,9... | collective-permute-start | bytes 1597448 | tf_op jit(solution)/shard_map/ppermute | solution.py:48
  88.3 0.1 all-to-all-done.x_ref
  88.4 0.7 collective-permute-start.6
  89.1 0.0 collective-permute-done.18.rest_20_
  89.1 0.7 collective-permute-start.13
  89.8 1.3 collective-permute-start.4
  91.1 2.4 %collective-permute-done.16.rest_16_ = bf16[2080,128]{1,0:T(8,128)(2,1)} collective-permute-done((bf16[2080,128]{1,0:T(8,128)(2,1)}, bf16[2080,128]{1,0:T(8,128)(2,1)}, u32[]{:S(2)}, u32[]{:S(2)}) %collective-permute-start.16) | collective-permute-done | bytes 532512 | tf_op jit(solution)/shard_map/ppermute | solution.py:48
  93.5 3.4 %collective-permute-start.1 = (bf16[2080,128]{1,0:T(8,128)(2,1)}, bf16[2080,128]{1,0:T(8,128)(2,1)S(1)}, u32[]{:S(2)}, u32[]{:S(2)}) collective-permute-start(bf16[2080,128]{1,0:T(8,128)(2,1)} %get-tuple-element.14), channel_id=1, source_target_pairs={{0,1},{1,2},{2,3},{3,0},{4,5},{5,6},{6,7},{7,4},{8,11},{9,8},{10,9... | collective-permute-start | bytes 1597448 | tf_op jit(solution)/shard_map/ppermute | solution.py:48
  96.9 2.2 %collective-permute-start.20 = (bf16[2080,128]{1,0:T(8,128)(2,1)}, bf16[2080,128]{1,0:T(8,128)(2,1)S(1)}, u32[]{:S(2)}, u32[]{:S(2)}) collective-permute-start(bf16[2080,128]{1,0:T(8,128)(2,1)} %collective-permute-done.18.rest_20_), channel_id=1, source_target_pairs={{0,32},{1,33},{2,34},{3,35},{4,36},{5,37},{6,38},{7,39},{8,104},{9... | collective-permute-start | bytes 1597448 | tf_op jit(solution)/shard_map/ppermute | solution.py:48
  99.1 0.0 collective-permute-done.6.rest_6_
  99.1 2.0 %collective-permute-start.19 = (bf16[2080,128]{1,0:T(8,128)(2,1)}, bf16[2080,128]{1,0:T(8,128)(2,1)S(1)}, u32[]{:S(2)}, u32[]{:S(2)}) collective-permute-start(bf16[2080,128]{1,0:T(8,128)(2,1)} %collective-permute-done.18.rest_20_), channel_id=1, source_target_pairs={{0,8},{1,9},{2,10},{3,11},{4,12},{5,13},{6,14},{7,15},{8,0},{9,1},... | collective-permute-start | bytes 1597448 | tf_op jit(solution)/shard_map/ppermute | solution.py:48
  101.1 2.5 %collective-permute-start.22 = (bf16[2080,128]{1,0:T(8,128)(2,1)}, bf16[2080,128]{1,0:T(8,128)(2,1)S(1)}, u32[]{:S(2)}, u32[]{:S(2)}) collective-permute-start(bf16[2080,128]{1,0:T(8,128)(2,1)} %collective-permute-done.16.rest_16_), channel_id=1, source_target_pairs={{0,8},{1,9},{2,10},{3,11},{4,12},{5,13},{6,14},{7,15},{8,0},{9,1},... | collective-permute-start | bytes 1597448 | tf_op jit(solution)/shard_map/ppermute | solution.py:48
  103.6 0.0 collective-permute-done.4.rest_5_
  103.6 4.3 %collective-permute-start.17 = (bf16[2080,128]{1,0:T(8,128)(2,1)}, bf16[2080,128]{1,0:T(8,128)(2,1)S(1)}, u32[]{:S(2)}, u32[]{:S(2)}) collective-permute-start(bf16[2080,128]{1,0:T(8,128)(2,1)} %collective-permute-done.16.rest_16_), channel_id=1, source_target_pairs={{0,32},{1,33},{2,34},{3,35},{4,36},{5,37},{6,38},{7,39},{8,104},{9... | collective-permute-start | bytes 1597448 | tf_op jit(solution)/shard_map/ppermute | solution.py:48
  107.9 0.9 collective-permute-done.1.rest_1_
  108.8 1.2 collective-permute-start.24
  110.0 0.0 collective-permute-done.20.rest_21_
  110.0 0.8 collective-permute-start.10
  110.8 0.0 collective-permute-done.19.rest_18_
  110.8 2.8 %collective-permute-start.9 = (bf16[2080,128]{1,0:T(8,128)(2,1)}, bf16[2080,128]{1,0:T(8,128)(2,1)S(1)}, u32[]{:S(2)}, u32[]{:S(2)}) collective-permute-start(bf16[2080,128]{1,0:T(8,128)(2,1)} %collective-permute-done.8.rest_8_), channel_id=1, source_target_pairs={{0,32},{1,33},{2,34},{3,35},{4,36},{5,37},{6,38},{7,39},{8,104},{9... | collective-permute-start | bytes 1597448 | tf_op jit(solution)/shard_map/ppermute | solution.py:48
  113.7 0.8 collective-permute-done.17.rest_17_
  114.4 5.1 %collective-permute-start.5 = (bf16[2080,128]{1,0:T(8,128)(2,1)S(1)}, bf16[2080,128]{1,0:T(8,128)(2,1)S(1)}, u32[]{:S(2)}, u32[]{:S(2)}) collective-permute-start(bf16[2080,128]{1,0:T(8,128)(2,1)S(1)} %collective-permute-done.4.rest_5_), channel_id=1, source_target_pairs={{0,8},{1,9},{2,10},{3,11},{4,12},{5,13},{6,14},{7,15},{8,0},{9,1},... | collective-permute-start | bytes 1597448 | tf_op jit(solution)/shard_map/ppermute | solution.py:48
  119.6 1.9 %collective-permute-start.7 = (bf16[2080,128]{1,0:T(8,128)(2,1)S(1)}, bf16[2080,128]{1,0:T(8,128)(2,1)S(1)}, u32[]{:S(2)}, u32[]{:S(2)}) collective-permute-start(bf16[2080,128]{1,0:T(8,128)(2,1)S(1)} %collective-permute-done.1.rest_1_), channel_id=1, source_target_pairs={{0,8},{1,9},{2,10},{3,11},{4,12},{5,13},{6,14},{7,15},{8,0},{9,1},... | collective-permute-start | bytes 1597448 | tf_op jit(solution)/shard_map/ppermute | solution.py:48
  121.4 2.9 %collective-permute-start.25 = (bf16[2080,128]{1,0:T(8,128)(2,1)S(1)}, bf16[2080,128]{1,0:T(8,128)(2,1)S(1)}, u32[]{:S(2)}, u32[]{:S(2)}) collective-permute-start(bf16[2080,128]{1,0:T(8,128)(2,1)S(1)} %collective-permute-done.24.rest_24_), channel_id=1, source_target_pairs={{0,32},{1,33},{2,34},{3,35},{4,36},{5,37},{6,38},{7,39},{8,104},{9... | collective-permute-start | bytes 1597448 | tf_op jit(solution)/shard_map/ppermute | solution.py:48
  124.3 0.9 collective-permute-start.26
  125.3 0.0 collective-permute-start.21
  125.3 0.5 collective-permute-start.23
  125.8 0.1 collective-permute-start.11
  125.9 4.7 %collective-permute-done.25.rest_25_ = bf16[2080,128]{1,0:T(8,128)(2,1)S(1)} collective-permute-done((bf16[2080,128]{1,0:T(8,128)(2,1)S(1)}, bf16[2080,128]{1,0:T(8,128)(2,1)S(1)}, u32[]{:S(2)}, u32[]{:S(2)}) %collective-permute-start.25) | collective-permute-done | bytes 532512 | tf_op jit(solution)/shard_map/ppermute | solution.py:48
  130.5 1.4 collective-permute-start.27
  132.0 1.5 collective-permute-done.27.rest_27_
  133.5 16.6 %blocks.1 = bf16[128,24,128]{2,1,0:T(8,128)(2,1)S(1)} custom-call(s32[12]{0:T(128)S(1)} %copy-done.2, bf16[128,24,128]{2,1,0:T(8,128)(2,1)S(1)} %all-to-all-done.x_ref, f32[2,1024]{1,0:T(2,128)S(1)} %copy-done.4, bf16[2,3,1024,128]{3,2,1,0:T(8,128)(2,1)S(1)} %copy-done, bf16[2,1024,128]{2,1,0:T(8,128)(2,1)S(1)} %copy-done.1, ...), custom_call_target="tpu_custom_call" | custom-call | flops 6442450944 | bytes 18874368 | tf_op jit(solution)/shard_map/blocks/pallas_call | solution.py:203
  150.1 24.6 %all_to_all.10 = bf16[128,24,128]{2,1,0:T(8,128)(2,1)S(1)} all-to-all(bf16[128,24,128]{2,1,0:T(8,128)(2,1)S(1)} %blocks.1), channel_id=1, replica_groups=mesh['seq'=16,'filt'=8] {'seq','filt'}, dimensions={0} | all-to-all | bytes 1572864 | tf_op jit(solution)/shard_map/all_to_all | solution.py:257
  174.7 0.9 slice.8
  (25 shorter events, 0.1 us)
Async XLA Ops:
  0.7 132.8 %copy-start = (bf16[2,3,1024,128]{3,2,1,0:T(8,128)(2,1)S(1)}, bf16[2,3,1024,128]{3,2,1,0:T(8,128)(2,1)}, u32[]{:S(2)}) copy-start(bf16[2,3,1024,128]{3,2,1,0:T(8,128)(2,1)} %conv_ref.3) | copy-start | bytes 4718596
  0.7 132.8 %copy-start.1 = (bf16[2,1024,128]{2,1,0:T(8,128)(2,1)S(1)}, bf16[2,1024,128]{2,1,0:T(8,128)(2,1)}, u32[]{:S(2)}) copy-start(bf16[2,1024,128]{2,1,0:T(8,128)(2,1)} %mix_ref.3) | copy-start | bytes 1572868
  0.7 132.8 %copy-start.2 = (s32[12]{0:T(128)S(1)}, s32[12]{0:T(128)}, u32[]{:S(2)}) copy-start(s32[12]{0:T(128)} %stack.51.where_ref) | copy-start | bytes 148
  0.7 132.8 %copy-start.4 = (f32[2,1024]{1,0:T(2,128)S(1)}, f32[2,1024]{1,0:T(2,128)}, u32[]{:S(2)}) copy-start(f32[2,1024]{1,0:T(2,128)} %gain_ref.1) | copy-start | bytes 24580
  55.5 78.0 %copy-start.3 = (bf16[2080,128]{1,0:T(8,128)(2,1)S(1)}, bf16[2080,128]{1,0:T(8,128)(2,1)}, u32[]{:S(2)}) copy-start(bf16[2080,128]{1,0:T(8,128)(2,1)} %get-tuple-element.13.own_ref) | copy-start | bytes 1597444
  55.5 16.1 %collective-permute-start.12 = (bf16[2080,128]{1,0:T(8,128)(2,1)}, bf16[2080,128]{1,0:T(8,128)(2,1)}, u32[]{:S(2)}, u32[]{:S(2)}) collective-permute-start(bf16[2080,128]{1,0:T(8,128)(2,1)} %get-tuple-element.13.own_ref), channel_id=1, source_target_pairs={{0,4},{1,5},{2,6},{3,7},{4,16},{5,17},{6,18},{7,19},{8,28},{9,29},... | collective-permute-start | bytes 1597448 | tf_op jit(solution)/shard_map/ppermute | solution.py:48
  59.1 13.8 %collective-permute-start.2 = (bf16[2080,128]{1,0:T(8,128)(2,1)}, bf16[2080,128]{1,0:T(8,128)(2,1)}, u32[]{:S(2)}, u32[]{:S(2)}) collective-permute-start(bf16[2080,128]{1,0:T(8,128)(2,1)} %get-tuple-element.13.own_ref), channel_id=1, source_target_pairs={{0,3},{1,0},{2,1},{3,2},{4,7},{5,4},{6,5},{7,6},{8,9},{9,10},{10,1... | collective-permute-start | bytes 1597448 | tf_op jit(solution)/shard_map/ppermute | solution.py:48
  60.8 20.7 %collective-permute-start = (bf16[2080,128]{1,0:T(8,128)(2,1)}, bf16[2080,128]{1,0:T(8,128)(2,1)}, u32[]{:S(2)}, u32[]{:S(2)}) collective-permute-start(bf16[2080,128]{1,0:T(8,128)(2,1)} %get-tuple-element.13.own_ref), channel_id=1, source_target_pairs={{0,1},{1,2},{2,3},{3,0},{4,5},{5,6},{6,7},{7,4},{8,11},{9,8},{10,9... | collective-permute-start | bytes 1597448 | tf_op jit(solution)/shard_map/ppermute | solution.py:48
  62.9 25.5 %all-to-all-start = ((bf16[128,24,128]{2,1,0:T(8,128)(2,1)}), bf16[128,24,128]{2,1,0:T(8,128)(2,1)S(1)}, u32[]{:S(2)}, u32[]{:S(2)}) async-start(bf16[128,24,128]{2,1,0:T(8,128)(2,1)} %bitcast.14), calls=%async_computation | async-start | bytes 1572864 | tf_op jit(solution)/shard_map/all_to_all | solution.py:239
  71.6 16.7 %collective-permute-start.14 = (bf16[2080,128]{1,0:T(8,128)(2,1)}, bf16[2080,128]{1,0:T(8,128)(2,1)}, u32[]{:S(2)}, u32[]{:S(2)}) collective-permute-start(bf16[2080,128]{1,0:T(8,128)(2,1)} %collective-permute-done.12.rest_12_), channel_id=1, source_target_pairs={{0,8},{1,9},{2,10},{3,11},{4,12},{5,13},{6,14},{7,15},{8,0},{9,1},... | collective-permute-start | bytes 1597448 | tf_op jit(solution)/shard_map/ppermute | solution.py:48
  72.9 16.2 %collective-permute-start.18 = (bf16[2080,128]{1,0:T(8,128)(2,1)}, bf16[2080,128]{1,0:T(8,128)(2,1)}, u32[]{:S(2)}, u32[]{:S(2)}) collective-permute-start(bf16[2080,128]{1,0:T(8,128)(2,1)} %collective-permute-done.2.rest_4_), channel_id=1, source_target_pairs={{0,4},{1,5},{2,6},{3,7},{4,16},{5,17},{6,18},{7,19},{8,28},{9,29},... | collective-permute-start | bytes 1597448 | tf_op jit(solution)/shard_map/ppermute | solution.py:48
  74.7 15.0 %collective-permute-start.3 = (bf16[2080,128]{1,0:T(8,128)(2,1)}, bf16[2080,128]{1,0:T(8,128)(2,1)}, u32[]{:S(2)}, u32[]{:S(2)}) collective-permute-start(bf16[2080,128]{1,0:T(8,128)(2,1)} %collective-permute-done.2.rest_4_), channel_id=1, source_target_pairs={{0,8},{1,9},{2,10},{3,11},{4,12},{5,13},{6,14},{7,15},{8,0},{9,1},... | collective-permute-start | bytes 1597448 | tf_op jit(solution)/shard_map/ppermute | solution.py:48
  81.5 12.0 %collective-permute-start.16 = (bf16[2080,128]{1,0:T(8,128)(2,1)}, bf16[2080,128]{1,0:T(8,128)(2,1)}, u32[]{:S(2)}, u32[]{:S(2)}) collective-permute-start(bf16[2080,128]{1,0:T(8,128)(2,1)} %collective-permute-done.rest_0_), channel_id=1, source_target_pairs={{0,4},{1,5},{2,6},{3,7},{4,16},{5,17},{6,18},{7,19},{8,28},{9,29},... | collective-permute-start | bytes 1597448 | tf_op jit(solution)/shard_map/ppermute | solution.py:48
  84.5 12.4 %collective-permute-start.8 = (bf16[2080,128]{1,0:T(8,128)(2,1)}, bf16[2080,128]{1,0:T(8,128)(2,1)}, u32[]{:S(2)}, u32[]{:S(2)}) collective-permute-start(bf16[2080,128]{1,0:T(8,128)(2,1)} %collective-permute-done.rest_0_), channel_id=1, source_target_pairs={{0,1},{1,2},{2,3},{3,0},{4,5},{5,6},{6,7},{7,4},{8,11},{9,8},{10,9... | collective-permute-start | bytes 1597448 | tf_op jit(solution)/shard_map/ppermute | solution.py:48
  88.4 10.7 %collective-permute-start.6 = (bf16[2080,128]{1,0:T(8,128)(2,1)}, bf16[2080,128]{1,0:T(8,128)(2,1)S(1)}, u32[]{:S(2)}, u32[]{:S(2)}) collective-permute-start(bf16[2080,128]{1,0:T(8,128)(2,1)} %collective-permute-done.rest_0_), channel_id=1, source_target_pairs={{0,8},{1,9},{2,10},{3,11},{4,12},{5,13},{6,14},{7,15},{8,0},{9,1},... | collective-permute-start | bytes 1597448 | tf_op jit(solution)/shard_map/ppermute | solution.py:48
  89.1 12.0 %collective-permute-start.13 = (bf16[2080,128]{1,0:T(8,128)(2,1)}, bf16[2080,128]{1,0:T(8,128)(2,1)S(1)}, u32[]{:S(2)}, u32[]{:S(2)}) collective-permute-start(bf16[2080,128]{1,0:T(8,128)(2,1)} %get-tuple-element.14), channel_id=1, source_target_pairs={{0,4},{1,5},{2,6},{3,7},{4,16},{5,17},{6,18},{7,19},{8,28},{9,29},... | collective-permute-start | bytes 1597448 | tf_op jit(solution)/shard_map/ppermute | solution.py:48
  89.8 13.8 %collective-permute-start.4 = (bf16[2080,128]{1,0:T(8,128)(2,1)}, bf16[2080,128]{1,0:T(8,128)(2,1)S(1)}, u32[]{:S(2)}, u32[]{:S(2)}) collective-permute-start(bf16[2080,128]{1,0:T(8,128)(2,1)} %get-tuple-element.14), channel_id=1, source_target_pairs={{0,3},{1,0},{2,1},{3,2},{4,7},{5,4},{6,5},{7,6},{8,9},{9,10},{10,1... | collective-permute-start | bytes 1597448 | tf_op jit(solution)/shard_map/ppermute | solution.py:48
  93.5 15.3 %collective-permute-start.1 = (bf16[2080,128]{1,0:T(8,128)(2,1)}, bf16[2080,128]{1,0:T(8,128)(2,1)S(1)}, u32[]{:S(2)}, u32[]{:S(2)}) collective-permute-start(bf16[2080,128]{1,0:T(8,128)(2,1)} %get-tuple-element.14), channel_id=1, source_target_pairs={{0,1},{1,2},{2,3},{3,0},{4,5},{5,6},{6,7},{7,4},{8,11},{9,8},{10,9... | collective-permute-start | bytes 1597448 | tf_op jit(solution)/shard_map/ppermute | solution.py:48
  96.9 13.2 %collective-permute-start.20 = (bf16[2080,128]{1,0:T(8,128)(2,1)}, bf16[2080,128]{1,0:T(8,128)(2,1)S(1)}, u32[]{:S(2)}, u32[]{:S(2)}) collective-permute-start(bf16[2080,128]{1,0:T(8,128)(2,1)} %collective-permute-done.18.rest_20_), channel_id=1, source_target_pairs={{0,32},{1,33},{2,34},{3,35},{4,36},{5,37},{6,38},{7,39},{8,104},{9... | collective-permute-start | bytes 1597448 | tf_op jit(solution)/shard_map/ppermute | solution.py:48
  99.1 11.8 %collective-permute-start.19 = (bf16[2080,128]{1,0:T(8,128)(2,1)}, bf16[2080,128]{1,0:T(8,128)(2,1)S(1)}, u32[]{:S(2)}, u32[]{:S(2)}) collective-permute-start(bf16[2080,128]{1,0:T(8,128)(2,1)} %collective-permute-done.18.rest_20_), channel_id=1, source_target_pairs={{0,8},{1,9},{2,10},{3,11},{4,12},{5,13},{6,14},{7,15},{8,0},{9,1},... | collective-permute-start | bytes 1597448 | tf_op jit(solution)/shard_map/ppermute | solution.py:48
  101.1 12.5 %collective-permute-start.22 = (bf16[2080,128]{1,0:T(8,128)(2,1)}, bf16[2080,128]{1,0:T(8,128)(2,1)S(1)}, u32[]{:S(2)}, u32[]{:S(2)}) collective-permute-start(bf16[2080,128]{1,0:T(8,128)(2,1)} %collective-permute-done.16.rest_16_), channel_id=1, source_target_pairs={{0,8},{1,9},{2,10},{3,11},{4,12},{5,13},{6,14},{7,15},{8,0},{9,1},... | collective-permute-start | bytes 1597448 | tf_op jit(solution)/shard_map/ppermute | solution.py:48
  103.6 10.8 %collective-permute-start.17 = (bf16[2080,128]{1,0:T(8,128)(2,1)}, bf16[2080,128]{1,0:T(8,128)(2,1)S(1)}, u32[]{:S(2)}, u32[]{:S(2)}) collective-permute-start(bf16[2080,128]{1,0:T(8,128)(2,1)} %collective-permute-done.16.rest_16_), channel_id=1, source_target_pairs={{0,32},{1,33},{2,34},{3,35},{4,36},{5,37},{6,38},{7,39},{8,104},{9... | collective-permute-start | bytes 1597448 | tf_op jit(solution)/shard_map/ppermute | solution.py:48
  108.8 10.8 %collective-permute-start.24 = (bf16[2080,128]{1,0:T(8,128)(2,1)}, bf16[2080,128]{1,0:T(8,128)(2,1)S(1)}, u32[]{:S(2)}, u32[]{:S(2)}) collective-permute-start(bf16[2080,128]{1,0:T(8,128)(2,1)} %collective-permute-done.8.rest_8_), channel_id=1, source_target_pairs={{0,4},{1,5},{2,6},{3,7},{4,16},{5,17},{6,18},{7,19},{8,28},{9,29},... | collective-permute-start | bytes 1597448 | tf_op jit(solution)/shard_map/ppermute | solution.py:48
  110.0 11.4 %collective-permute-start.10 = (bf16[2080,128]{1,0:T(8,128)(2,1)}, bf16[2080,128]{1,0:T(8,128)(2,1)S(1)}, u32[]{:S(2)}, u32[]{:S(2)}) collective-permute-start(bf16[2080,128]{1,0:T(8,128)(2,1)} %collective-permute-done.8.rest_8_), channel_id=1, source_target_pairs={{0,8},{1,9},{2,10},{3,11},{4,12},{5,13},{6,14},{7,15},{8,0},{9,1},... | collective-permute-start | bytes 1597448 | tf_op jit(solution)/shard_map/ppermute | solution.py:48
  110.8 13.5 %collective-permute-start.9 = (bf16[2080,128]{1,0:T(8,128)(2,1)}, bf16[2080,128]{1,0:T(8,128)(2,1)S(1)}, u32[]{:S(2)}, u32[]{:S(2)}) collective-permute-start(bf16[2080,128]{1,0:T(8,128)(2,1)} %collective-permute-done.8.rest_8_), channel_id=1, source_target_pairs={{0,32},{1,33},{2,34},{3,35},{4,36},{5,37},{6,38},{7,39},{8,104},{9... | collective-permute-start | bytes 1597448 | tf_op jit(solution)/shard_map/ppermute | solution.py:48
  113.7 11.6 %collective-permute-start.15 = (bf16[2080,128]{1,0:T(8,128)(2,1)S(1)}, bf16[2080,128]{1,0:T(8,128)(2,1)S(1)}, u32[]{:S(2)}, u32[]{:S(2)}) collective-permute-start(bf16[2080,128]{1,0:T(8,128)(2,1)S(1)} %collective-permute-done.13.rest_13_), channel_id=1, source_target_pairs={{0,8},{1,9},{2,10},{3,11},{4,12},{5,13},{6,14},{7,15},{8,0},{9,1},... | collective-permute-start | bytes 1597448 | tf_op jit(solution)/shard_map/ppermute | solution.py:48
  114.4 10.9 %collective-permute-start.5 = (bf16[2080,128]{1,0:T(8,128)(2,1)S(1)}, bf16[2080,128]{1,0:T(8,128)(2,1)S(1)}, u32[]{:S(2)}, u32[]{:S(2)}) collective-permute-start(bf16[2080,128]{1,0:T(8,128)(2,1)S(1)} %collective-permute-done.4.rest_5_), channel_id=1, source_target_pairs={{0,8},{1,9},{2,10},{3,11},{4,12},{5,13},{6,14},{7,15},{8,0},{9,1},... | collective-permute-start | bytes 1597448 | tf_op jit(solution)/shard_map/ppermute | solution.py:48
  119.6 6.2 %collective-permute-start.7 = (bf16[2080,128]{1,0:T(8,128)(2,1)S(1)}, bf16[2080,128]{1,0:T(8,128)(2,1)S(1)}, u32[]{:S(2)}, u32[]{:S(2)}) collective-permute-start(bf16[2080,128]{1,0:T(8,128)(2,1)S(1)} %collective-permute-done.1.rest_1_), channel_id=1, source_target_pairs={{0,8},{1,9},{2,10},{3,11},{4,12},{5,13},{6,14},{7,15},{8,0},{9,1},... | collective-permute-start | bytes 1597448 | tf_op jit(solution)/shard_map/ppermute | solution.py:48
  121.4 9.1 %collective-permute-start.25 = (bf16[2080,128]{1,0:T(8,128)(2,1)S(1)}, bf16[2080,128]{1,0:T(8,128)(2,1)S(1)}, u32[]{:S(2)}, u32[]{:S(2)}) collective-permute-start(bf16[2080,128]{1,0:T(8,128)(2,1)S(1)} %collective-permute-done.24.rest_24_), channel_id=1, source_target_pairs={{0,32},{1,33},{2,34},{3,35},{4,36},{5,37},{6,38},{7,39},{8,104},{9... | collective-permute-start | bytes 1597448 | tf_op jit(solution)/shard_map/ppermute | solution.py:48
  124.3 7.6 %collective-permute-start.26 = (bf16[2080,128]{1,0:T(8,128)(2,1)S(1)}, bf16[2080,128]{1,0:T(8,128)(2,1)S(1)}, u32[]{:S(2)}, u32[]{:S(2)}) collective-permute-start(bf16[2080,128]{1,0:T(8,128)(2,1)S(1)} %collective-permute-done.24.rest_24_), channel_id=1, source_target_pairs={{0,8},{1,9},{2,10},{3,11},{4,12},{5,13},{6,14},{7,15},{8,0},{9,1},... | collective-permute-start | bytes 1597448 | tf_op jit(solution)/shard_map/ppermute | solution.py:48
  125.3 6.7 %collective-permute-start.21 = (bf16[2080,128]{1,0:T(8,128)(2,1)S(1)}, bf16[2080,128]{1,0:T(8,128)(2,1)S(1)}, u32[]{:S(2)}, u32[]{:S(2)}) collective-permute-start(bf16[2080,128]{1,0:T(8,128)(2,1)S(1)} %collective-permute-done.20.rest_21_), channel_id=1, source_target_pairs={{0,8},{1,9},{2,10},{3,11},{4,12},{5,13},{6,14},{7,15},{8,0},{9,1},... | collective-permute-start | bytes 1597448 | tf_op jit(solution)/shard_map/ppermute | solution.py:48
  125.3 6.7 %collective-permute-start.23 = (bf16[2080,128]{1,0:T(8,128)(2,1)S(1)}, bf16[2080,128]{1,0:T(8,128)(2,1)S(1)}, u32[]{:S(2)}, u32[]{:S(2)}) collective-permute-start(bf16[2080,128]{1,0:T(8,128)(2,1)S(1)} %collective-permute-done.17.rest_17_), channel_id=1, source_target_pairs={{0,8},{1,9},{2,10},{3,11},{4,12},{5,13},{6,14},{7,15},{8,0},{9,1},... | collective-permute-start | bytes 1597448 | tf_op jit(solution)/shard_map/ppermute | solution.py:48
  125.8 6.2 %collective-permute-start.11 = (bf16[2080,128]{1,0:T(8,128)(2,1)S(1)}, bf16[2080,128]{1,0:T(8,128)(2,1)S(1)}, u32[]{:S(2)}, u32[]{:S(2)}) collective-permute-start(bf16[2080,128]{1,0:T(8,128)(2,1)S(1)} %collective-permute-done.9.rest_9_), channel_id=1, source_target_pairs={{0,8},{1,9},{2,10},{3,11},{4,12},{5,13},{6,14},{7,15},{8,0},{9,1},... | collective-permute-start | bytes 1597448 | tf_op jit(solution)/shard_map/ppermute | solution.py:48
  130.5 2.9 %collective-permute-start.27 = (bf16[2080,128]{1,0:T(8,128)(2,1)S(1)}, bf16[2080,128]{1,0:T(8,128)(2,1)S(1)}, u32[]{:S(2)}, u32[]{:S(2)}) collective-permute-start(bf16[2080,128]{1,0:T(8,128)(2,1)S(1)} %collective-permute-done.25.rest_25_), channel_id=1, source_target_pairs={{0,8},{1,9},{2,10},{3,11},{4,12},{5,13},{6,14},{7,15},{8,0},{9,1},... | collective-permute-start | bytes 1597448 | tf_op jit(solution)/shard_map/ppermute | solution.py:48

commit v3 on v2

v3 whole, which is shorter than its diff:
```python
import functools

import jax
import jax.numpy as jnp
from jax import lax
from jax.experimental import pallas as pl
from jax.experimental.pallas import tpu as pltpu
from jax.sharding import PartitionSpec as P

LAYERS = 2
C = 1024
BLOCKS = 16
LANES = 128
SHARDS = 8
RES = 24
ROWS = BLOCKS * RES
EXTRA = 16
HALF = C // 2
PART = 4 * HALF + EXTRA
AXES = ("seq", "filt")


def coords(i):
    z, i = i % 4, i // 4
    yl, i = i % 2, i // 2
    c, i = i % 2, i // 2
    yh, x = i % 2, i // 2
    return x, yh * 2 + yl, z, c


def linear(x, y, z, c):
    x, y, z = x % 4, y % 4, z % 4
    return (((x * 2 + y // 2) * 2 + c) * 2 + y % 2) * 4 + z


def route(step):
    return [(i, linear(*step(*coords(i)))) for i in range(128)]


Z_AWAY = route(lambda x, y, z, c: (x, y, z + 1 - 2 * c, c))
Z_BACK = route(lambda x, y, z, c: (x, y, z - 1 + 2 * c, c))
Y_SIDE = route(lambda x, y, z, c: (x, y + 1 - 2 * c, z, c))
SWAP = route(lambda x, y, z, c: (x, y, z, 1 - c))


def send(block, path):
    return lax.ppermute(block, AXES, path)


def three_parts(v):
    hi = v.astype(jnp.bfloat16).astype(jnp.float32)
    mid = (v - hi).astype(jnp.bfloat16).astype(jnp.float32)
    lo = v - hi - mid
    return [hi, mid, lo]


def prepare_kernel(where_ref, tokens_ref, conv_ref, mix_ref, conv_bias_ref, mix_bias_ref, padded_ref, own_ref, sems):
    length = tokens_ref.shape[0]
    rows = pl.ds(pl.multiple_of(where_ref[0] * HALF, HALF), HALF)
    moves = []
    for layer in range(LAYERS):
        for t in range(4):
            source = conv_ref.at[layer, t, rows] if t < 3 else mix_ref.at[layer, rows]
            moves.append((source, own_ref.at[pl.ds(layer * PART + t * HALF, HALF)]))
    moves.append((tokens_ref, padded_ref.at[pl.ds(0, length)]))
    copies = [pltpu.make_async_copy(a, b, sems.at[i]) for i, (a, b) in enumerate(moves)]
    for copy in copies:
        copy.start()
    padded_ref[length:, :] = jnp.zeros((128 * RES - length, LANES), jnp.bfloat16)
    for layer in range(LAYERS):
        lines = three_parts(conv_bias_ref[layer:layer + 1, :]) + three_parts(mix_bias_ref[layer:layer + 1, :])
        lines.append(jnp.zeros((EXTRA - 6, LANES), jnp.float32))
        own_ref[layer * PART + 4 * HALF:(layer + 1) * PART, :] = jnp.concatenate(lines, axis=0).astype(jnp.bfloat16)
    for copy in copies:
        copy.wait()


def prepare(where, tokens, conv, mix, conv_bias, mix_bias):
    anywhere = pl.BlockSpec(memory_space=pl.ANY)
    vmem = pl.BlockSpec(memory_space=pltpu.VMEM)
    return pl.pallas_call(
        prepare_kernel,
        out_shape=[
            jax.ShapeDtypeStruct((128 * RES, LANES), jnp.bfloat16),
            jax.ShapeDtypeStruct((LAYERS * PART, LANES), jnp.bfloat16),
        ],
        in_specs=[pl.BlockSpec(memory_space=pltpu.SMEM), anywhere, anywhere, anywhere, vmem, vmem],
        out_specs=[vmem, vmem],
        scratch_shapes=[pltpu.SemaphoreType.DMA((1 + 4 * LAYERS,))],
        compiler_params=pltpu.CompilerParams(vmem_limit_bytes=60 * 2**20),
        cost_estimate=pl.CostEstimate(flops=0, bytes_accessed=4 * 2**20, transcendentals=0),
        name="prepare",
    )(where, tokens, conv, mix, conv_bias, mix_bias)


def blocks_kernel(where_ref, x_ref, gain_ref, conv_ref, mix_ref, own_ref, *rest):
    parts = rest[:2 * (SHARDS - 1)]
    out_ref, w, mine, bias, x, normed, n, act, mixing, sems, mine_sems, bias_sems = rest[2 * (SHARDS - 1):]
    width = 2 * LANES

    def half(i):
        return pl.ds(pl.multiple_of(where_ref[i] * HALF, HALF), HALF)

    def home(k):
        return pl.ds(pl.multiple_of(where_ref[2 + k] * LANES, LANES), LANES)

    arriving = []
    for layer in range(LAYERS):
        layer_rows = pl.ds(layer * PART, PART)
        for k in range(SHARDS):
            if k == 0:
                moves = [
                    (conv_ref.at[layer], mine.at[layer, pl.ds(0, 3)], mine_sems.at[layer, 0]),
                    (mix_ref.at[layer], mine.at[layer, 3], mine_sems.at[layer, 1]),
                    (own_ref.at[pl.ds(layer * PART + 4 * HALF, EXTRA)], bias.at[layer], bias_sems.at[layer]),
                ]
            else:
                moves = []
                for i in range(2):
                    p = 2 * (k - 1) + i
                    moves.append((parts[p].at[layer_rows], w.at[p, layer_rows], sems.at[layer, p]))
            copies = [pltpu.make_async_copy(*move) for move in moves]
            for copy in copies:
                copy.start()
            arriving.append(copies)

    for b in range(BLOCKS):
        for f in range(SHARDS):
            x[b * RES:(b + 1) * RES, f * LANES:(f + 1) * LANES] = x_ref[b * SHARDS + f].astype(jnp.float32)

    for layer in range(LAYERS):
        base = layer * PART
        wide = x[...]
        scale = lax.rsqrt(jnp.mean(wide * wide, axis=-1, keepdims=True) + 1e-06)
        normed[...] = wide * scale * gain_ref[layer:layer + 1, :]
        shift = RES * 2**layer
        edge = jnp.zeros((shift, HALF), jnp.float32)
        for i in range(2):
            here = normed[:, half(i)]
            earlier = jnp.concatenate([edge, here[:ROWS - shift]], axis=0)
            later = jnp.concatenate([here[shift:], edge], axis=0)
            for t, rows in enumerate((earlier, here, later)):
                start = (3 * i + t) * HALF
                n[:, start:start + HALF] = rows.astype(jnp.bfloat16)

        def conv_column(k):
            if k == 0:
                return jnp.concatenate([mine[layer, t, half(i), :] for i in range(2) for t in range(3)], axis=0)
            return jnp.concatenate([w[2 * (k - 1) + i, base:base + 3 * HALF, :] for i in range(2)], axis=0)

        def mix_column(k):
            if k == 0:
                return jnp.concatenate([mine[layer, 3, half(i), :] for i in range(2)], axis=0)
            return jnp.concatenate([w[2 * (k - 1) + i, base + 3 * HALF:base + 4 * HALF, :] for i in range(2)], axis=0)

        def bias_row(k, start):
            rows = bias[layer] if k == 0 else w[2 * (k - 1), base + 4 * HALF:base + PART, :]
            rows = rows.astype(jnp.float32)
            return rows[start:start + 1] + rows[start + 1:start + 2] + rows[start + 2:start + 3]

        for j in range(SHARDS // 2):
            pair = (2 * j, 2 * j + 1)
            for k in pair:
                for copy in arriving[layer * SHARDS + k]:
                    copy.wait()
            taps = jnp.concatenate([conv_column(k) for k in pair], axis=1)
            hidden = jnp.dot(n[...], taps, preferred_element_type=jnp.float32)
            hidden = hidden + jnp.concatenate([bias_row(k, 0) for k in pair], axis=1)
            done = (hidden * (1.0 + lax.erf(hidden * 0.7071067811865476)) * 0.5).astype(jnp.bfloat16)
            for h, k in enumerate(pair):
                act[:, home(k)] = done[:, h * LANES:(h + 1) * LANES]

        for i in range(2):
            mixing[:, i * HALF:(i + 1) * HALF] = act[:, half(i)]

        for j in range(SHARDS // 2):
            pair = (2 * j, 2 * j + 1)
            mixed = jnp.dot(mixing[...], jnp.concatenate([mix_column(k) for k in pair], axis=1), preferred_element_type=jnp.float32)
            mixed = mixed + jnp.concatenate([bias_row(k, 3) for k in pair], axis=1)
            for h, k in enumerate(pair):
                total = x[:, home(k)] + mixed[:, h * LANES:(h + 1) * LANES]
                if layer == LAYERS - 1:
                    f = where_ref[2 + k]
                    for b in range(BLOCKS):
                        out_ref[b * SHARDS + f] = total[b * RES:(b + 1) * RES].astype(jnp.bfloat16)
                else:
                    x[:, home(k)] = total.astype(jnp.bfloat16).astype(jnp.float32)


def run_blocks(where, x, gain, conv, mix, own, parts):
    vmem = pl.BlockSpec(memory_space=pltpu.VMEM)
    anywhere = pl.BlockSpec(memory_space=pl.ANY)
    return pl.pallas_call(
        blocks_kernel,
        out_shape=jax.ShapeDtypeStruct((BLOCKS * SHARDS, RES, LANES), jnp.bfloat16),
        in_specs=[pl.BlockSpec(memory_space=pltpu.SMEM), vmem, vmem] + [anywhere] * (3 + len(parts)),
        out_specs=vmem,
        scratch_shapes=[
            pltpu.VMEM((len(parts), LAYERS * PART, LANES), jnp.bfloat16),
            pltpu.VMEM((LAYERS, 4, C, LANES), jnp.bfloat16),
            pltpu.VMEM((LAYERS, EXTRA, LANES), jnp.bfloat16),
            pltpu.VMEM((ROWS, C), jnp.float32),
            pltpu.VMEM((ROWS, C), jnp.float32),
            pltpu.VMEM((ROWS, 3 * C), jnp.bfloat16),
            pltpu.VMEM((ROWS, C), jnp.bfloat16),
            pltpu.VMEM((ROWS, C), jnp.bfloat16),
            pltpu.SemaphoreType.DMA((LAYERS, len(parts))),
            pltpu.SemaphoreType.DMA((LAYERS, 2)),
            pltpu.SemaphoreType.DMA((LAYERS,)),
        ],
        compiler_params=pltpu.CompilerParams(vmem_limit_bytes=32 * 2**20),
        cost_estimate=pl.CostEstimate(flops=16 * ROWS * C * C, bytes_accessed=18 * 2**20, transcendentals=2 * ROWS * C),
        name="blocks",
    )(where, x, gain, conv, mix, own, *parts)


def per_device(tokens, conv_weight, conv_bias, mix_weight, mix_bias, norm_gain):
    seq, filt = lax.axis_index("seq"), lax.axis_index("filt")
    core = seq & 1
    z, yl = filt & 3, filt >> 2
    zs = [z, (z - 1 + 2 * core) & 3, (z + 1 - 2 * core) & 3, (z + 2) & 3]
    shards = [yl * 4 + v for v in zs] + [(1 - yl) * 4 + v for v in zs]
    where = jnp.stack([core, 1 - core] + shards).astype(jnp.int32)

    padded, own = prepare(where, tokens, conv_weight, mix_weight, conv_bias, mix_bias)
    near, far = send(own, Z_AWAY), send(own, Z_BACK)
    cross = send(own, Y_SIDE)
    x = lax.all_to_all(padded.reshape(128, RES, LANES), AXES, split_axis=0, concat_axis=0, tiled=True)
    near, far, cross, x = lax.optimization_barrier((near, far, cross, x))
    beyond = send(near, Z_AWAY)
    cross_near = send(near, Y_SIDE)
    far, cross_near = lax.optimization_barrier((far, cross_near))
    cross_far = send(far, Y_SIDE)
    cross_beyond = send(cross_near, Z_AWAY)
    mine = [near, far, beyond, cross, cross_near, cross_far, cross_beyond]
    swapped = [send(v, SWAP) for v in mine]
    parts = []
    for k, i in enumerate([1, 0, 2, 3, 5, 4, 6]):
        parts += [mine[k], swapped[i]]
    x = run_blocks(where, x, norm_gain, conv_weight, mix_weight, own, parts)
    y = lax.all_to_all(x, AXES, split_axis=0, concat_axis=0, tiled=True)
    return y.reshape(128 * RES, LANES)[:tokens.shape[0]]


def solution(mesh):
    in_specs = (
        P("seq", "filt"),
        P(None, None, None, "filt"),
        P(None, "filt"),
        P(None, None, "filt"),
        P(None, "filt"),
        P(),
    )
    out_specs = P("seq", "filt")
    return jax.shard_map(
        per_device, mesh=mesh, in_specs=in_specs, out_specs=out_specs, check_vma=False
    )
```

time: 176 us -> 123 us (0.70)
  Pallas kernels: 71.4 us -> 20 us
  starting transfers between devices: 67.3 us -> 18.5 us
  blocking collectives: 24.6 us -> 55.4 us
  waiting for transfers between devices: 10.6 us -> 25.6 us
    pallas_call x1, Pallas kernels: 54.8 us -> 3.63 us  [prepare(): pl.pallas_call(prepare_kernel, out_shape=[jax.ShapeDtypeStruct((128 * RES...]
    ppermute x28 -> x14, starting transfers between devices: 58.6 us -> 18.5 us  [send(): return lax.ppermute(block, AXES, path)]
    all_to_all x0 -> x1, blocking collectives: none -> 33.4 us  [per_device(): lax.all_to_all(padded.reshape(128, RES, LANES), AXES, split_axis=0, conca...]
    ppermute x28 -> x14, waiting for transfers between devices: 10.5 us -> 25.6 us  [send(): return lax.ppermute(block, AXES, path)]
    all_to_all x1 -> x0, starting transfers between devices: 8.69 us -> none  [per_device(): lax.all_to_all(padded.reshape(128, RES, LANES), AXES, split_axis=0, conca...]
    all_to_all x1, blocking collectives: 24.6 us -> 22 us  [per_device(): y = lax.all_to_all(x, AXES, split_axis=0, concat_axis=0, tiled=True)]
  transfers between devices with their start and end apart: 29 -> 14, of which waited for: 7 -> 4; matrix products, arithmetic and copies ran while one was open for 0% -> 0% of each run, Pallas kernels for 0% -> 0%
where the time goes in v3:
time: 123 us; the launch traced here: 122 us
  blocking collectives  55.4 us (45%)
  waiting for transfers between devices  25.6 us (21%)
  Pallas kernels  20 us (16%)
  starting transfers between devices  18.5 us (15%)
  local copies, waits for them, and re-layouts  2.77 us (2%)
    all_to_all x1, blocking collectives, per_device(): lax.all_to_all(padded.reshape(128, RES, LANES), AXES, split_axis=0, conca...  33.4 us
    ppermute x14, waiting for transfers between devices, send(): return lax.ppermute(block, AXES, path)  25.6 us
    all_to_all x1, blocking collectives, per_device(): y = lax.all_to_all(x, AXES, split_axis=0, concat_axis=0, tiled=True)  22 us
    ppermute x14, starting transfers between devices, send(): return lax.ppermute(block, AXES, path)  18.5 us
    pallas_call x1, Pallas kernels, run_blocks(): pl.pallas_call(blocks_kernel, out_shape=jax.ShapeDtypeStruct((BLOCKS * SH...  16.4 us
    pallas_call x1, Pallas kernels, prepare(): pl.pallas_call(prepare_kernel, out_shape=[jax.ShapeDtypeStruct((128 * RES...  3.63 us
  transfers between devices with their start and end apart: 14, of which 4 were waited for; matrix products, arithmetic and copies ran while one was open for 0% of the time, Pallas kernels for 0%

profile of v3, /device:TPU:1, one launch (start us, length us, event | category | flops | bytes accessed | tf_op | source)
XLA Modules:
  0.0 122.4 jit_solution(14637195329613786056)
XLA Ops:
  0.0 0.6 stack.43.where_ref
  0.6 0.0 copy-start.1
  0.6 0.0 copy-start.4
  0.6 3.6 %prepare.1 = (bf16[3072,128]{1,0:T(8,128)(2,1)}, bf16[4128,128]{1,0:T(8,128)(2,1)}) custom-call(s32[10]{0:T(128)} %stack.43.where_ref, bf16[2688,128]{1,0:T(8,128)(2,1)} %tokens_ref.1, bf16[2,3,1024,128]{3,2,1,0:T(8,128)(2,1)} %conv_ref.3, bf16[2,1024,128]{2,1,0:T(8,128)(2,1)} %mix_ref.3, f32[2,128]{1,0:T(2,128)} %conv_bias_ref.1, f32[2,128]{1,0:T(2,128)} %mix_bias_ref.1), custom_call_target="tpu_custom_call" | custom-call | bytes 4194304 | tf_op jit(solution)/shard_map/prepare/pallas_call | solution.py:81
  4.3 0.0 copy-start
  4.3 0.0 copy-start.2
  4.3 3.6 %collective-permute-start.2 = (bf16[4128,128]{1,0:T(8,128)(2,1)}, bf16[4128,128]{1,0:T(8,128)(2,1)S(1)}, u32[]{:S(2)}, u32[]{:S(2)}) collective-permute-start(bf16[4128,128]{1,0:T(8,128)(2,1)} %get-tuple-element.13.own_ref), channel_id=1, source_target_pairs={{0,4},{1,5},{2,6},{3,7},{4,16},{5,17},{6,18},{7,19},{8,28},{9,29},... | collective-permute-start | bytes 3170312 | tf_op jit(solution)/shard_map/ppermute | solution.py:47
  7.9 1.6 %collective-permute-start.1 = (bf16[4128,128]{1,0:T(8,128)(2,1)}, bf16[4128,128]{1,0:T(8,128)(2,1)S(1)}, u32[]{:S(2)}, u32[]{:S(2)}) collective-permute-start(bf16[4128,128]{1,0:T(8,128)(2,1)} %get-tuple-element.13.own_ref), channel_id=1, source_target_pairs={{0,3},{1,0},{2,1},{3,2},{4,7},{5,4},{6,5},{7,6},{8,9},{9,10},{10,1... | collective-permute-start | bytes 3170312 | tf_op jit(solution)/shard_map/ppermute | solution.py:47
  9.6 2.1 %collective-permute-start = (bf16[4128,128]{1,0:T(8,128)(2,1)}, bf16[4128,128]{1,0:T(8,128)(2,1)S(1)}, u32[]{:S(2)}, u32[]{:S(2)}) collective-permute-start(bf16[4128,128]{1,0:T(8,128)(2,1)} %get-tuple-element.13.own_ref), channel_id=1, source_target_pairs={{0,1},{1,2},{2,3},{3,0},{4,5},{5,6},{6,7},{7,4},{8,11},{9,8},{10,9... | collective-permute-start | bytes 3170312 | tf_op jit(solution)/shard_map/ppermute | solution.py:47
  11.7 33.4 %all_to_all.10.x_ref = bf16[128,24,128]{2,1,0:T(8,128)(2,1)S(1)} all-to-all(bf16[128,24,128]{2,1,0:T(8,128)(2,1)} %bitcast.12), channel_id=1, replica_groups=mesh['seq'=16,'filt'=8] {'seq','filt'}, dimensions={0} | all-to-all | bytes 1572864 | tf_op jit(solution)/shard_map/all_to_all | solution.py:228
  45.1 0.0 collective-permute-done.2.rest_6_
  45.1 0.0 collective-permute-done.1.rest_2_
  45.1 0.0 collective-permute-done.rest_0_
  45.1 0.3 collective-permute-start.3
  45.4 1.9 %collective-permute-start.6 = (bf16[4128,128]{1,0:T(8,128)(2,1)S(1)}, bf16[4128,128]{1,0:T(8,128)(2,1)S(1)}, u32[]{:S(2)}, u32[]{:S(2)}) collective-permute-start(bf16[4128,128]{1,0:T(8,128)(2,1)S(1)} %collective-permute-done.rest_0_), channel_id=1, source_target_pairs={{0,1},{1,2},{2,3},{3,0},{4,5},{5,6},{6,7},{7,4},{8,11},{9,8},{10,9... | collective-permute-start | bytes 3170312 | tf_op jit(solution)/shard_map/ppermute | solution.py:47
  47.3 0.0 collective-permute-start.5
  47.3 0.5 collective-permute-start.8
  47.8 11.4 %collective-permute-done.3.rest_8_ = bf16[4128,128]{1,0:T(8,128)(2,1)S(1)} collective-permute-done((bf16[4128,128]{1,0:T(8,128)(2,1)S(1)}, bf16[4128,128]{1,0:T(8,128)(2,1)S(1)}, u32[]{:S(2)}, u32[]{:S(2)}) %collective-permute-start.3) | collective-permute-done | bytes 1056800 | tf_op jit(solution)/shard_map/ppermute | solution.py:47
  59.2 1.5 %collective-permute-start.9 = (bf16[4128,128]{1,0:T(8,128)(2,1)S(1)}, bf16[4128,128]{1,0:T(8,128)(2,1)S(1)}, u32[]{:S(2)}, u32[]{:S(2)}) collective-permute-start(bf16[4128,128]{1,0:T(8,128)(2,1)S(1)} %collective-permute-done.1.rest_2_), channel_id=1, source_target_pairs={{0,4},{1,5},{2,6},{3,7},{4,16},{5,17},{6,18},{7,19},{8,28},{9,29},... | collective-permute-start | bytes 3170312 | tf_op jit(solution)/shard_map/ppermute | solution.py:47
  60.7 1.6 %collective-permute-start.12 = (bf16[4128,128]{1,0:T(8,128)(2,1)S(1)}, bf16[4128,128]{1,0:T(8,128)(2,1)S(1)}, u32[]{:S(2)}, u32[]{:S(2)}) collective-permute-start(bf16[4128,128]{1,0:T(8,128)(2,1)S(1)} %collective-permute-done.3.rest_8_), channel_id=1, source_target_pairs={{0,1},{1,2},{2,3},{3,0},{4,5},{5,6},{6,7},{7,4},{8,11},{9,8},{10,9... | collective-permute-start | bytes 3170312 | tf_op jit(solution)/shard_map/ppermute | solution.py:47
  62.2 0.0 collective-permute-done.8.rest_7_
  62.2 0.0 collective-permute-start.4
  62.2 0.0 collective-permute-done.6.rest_4_
  62.3 0.5 collective-permute-start.11
  62.8 0.0 collective-permute-done.5.rest_3_
  62.8 0.1 collective-permute-start.7
  62.8 10.4 %collective-permute-done.9.rest_10_ = bf16[4128,128]{1,0:T(8,128)(2,1)S(1)} collective-permute-done((bf16[4128,128]{1,0:T(8,128)(2,1)S(1)}, bf16[4128,128]{1,0:T(8,128)(2,1)S(1)}, u32[]{:S(2)}, u32[]{:S(2)}) %collective-permute-start.9) | collective-permute-done | bytes 1056800 | tf_op jit(solution)/shard_map/ppermute | solution.py:47
  73.2 4.8 %collective-permute-start.10 = (bf16[4128,128]{1,0:T(8,128)(2,1)S(1)}, bf16[4128,128]{1,0:T(8,128)(2,1)S(1)}, u32[]{:S(2)}, u32[]{:S(2)}) collective-permute-start(bf16[4128,128]{1,0:T(8,128)(2,1)S(1)} %collective-permute-done.9.rest_10_), channel_id=1, source_target_pairs={{0,8},{1,9},{2,10},{3,11},{4,12},{5,13},{6,14},{7,15},{8,0},{9,1},... | collective-permute-start | bytes 3170312 | tf_op jit(solution)/shard_map/ppermute | solution.py:47
  78.0 0.0 collective-permute-done.12.rest_12_
  78.0 0.0 collective-permute-start.13
  78.0 0.0 collective-permute-done.7.rest_5_
  78.0 0.0 collective-permute-done.4.rest_1_
  78.0 0.0 collective-permute-done.11.rest_11_
  78.0 2.3 %collective-permute-done.10.rest_9_ = bf16[4128,128]{1,0:T(8,128)(2,1)S(1)} collective-permute-done((bf16[4128,128]{1,0:T(8,128)(2,1)S(1)}, bf16[4128,128]{1,0:T(8,128)(2,1)S(1)}, u32[]{:S(2)}, u32[]{:S(2)}) %collective-permute-start.10) | collective-permute-done | bytes 1056800 | tf_op jit(solution)/shard_map/ppermute | solution.py:47
  80.3 1.5 %collective-permute-done.13.rest_13_ = bf16[4128,128]{1,0:T(8,128)(2,1)S(1)} collective-permute-done((bf16[4128,128]{1,0:T(8,128)(2,1)S(1)}, bf16[4128,128]{1,0:T(8,128)(2,1)S(1)}, u32[]{:S(2)}, u32[]{:S(2)}) %collective-permute-start.13) | collective-permute-done | bytes 1056800 | tf_op jit(solution)/shard_map/ppermute | solution.py:47
  81.8 0.0 copy-done.1
  81.8 0.0 copy-done.4
  81.8 0.0 copy-done
  81.8 0.0 copy-done.2
  81.8 0.0 copy-start.3
  81.8 1.2 copy-done.3
  83.0 16.4 %blocks.1 = bf16[128,24,128]{2,1,0:T(8,128)(2,1)S(1)} custom-call(s32[10]{0:T(128)S(1)} %copy-done.2, bf16[128,24,128]{2,1,0:T(8,128)(2,1)S(1)} %all_to_all.10.x_ref, f32[2,1024]{1,0:T(2,128)S(1)} %copy-done.4, bf16[2,3,1024,128]{3,2,1,0:T(8,128)(2,1)S(1)} %copy-done, bf16[2,1024,128]{2,1,0:T(8,128)(2,1)S(1)} %copy-done.1, bf16[4128,128]{1,0:T(8,128)(2,1)S(1)} %copy-done.3, ...), custom_call_target="tpu_custom_call" | custom-call | flops 6442450944 | bytes 18874368 | tf_op jit(solution)/shard_map/blocks/pallas_call | solution.py:193
  99.4 22.0 %all_to_all.11 = bf16[128,24,128]{2,1,0:T(8,128)(2,1)S(1)} all-to-all(bf16[128,24,128]{2,1,0:T(8,128)(2,1)S(1)} %blocks.1), channel_id=1, replica_groups=mesh['seq'=16,'filt'=8] {'seq','filt'}, dimensions={0} | all-to-all | bytes 1572864 | tf_op jit(solution)/shard_map/all_to_all | solution.py:241
  121.5 0.9 slice.8
Async XLA Ops:
  0.6 81.2 %copy-start.1 = (bf16[2,1024,128]{2,1,0:T(8,128)(2,1)S(1)}, bf16[2,1024,128]{2,1,0:T(8,128)(2,1)}, u32[]{:S(2)}) copy-start(bf16[2,1024,128]{2,1,0:T(8,128)(2,1)} %mix_ref.3) | copy-start | bytes 1572868
  0.6 81.2 %copy-start.4 = (f32[2,1024]{1,0:T(2,128)S(1)}, f32[2,1024]{1,0:T(2,128)}, u32[]{:S(2)}) copy-start(f32[2,1024]{1,0:T(2,128)} %gain_ref.1) | copy-start | bytes 24580
  4.3 77.5 %copy-start = (bf16[2,3,1024,128]{3,2,1,0:T(8,128)(2,1)S(1)}, bf16[2,3,1024,128]{3,2,1,0:T(8,128)(2,1)}, u32[]{:S(2)}) copy-start(bf16[2,3,1024,128]{3,2,1,0:T(8,128)(2,1)} %conv_ref.3) | copy-start | bytes 4718596
  4.3 77.5 %copy-start.2 = (s32[10]{0:T(128)S(1)}, s32[10]{0:T(128)}, u32[]{:S(2)}) copy-start(s32[10]{0:T(128)} %stack.43.where_ref) | copy-start | bytes 124
  4.3 40.8 %collective-permute-start.2 = (bf16[4128,128]{1,0:T(8,128)(2,1)}, bf16[4128,128]{1,0:T(8,128)(2,1)S(1)}, u32[]{:S(2)}, u32[]{:S(2)}) collective-permute-start(bf16[4128,128]{1,0:T(8,128)(2,1)} %get-tuple-element.13.own_ref), channel_id=1, source_target_pairs={{0,4},{1,5},{2,6},{3,7},{4,16},{5,17},{6,18},{7,19},{8,28},{9,29},... | collective-permute-start | bytes 3170312 | tf_op jit(solution)/shard_map/ppermute | solution.py:47
  7.9 37.2 %collective-permute-start.1 = (bf16[4128,128]{1,0:T(8,128)(2,1)}, bf16[4128,128]{1,0:T(8,128)(2,1)S(1)}, u32[]{:S(2)}, u32[]{:S(2)}) collective-permute-start(bf16[4128,128]{1,0:T(8,128)(2,1)} %get-tuple-element.13.own_ref), channel_id=1, source_target_pairs={{0,3},{1,0},{2,1},{3,2},{4,7},{5,4},{6,5},{7,6},{8,9},{9,10},{10,1... | collective-permute-start | bytes 3170312 | tf_op jit(solution)/shard_map/ppermute | solution.py:47
  9.6 35.5 %collective-permute-start = (bf16[4128,128]{1,0:T(8,128)(2,1)}, bf16[4128,128]{1,0:T(8,128)(2,1)S(1)}, u32[]{:S(2)}, u32[]{:S(2)}) collective-permute-start(bf16[4128,128]{1,0:T(8,128)(2,1)} %get-tuple-element.13.own_ref), channel_id=1, source_target_pairs={{0,1},{1,2},{2,3},{3,0},{4,5},{5,6},{6,7},{7,4},{8,11},{9,8},{10,9... | collective-permute-start | bytes 3170312 | tf_op jit(solution)/shard_map/ppermute | solution.py:47
  45.1 14.1 %collective-permute-start.3 = (bf16[4128,128]{1,0:T(8,128)(2,1)S(1)}, bf16[4128,128]{1,0:T(8,128)(2,1)S(1)}, u32[]{:S(2)}, u32[]{:S(2)}) collective-permute-start(bf16[4128,128]{1,0:T(8,128)(2,1)S(1)} %collective-permute-done.rest_0_), channel_id=1, source_target_pairs={{0,4},{1,5},{2,6},{3,7},{4,16},{5,17},{6,18},{7,19},{8,28},{9,29},... | collective-permute-start | bytes 3170312 | tf_op jit(solution)/shard_map/ppermute | solution.py:47
  45.4 16.8 %collective-permute-start.6 = (bf16[4128,128]{1,0:T(8,128)(2,1)S(1)}, bf16[4128,128]{1,0:T(8,128)(2,1)S(1)}, u32[]{:S(2)}, u32[]{:S(2)}) collective-permute-start(bf16[4128,128]{1,0:T(8,128)(2,1)S(1)} %collective-permute-done.rest_0_), channel_id=1, source_target_pairs={{0,1},{1,2},{2,3},{3,0},{4,5},{5,6},{6,7},{7,4},{8,11},{9,8},{10,9... | collective-permute-start | bytes 3170312 | tf_op jit(solution)/shard_map/ppermute | solution.py:47
  47.3 15.5 %collective-permute-start.5 = (bf16[4128,128]{1,0:T(8,128)(2,1)S(1)}, bf16[4128,128]{1,0:T(8,128)(2,1)S(1)}, u32[]{:S(2)}, u32[]{:S(2)}) collective-permute-start(bf16[4128,128]{1,0:T(8,128)(2,1)S(1)} %collective-permute-done.rest_0_), channel_id=1, source_target_pairs={{0,8},{1,9},{2,10},{3,11},{4,12},{5,13},{6,14},{7,15},{8,0},{9,1},... | collective-permute-start | bytes 3170312 | tf_op jit(solution)/shard_map/ppermute | solution.py:47
  47.3 14.9 %collective-permute-start.8 = (bf16[4128,128]{1,0:T(8,128)(2,1)S(1)}, bf16[4128,128]{1,0:T(8,128)(2,1)S(1)}, u32[]{:S(2)}, u32[]{:S(2)}) collective-permute-start(bf16[4128,128]{1,0:T(8,128)(2,1)S(1)} %collective-permute-done.2.rest_6_), channel_id=1, source_target_pairs={{0,8},{1,9},{2,10},{3,11},{4,12},{5,13},{6,14},{7,15},{8,0},{9,1},... | collective-permute-start | bytes 3170312 | tf_op jit(solution)/shard_map/ppermute | solution.py:47
  59.2 14.0 %collective-permute-start.9 = (bf16[4128,128]{1,0:T(8,128)(2,1)S(1)}, bf16[4128,128]{1,0:T(8,128)(2,1)S(1)}, u32[]{:S(2)}, u32[]{:S(2)}) collective-permute-start(bf16[4128,128]{1,0:T(8,128)(2,1)S(1)} %collective-permute-done.1.rest_2_), channel_id=1, source_target_pairs={{0,4},{1,5},{2,6},{3,7},{4,16},{5,17},{6,18},{7,19},{8,28},{9,29},... | collective-permute-start | bytes 3170312 | tf_op jit(solution)/shard_map/ppermute | solution.py:47
  60.7 17.3 %collective-permute-start.12 = (bf16[4128,128]{1,0:T(8,128)(2,1)S(1)}, bf16[4128,128]{1,0:T(8,128)(2,1)S(1)}, u32[]{:S(2)}, u32[]{:S(2)}) collective-permute-start(bf16[4128,128]{1,0:T(8,128)(2,1)S(1)} %collective-permute-done.3.rest_8_), channel_id=1, source_target_pairs={{0,1},{1,2},{2,3},{3,0},{4,5},{5,6},{6,7},{7,4},{8,11},{9,8},{10,9... | collective-permute-start | bytes 3170312 | tf_op jit(solution)/shard_map/ppermute | solution.py:47
  62.2 15.8 %collective-permute-start.4 = (bf16[4128,128]{1,0:T(8,128)(2,1)S(1)}, bf16[4128,128]{1,0:T(8,128)(2,1)S(1)}, u32[]{:S(2)}, u32[]{:S(2)}) collective-permute-start(bf16[4128,128]{1,0:T(8,128)(2,1)S(1)} %collective-permute-done.1.rest_2_), channel_id=1, source_target_pairs={{0,8},{1,9},{2,10},{3,11},{4,12},{5,13},{6,14},{7,15},{8,0},{9,1},... | collective-permute-start | bytes 3170312 | tf_op jit(solution)/shard_map/ppermute | solution.py:47
  62.3 15.8 %collective-permute-start.11 = (bf16[4128,128]{1,0:T(8,128)(2,1)S(1)}, bf16[4128,128]{1,0:T(8,128)(2,1)S(1)}, u32[]{:S(2)}, u32[]{:S(2)}) collective-permute-start(bf16[4128,128]{1,0:T(8,128)(2,1)S(1)} %collective-permute-done.3.rest_8_), channel_id=1, source_target_pairs={{0,8},{1,9},{2,10},{3,11},{4,12},{5,13},{6,14},{7,15},{8,0},{9,1},... | collective-permute-start | bytes 3170312 | tf_op jit(solution)/shard_map/ppermute | solution.py:47
  62.8 15.2 %collective-permute-start.7 = (bf16[4128,128]{1,0:T(8,128)(2,1)S(1)}, bf16[4128,128]{1,0:T(8,128)(2,1)S(1)}, u32[]{:S(2)}, u32[]{:S(2)}) collective-permute-start(bf16[4128,128]{1,0:T(8,128)(2,1)S(1)} %collective-permute-done.6.rest_4_), channel_id=1, source_target_pairs={{0,8},{1,9},{2,10},{3,11},{4,12},{5,13},{6,14},{7,15},{8,0},{9,1},... | collective-permute-start | bytes 3170312 | tf_op jit(solution)/shard_map/ppermute | solution.py:47
  73.2 7.1 %collective-permute-start.10 = (bf16[4128,128]{1,0:T(8,128)(2,1)S(1)}, bf16[4128,128]{1,0:T(8,128)(2,1)S(1)}, u32[]{:S(2)}, u32[]{:S(2)}) collective-permute-start(bf16[4128,128]{1,0:T(8,128)(2,1)S(1)} %collective-permute-done.9.rest_10_), channel_id=1, source_target_pairs={{0,8},{1,9},{2,10},{3,11},{4,12},{5,13},{6,14},{7,15},{8,0},{9,1},... | collective-permute-start | bytes 3170312 | tf_op jit(solution)/shard_map/ppermute | solution.py:47
  78.0 3.8 %collective-permute-start.13 = (bf16[4128,128]{1,0:T(8,128)(2,1)S(1)}, bf16[4128,128]{1,0:T(8,128)(2,1)S(1)}, u32[]{:S(2)}, u32[]{:S(2)}) collective-permute-start(bf16[4128,128]{1,0:T(8,128)(2,1)S(1)} %collective-permute-done.12.rest_12_), channel_id=1, source_target_pairs={{0,8},{1,9},{2,10},{3,11},{4,12},{5,13},{6,14},{7,15},{8,0},{9,1},... | collective-permute-start | bytes 3170312 | tf_op jit(solution)/shard_map/ppermute | solution.py:47
  81.8 1.2 %copy-start.3 = (bf16[4128,128]{1,0:T(8,128)(2,1)S(1)}, bf16[4128,128]{1,0:T(8,128)(2,1)}, u32[]{:S(2)}) copy-start(bf16[4128,128]{1,0:T(8,128)(2,1)} %get-tuple-element.13.own_ref) | copy-start | bytes 3170308

commit v4 on v3

v4 whole, which is shorter than its diff:
```python
import functools

import jax
import jax.numpy as jnp
from jax import lax
from jax.experimental import pallas as pl
from jax.experimental.pallas import tpu as pltpu
from jax.sharding import PartitionSpec as P

LAYERS = 2
C = 1024
BLOCKS = 16
LANES = 128
SHARDS = 8
RES = 24
ROWS = BLOCKS * RES
EXTRA = 16
HALF = C // 2
PART = 4 * HALF + EXTRA
AXES = ("seq", "filt")


def coords(i):
    z, i = i % 4, i // 4
    yl, i = i % 2, i // 2
    c, i = i % 2, i // 2
    yh, x = i % 2, i // 2
    return x, yh * 2 + yl, z, c


def linear(x, y, z, c):
    x, y, z = x % 4, y % 4, z % 4
    return (((x * 2 + y // 2) * 2 + c) * 2 + y % 2) * 4 + z


def route(step):
    return [(i, linear(*step(*coords(i)))) for i in range(128)]


Z_AWAY = route(lambda x, y, z, c: (x, y, z + 1 - 2 * c, c))
Z_BACK = route(lambda x, y, z, c: (x, y, z - 1 + 2 * c, c))
Y_SIDE = route(lambda x, y, z, c: (x, y + 1 - 2 * c, z, c))
SWAP = route(lambda x, y, z, c: (x, y, z, 1 - c))


def send(block, path):
    return lax.ppermute(block, AXES, path)


def three_parts(v):
    hi = v.astype(jnp.bfloat16).astype(jnp.float32)
    mid = (v - hi).astype(jnp.bfloat16).astype(jnp.float32)
    lo = v - hi - mid
    return [hi, mid, lo]


def prepare_kernel(where_ref, tokens_ref, conv_ref, mix_ref, conv_bias_ref, mix_bias_ref, padded_ref, own_ref, *rest):
    singles, sems = rest[:LAYERS], rest[LAYERS]
    length = tokens_ref.shape[0]
    rows = pl.ds(pl.multiple_of(where_ref[0] * HALF, HALF), HALF)
    moves = []
    for layer in range(LAYERS):
        for t in range(4):
            source = conv_ref.at[layer, t, rows] if t < 3 else mix_ref.at[layer, rows]
            moves.append((source, own_ref.at[pl.ds(layer * PART + t * HALF, HALF)]))
            moves.append((source, singles[layer].at[pl.ds(t * HALF, HALF)]))
    moves.append((tokens_ref, padded_ref.at[pl.ds(0, length)]))
    copies = [pltpu.make_async_copy(a, b, sems.at[i]) for i, (a, b) in enumerate(moves)]
    for copy in copies:
        copy.start()
    padded_ref[length:, :] = jnp.zeros((128 * RES - length, LANES), jnp.bfloat16)
    for layer in range(LAYERS):
        lines = three_parts(conv_bias_ref[layer:layer + 1, :]) + three_parts(mix_bias_ref[layer:layer + 1, :])
        lines.append(jnp.zeros((EXTRA - 6, LANES), jnp.float32))
        block = jnp.concatenate(lines, axis=0).astype(jnp.bfloat16)
        own_ref[layer * PART + 4 * HALF:(layer + 1) * PART, :] = block
        singles[layer][4 * HALF:, :] = block
    for copy in copies:
        copy.wait()


def prepare(where, tokens, conv, mix, conv_bias, mix_bias):
    anywhere = pl.BlockSpec(memory_space=pl.ANY)
    vmem = pl.BlockSpec(memory_space=pltpu.VMEM)
    single = jax.ShapeDtypeStruct((PART, LANES), jnp.bfloat16)
    return pl.pallas_call(
        prepare_kernel,
        out_shape=[
            jax.ShapeDtypeStruct((128 * RES, LANES), jnp.bfloat16),
            jax.ShapeDtypeStruct((LAYERS * PART, LANES), jnp.bfloat16),
        ] + [single] * LAYERS,
        in_specs=[pl.BlockSpec(memory_space=pltpu.SMEM), anywhere, anywhere, anywhere, vmem, vmem],
        out_specs=[vmem] * (2 + LAYERS),
        scratch_shapes=[pltpu.SemaphoreType.DMA((1 + 8 * LAYERS,))],
        compiler_params=pltpu.CompilerParams(vmem_limit_bytes=60 * 2**20),
        cost_estimate=pl.CostEstimate(flops=0, bytes_accessed=6 * 2**20, transcendentals=0),
        name="prepare",
    )(where, tokens, conv, mix, conv_bias, mix_bias)


def layer_kernel(layer, bases, where_ref, x_ref, gain_ref, conv_ref, mix_ref, *rest):
    parts = rest[:2 * SHARDS - 1]
    out_ref, w, mine, bias, x, normed, n, act, mixing, sems, mine_sems, bias_sem = rest[2 * SHARDS - 1:]
    width = 2 * LANES
    first, last = layer == 0, layer == LAYERS - 1

    def half(i):
        return pl.ds(pl.multiple_of(where_ref[i] * HALF, HALF), HALF)

    def home(k):
        return pl.ds(pl.multiple_of(where_ref[2 + k] * LANES, LANES), LANES)

    arriving = []
    for k in range(SHARDS):
        if k == 0:
            moves = [
                (conv_ref.at[layer], mine.at[pl.ds(0, 3)], mine_sems.at[0]),
                (mix_ref.at[layer], mine.at[3], mine_sems.at[1]),
                (parts[0].at[pl.ds(bases[0] + 4 * HALF, EXTRA)], bias, bias_sem.at[0]),
            ]
        else:
            moves = []
            for p in (2 * k - 1, 2 * k):
                moves.append((parts[p].at[pl.ds(bases[p], PART)], w.at[p - 1], sems.at[p - 1]))
        copies = [pltpu.make_async_copy(*move) for move in moves]
        for copy in copies:
            copy.start()
        arriving.append(copies)

    if first:
        for b in range(BLOCKS):
            for f in range(SHARDS):
                x[b * RES:(b + 1) * RES, f * LANES:(f + 1) * LANES] = x_ref[b * SHARDS + f].astype(jnp.float32)
    else:
        x[...] = x_ref[...].astype(jnp.float32)
    wide = x[...]
    scale = lax.rsqrt(jnp.mean(wide * wide, axis=-1, keepdims=True) + 1e-06)
    normed[...] = wide * scale * gain_ref[layer:layer + 1, :]
    shift = RES * 2**layer
    edge = jnp.zeros((shift, HALF), jnp.float32)
    for i in range(2):
        here = normed[:, half(i)]
        earlier = jnp.concatenate([edge, here[:ROWS - shift]], axis=0)
        later = jnp.concatenate([here[shift:], edge], axis=0)
        for t, rows in enumerate((earlier, here, later)):
            start = (3 * i + t) * HALF
            n[:, start:start + HALF] = rows.astype(jnp.bfloat16)

    def conv_column(k):
        if k == 0:
            return jnp.concatenate([mine[t, half(i), :] for i in range(2) for t in range(3)], axis=0)
        return jnp.concatenate([w[2 * (k - 1) + i, :3 * HALF, :] for i in range(2)], axis=0)

    def mix_column(k):
        if k == 0:
            return jnp.concatenate([mine[3, half(i), :] for i in range(2)], axis=0)
        return jnp.concatenate([w[2 * (k - 1) + i, 3 * HALF:4 * HALF, :] for i in range(2)], axis=0)

    def bias_row(k, start):
        rows = bias[...] if k == 0 else w[2 * (k - 1), 4 * HALF:PART, :]
        rows = rows.astype(jnp.float32)
        return rows[start:start + 1] + rows[start + 1:start + 2] + rows[start + 2:start + 3]

    for j in range(SHARDS // 2):
        pair = (2 * j, 2 * j + 1)
        for k in pair:
            for copy in arriving[k]:
                copy.wait()
        taps = jnp.concatenate([conv_column(k) for k in pair], axis=1)
        hidden = jnp.dot(n[...], taps, preferred_element_type=jnp.float32)
        hidden = hidden + jnp.concatenate([bias_row(k, 0) for k in pair], axis=1)
        done = (hidden * (1.0 + lax.erf(hidden * 0.7071067811865476)) * 0.5).astype(jnp.bfloat16)
        for h, k in enumerate(pair):
            act[:, home(k)] = done[:, h * LANES:(h + 1) * LANES]

    for i in range(2):
        mixing[:, i * HALF:(i + 1) * HALF] = act[:, half(i)]

    for j in range(SHARDS // 2):
        pair = (2 * j, 2 * j + 1)
        mixed = jnp.dot(mixing[...], jnp.concatenate([mix_column(k) for k in pair], axis=1), preferred_element_type=jnp.float32)
        mixed = mixed + jnp.concatenate([bias_row(k, 3) for k in pair], axis=1)
        for h, k in enumerate(pair):
            total = x[:, home(k)] + mixed[:, h * LANES:(h + 1) * LANES]
            if last:
                f = where_ref[2 + k]
                for b in range(BLOCKS):
                    out_ref[b * SHARDS + f] = total[b * RES:(b + 1) * RES].astype(jnp.bfloat16)
            else:
                out_ref[:, home(k)] = total.astype(jnp.bfloat16)


def run_layer(layer, where, x, gain, conv, mix, parts, bases):
    vmem = pl.BlockSpec(memory_space=pltpu.VMEM)
    anywhere = pl.BlockSpec(memory_space=pl.ANY)
    out = (BLOCKS * SHARDS, RES, LANES) if layer == LAYERS - 1 else (ROWS, C)
    return pl.pallas_call(
        functools.partial(layer_kernel, layer, bases),
        out_shape=jax.ShapeDtypeStruct(out, jnp.bfloat16),
        in_specs=[pl.BlockSpec(memory_space=pltpu.SMEM), vmem, vmem] + [anywhere] * (2 + len(parts)),
        out_specs=vmem,
        scratch_shapes=[
            pltpu.VMEM((len(parts) - 1, PART, LANES), jnp.bfloat16),
            pltpu.VMEM((4, C, LANES), jnp.bfloat16),
            pltpu.VMEM((EXTRA, LANES), jnp.bfloat16),
            pltpu.VMEM((ROWS, C), jnp.float32),
            pltpu.VMEM((ROWS, C), jnp.float32),
            pltpu.VMEM((ROWS, 3 * C), jnp.bfloat16),
            pltpu.VMEM((ROWS, C), jnp.bfloat16),
            pltpu.VMEM((ROWS, C), jnp.bfloat16),
            pltpu.SemaphoreType.DMA((len(parts) - 1,)),
            pltpu.SemaphoreType.DMA((2,)),
            pltpu.SemaphoreType.DMA((1,)),
        ],
        compiler_params=pltpu.CompilerParams(vmem_limit_bytes=24 * 2**20),
        cost_estimate=pl.CostEstimate(flops=8 * ROWS * C * C, bytes_accessed=9 * 2**20, transcendentals=ROWS * C),
        name=f"layer{layer}",
    )(where, x, gain, conv, mix, *parts)


def per_device(tokens, conv_weight, conv_bias, mix_weight, mix_bias, norm_gain):
    seq, filt = lax.axis_index("seq"), lax.axis_index("filt")
    core = seq & 1
    z, yl = filt & 3, filt >> 2
    zs = [z, (z - 1 + 2 * core) & 3, (z + 1 - 2 * core) & 3, (z + 2) & 3]
    shards = [yl * 4 + v for v in zs] + [(1 - yl) * 4 + v for v in zs]
    where = jnp.stack([core, 1 - core] + shards).astype(jnp.int32)

    padded, own, *single = prepare(where, tokens, conv_weight, mix_weight, conv_bias, mix_bias)
    near = [send(v, Z_AWAY) for v in single]
    far = [send(v, Z_BACK) for v in single]
    cross = send(own, Y_SIDE)
    x = lax.all_to_all(padded.reshape(128, RES, LANES), AXES, split_axis=0, concat_axis=0, tiled=True)
    near, far, cross, x = lax.optimization_barrier((near, far, cross, x))
    swapped_cross = send(cross, SWAP)
    for layer in range(LAYERS):
        beyond = send(near[layer], Z_AWAY)
        cross_near = send(near[layer], Y_SIDE)
        far[layer], cross_near, beyond, x = lax.optimization_barrier((far[layer], cross_near, beyond, x))
        cross_far = send(far[layer], Y_SIDE)
        cross_beyond = send(cross_near, Z_AWAY)
        if layer + 1 < LAYERS:
            cross_far, cross_beyond, near[layer + 1] = lax.optimization_barrier((cross_far, cross_beyond, near[layer + 1]))
        mine = [near[layer], far[layer], beyond, cross, cross_near, cross_far, cross_beyond]
        swapped = [swapped_cross if v is cross else send(v, SWAP) for v in mine]
        parts, bases = [single[layer]], [0]
        for k, i in enumerate([1, 0, 2, 3, 5, 4, 6]):
            parts += [mine[k], swapped[i]]
            bases += [layer * PART if mine[k] is cross else 0] * 2
        x = run_layer(layer, where, x, norm_gain, conv_weight, mix_weight, parts, bases)
    y = lax.all_to_all(x, AXES, split_axis=0, concat_axis=0, tiled=True)
    return y.reshape(128 * RES, LANES)[:tokens.shape[0]]


def solution(mesh):
    in_specs = (
        P("seq", "filt"),
        P(None, None, None, "filt"),
        P(None, "filt"),
        P(None, None, "filt"),
        P(None, "filt"),
        P(),
    )
    out_specs = P("seq", "filt")
    return jax.shard_map(
        per_device, mesh=mesh, in_specs=in_specs, out_specs=out_specs, check_vma=False
    )
```

time: 123 us -> 137 us (1.11)
  blocking collectives: 55.4 us -> 22.7 us
  waiting for transfers between devices: 25.6 us -> 50.8 us
  starting transfers between devices: 18.5 us -> 38.4 us
  Pallas kernels: 20 us -> 22 us
    all_to_all x1 -> x0, blocking collectives: 33.4 us -> none  [per_device(): lax.all_to_all(padded.reshape(128, RES, LANES), AXES, split_axis=0, conca...]
    ppermute x14 -> x26, waiting for transfers between devices: 25.6 us -> 50.8 us  [send(): return lax.ppermute(block, AXES, path)]
    ppermute x14 -> x26, starting transfers between devices: 18.5 us -> 28.8 us  [send(): return lax.ppermute(block, AXES, path)]
    all_to_all x0 -> x1, starting transfers between devices: none -> 9.62 us  [per_device(): lax.all_to_all(padded.reshape(128, RES, LANES), AXES, split_axis=0, conca...]
    pallas_call x1 -> x2, Pallas kernels: 16.4 us -> 17.7 us  [run_layer(): pl.pallas_call(functools.partial(layer_kernel, layer, bases), out_shape=j...]
  transfers between devices with their start and end apart: 14 -> 27, of which waited for: 4 -> 10; matrix products, arithmetic and copies ran while one was open for 0% -> 0% of each run, Pallas kernels for 0% -> 7%
where the time goes in v4:
time: 137 us
  waiting for transfers between devices  50.8 us (37%)
  starting transfers between devices  38.4 us (28%)
  blocking collectives  22.7 us (17%)
  Pallas kernels  22 us (16%)
  local copies, waits for them, and re-layouts  2.59 us (2%)
    ppermute x26, waiting for transfers between devices, send(): return lax.ppermute(block, AXES, path)  50.8 us
    ppermute x26, starting transfers between devices, send(): return lax.ppermute(block, AXES, path)  28.8 us
    all_to_all x1, blocking collectives, per_device(): y = lax.all_to_all(x, AXES, split_axis=0, concat_axis=0, tiled=True)  22.7 us
    pallas_call x2, Pallas kernels, run_layer(): pl.pallas_call(functools.partial(layer_kernel, layer, bases), out_shape=j...  17.7 us
    all_to_all x1, starting transfers between devices, per_device(): lax.all_to_all(padded.reshape(128, RES, LANES), AXES, split_axis=0, conca...  9.62 us
    pallas_call x1, Pallas kernels, prepare(): pl.pallas_call(prepare_kernel, out_shape=[jax.ShapeDtypeStruct((128 * RES...  4.35 us
  transfers between devices with their start and end apart: 27, of which 10 were waited for; matrix products, arithmetic and copies ran while one was open for 0% of the time, Pallas kernels for 7%

profile of v4, /device:TPU:1, one launch (start us, length us, event | category | flops | bytes accessed | tf_op | source)
XLA Modules:
  0.0 136.8 jit_solution(6908801152222631333)
XLA Ops:
  0.0 0.6 stack.43.where_ref
  0.6 4.4 %prepare.1 = (bf16[3072,128]{1,0:T(8,128)(2,1)}, bf16[4128,128]{1,0:T(8,128)(2,1)}, bf16[2064,128]{1,0:T(8,128)(2,1)}, bf16[2064,128]{1,0:T(8,128)(2,1)}) custom-call(s32[10]{0:T(128)} %stack.43.where_ref, bf16[2688,128]{1,0:T(8,128)(2,1)} %tokens_ref.1, bf16[2,3,1024,128]{3,2,1,0:T(8,128)(2,1)} %conv_ref.5, bf16[2,1024,128]{2,1,0:T(8,128)(2,1)} %mix_ref.5, ...), custom_call_target="tpu_custom_call" | custom-call | bytes 6291456 | tf_op jit(solution)/shard_map/prepare/pallas_call | solution.py:86
  5.0 0.0 copy-start
  5.0 0.0 copy-start.4
  5.0 3.6 %collective-permute-start.4 = (bf16[4128,128]{1,0:T(8,128)(2,1)}, bf16[4128,128]{1,0:T(8,128)(2,1)S(1)}, u32[]{:S(2)}, u32[]{:S(2)}) collective-permute-start(bf16[4128,128]{1,0:T(8,128)(2,1)} %get-tuple-element.28), channel_id=1, source_target_pairs={{0,4},{1,5},{2,6},{3,7},{4,16},{5,17},{6,18},{7,19},{8,28},{9,29},... | collective-permute-start | bytes 3170312 | tf_op jit(solution)/shard_map/ppermute | solution.py:47
  8.6 9.6 %all-to-all-start = ((bf16[128,24,128]{2,1,0:T(8,128)(2,1)}), bf16[128,24,128]{2,1,0:T(8,128)(2,1)}, u32[]{:S(2)}, u32[]{:S(2)}) async-start(bf16[128,24,128]{2,1,0:T(8,128)(2,1)} %bitcast.12), calls=%async_computation | async-start | bytes 1572864 | tf_op jit(solution)/shard_map/all_to_all | solution.py:233
  18.3 3.3 %collective-permute-start = (bf16[2064,128]{1,0:T(8,128)(2,1)}, bf16[2064,128]{1,0:T(8,128)(2,1)}, u32[]{:S(2)}, u32[]{:S(2)}) collective-permute-start(bf16[2064,128]{1,0:T(8,128)(2,1)} %get-tuple-element.26.rest_0_), channel_id=1, source_target_pairs={{0,1},{1,2},{2,3},{3,0},{4,5},{5,6},{6,7},{7,4},{8,11},{9,8},{10,9... | collective-permute-start | bytes 1585160 | tf_op jit(solution)/shard_map/ppermute | solution.py:47
  21.6 0.3 collective-permute-start.1
  21.9 1.2 collective-permute-start.2
  23.1 0.0 collective-permute-start.3
  23.1 16.9 %collective-permute-done.rest_1_ = bf16[2064,128]{1,0:T(8,128)(2,1)} collective-permute-done((bf16[2064,128]{1,0:T(8,128)(2,1)}, bf16[2064,128]{1,0:T(8,128)(2,1)}, u32[]{:S(2)}, u32[]{:S(2)}) %collective-permute-start) | collective-permute-done | bytes 528416 | tf_op jit(solution)/shard_map/ppermute | solution.py:47
  40.0 11.3 %collective-permute-done.1.rest_1_ = bf16[2064,128]{1,0:T(8,128)(2,1)} collective-permute-done((bf16[2064,128]{1,0:T(8,128)(2,1)}, bf16[2064,128]{1,0:T(8,128)(2,1)}, u32[]{:S(2)}, u32[]{:S(2)}) %collective-permute-start.1) | collective-permute-done | bytes 528416 | tf_op jit(solution)/shard_map/ppermute | solution.py:47
  51.3 0.0 collective-permute-done.2.rest_3_
  51.4 2.5 %collective-permute-done.3.rest_3_ = bf16[2064,128]{1,0:T(8,128)(2,1)} collective-permute-done((bf16[2064,128]{1,0:T(8,128)(2,1)}, bf16[2064,128]{1,0:T(8,128)(2,1)}, u32[]{:S(2)}, u32[]{:S(2)}) %collective-permute-start.3) | collective-permute-done | bytes 528416 | tf_op jit(solution)/shard_map/ppermute | solution.py:47
  53.9 2.0 %collective-permute-start.5 = (bf16[2064,128]{1,0:T(8,128)(2,1)}, bf16[2064,128]{1,0:T(8,128)(2,1)S(1)}, u32[]{:S(2)}, u32[]{:S(2)}) collective-permute-start(bf16[2064,128]{1,0:T(8,128)(2,1)} %collective-permute-done.rest_1_), channel_id=1, source_target_pairs={{0,4},{1,5},{2,6},{3,7},{4,16},{5,17},{6,18},{7,19},{8,28},{9,29},... | collective-permute-start | bytes 1585160 | tf_op jit(solution)/shard_map/ppermute | solution.py:47
  55.9 0.9 collective-permute-start.6
  56.8 5.8 %collective-permute-done.5.rest_9_ = bf16[2064,128]{1,0:T(8,128)(2,1)S(1)} collective-permute-done((bf16[2064,128]{1,0:T(8,128)(2,1)}, bf16[2064,128]{1,0:T(8,128)(2,1)S(1)}, u32[]{:S(2)}, u32[]{:S(2)}) %collective-permute-start.5) | collective-permute-done | bytes 528416 | tf_op jit(solution)/shard_map/ppermute | solution.py:47
  62.6 1.9 %collective-permute-done.6.rest_5_ = bf16[2064,128]{1,0:T(8,128)(2,1)S(1)} collective-permute-done((bf16[2064,128]{1,0:T(8,128)(2,1)}, bf16[2064,128]{1,0:T(8,128)(2,1)S(1)}, u32[]{:S(2)}, u32[]{:S(2)}) %collective-permute-start.6) | collective-permute-done | bytes 528416 | tf_op jit(solution)/shard_map/ppermute | solution.py:47
  64.4 1.2 collective-permute-start.7
  65.7 1.2 collective-permute-start.8
  66.8 0.2 collective-permute-start.12
  67.0 0.3 collective-permute-start.14
  67.3 0.2 collective-permute-start.11
  67.5 5.5 %collective-permute-done.7.rest_11_ = bf16[2064,128]{1,0:T(8,128)(2,1)S(1)} collective-permute-done((bf16[2064,128]{1,0:T(8,128)(2,1)}, bf16[2064,128]{1,0:T(8,128)(2,1)S(1)}, u32[]{:S(2)}, u32[]{:S(2)}) %collective-permute-start.7) | collective-permute-done | bytes 528416 | tf_op jit(solution)/shard_map/ppermute | solution.py:47
  73.0 3.3 %collective-permute-start.13 = (bf16[2064,128]{1,0:T(8,128)(2,1)S(1)}, bf16[2064,128]{1,0:T(8,128)(2,1)S(1)}, u32[]{:S(2)}, u32[]{:S(2)}) collective-permute-start(bf16[2064,128]{1,0:T(8,128)(2,1)S(1)} %collective-permute-done.6.rest_5_), channel_id=1, source_target_pairs={{0,8},{1,9},{2,10},{3,11},{4,12},{5,13},{6,14},{7,15},{8,0},{9,1},... | collective-permute-start | bytes 1585160 | tf_op jit(solution)/shard_map/ppermute | solution.py:47
  76.3 1.1 collective-permute-start.16
  77.4 0.0 collective-permute-done.12.rest_4_
  77.4 0.0 collective-permute-start.15
  77.4 0.5 collective-permute-start.17
  77.9 0.0 collective-permute-done.13.rest_6_
  77.9 0.3 collective-permute-start.10
  78.3 0.7 collective-permute-done.16.rest_12_
  79.0 1.6 %collective-permute-start.9 = (bf16[2064,128]{1,0:T(8,128)(2,1)}, bf16[2064,128]{1,0:T(8,128)(2,1)S(1)}, u32[]{:S(2)}, u32[]{:S(2)}) collective-permute-start(bf16[2064,128]{1,0:T(8,128)(2,1)} %collective-permute-done.1.rest_1_), channel_id=1, source_target_pairs={{0,4},{1,5},{2,6},{3,7},{4,16},{5,17},{6,18},{7,19},{8,28},{9,29},... | collective-permute-start | bytes 1585160 | tf_op jit(solution)/shard_map/ppermute | solution.py:47
  80.7 0.0 copy-start.3
  80.7 1.0 copy-done.3
  81.7 9.2 %layer0.1.x_ref = bf16[384,1024]{1,0:T(8,128)(2,1)S(1)} custom-call(s32[10]{0:T(128)S(1)} %copy-done.5, bf16[128,24,128]{2,1,0:T(8,128)(2,1)} %all-to-all-done.x_ref, f32[2,1024]{1,0:T(2,128)S(1)} %copy-done.4, bf16[2,3,1024,128]{3,2,1,0:T(8,128)(2,1)S(1)} %copy-done, bf16[2,1024,128]{2,1,0:T(8,128)(2,1)S(1)} %copy-done.1, bf16[2064,128]{1,0:T(8,128)(2,1)S(1)} %copy-done.3, ...), custom_call_target="tpu_custom_call" | custom-call | flops 3221225472 | bytes 9437184 | tf_op jit(solution)/shard_map/layer0/pallas_call | solution.py:197
  90.9 1.9 %collective-permute-start.21 = (bf16[2064,128]{1,0:T(8,128)(2,1)}, bf16[2064,128]{1,0:T(8,128)(2,1)S(1)}, u32[]{:S(2)}, u32[]{:S(2)}) collective-permute-start(bf16[2064,128]{1,0:T(8,128)(2,1)} %collective-permute-done.3.rest_3_), channel_id=1, source_target_pairs={{0,4},{1,5},{2,6},{3,7},{4,16},{5,17},{6,18},{7,19},{8,28},{9,29},... | collective-permute-start | bytes 1585160 | tf_op jit(solution)/shard_map/ppermute | solution.py:47
  92.9 1.8 %collective-permute-start.24 = (bf16[2064,128]{1,0:T(8,128)(2,1)S(1)}, bf16[2064,128]{1,0:T(8,128)(2,1)S(1)}, u32[]{:S(2)}, u32[]{:S(2)}) collective-permute-start(bf16[2064,128]{1,0:T(8,128)(2,1)S(1)} %collective-permute-done.9.rest_9_), channel_id=1, source_target_pairs={{0,1},{1,2},{2,3},{3,0},{4,5},{5,6},{6,7},{7,4},{8,11},{9,8},{10,9... | collective-permute-start | bytes 1585160 | tf_op jit(solution)/shard_map/ppermute | solution.py:47
  94.7 0.5 collective-permute-start.23
  95.2 0.0 collective-permute-start.20
  95.2 4.5 %collective-permute-done.21.rest_11_ = bf16[2064,128]{1,0:T(8,128)(2,1)S(1)} collective-permute-done((bf16[2064,128]{1,0:T(8,128)(2,1)}, bf16[2064,128]{1,0:T(8,128)(2,1)S(1)}, u32[]{:S(2)}, u32[]{:S(2)}) %collective-permute-start.21) | collective-permute-done | bytes 528416 | tf_op jit(solution)/shard_map/ppermute | solution.py:47
  99.8 2.6 %collective-permute-start.22 = (bf16[2064,128]{1,0:T(8,128)(2,1)S(1)}, bf16[2064,128]{1,0:T(8,128)(2,1)S(1)}, u32[]{:S(2)}, u32[]{:S(2)}) collective-permute-start(bf16[2064,128]{1,0:T(8,128)(2,1)S(1)} %collective-permute-done.21.rest_11_), channel_id=1, source_target_pairs={{0,8},{1,9},{2,10},{3,11},{4,12},{5,13},{6,14},{7,15},{8,0},{9,1},... | collective-permute-start | bytes 1585160 | tf_op jit(solution)/shard_map/ppermute | solution.py:47
  102.3 0.7 collective-permute-start.25
  103.0 0.9 collective-permute-done.22.rest_10_
  103.9 0.8 collective-permute-done.25.rest_14_
  104.6 8.5 %layer1.1 = bf16[128,24,128]{2,1,0:T(8,128)(2,1)S(1)} custom-call(s32[10]{0:T(128)S(1)} %copy-done.5, bf16[384,1024]{1,0:T(8,128)(2,1)S(1)} %layer0.1.x_ref, f32[2,1024]{1,0:T(2,128)S(1)} %copy-done.4, bf16[2,3,1024,128]{3,2,1,0:T(8,128)(2,1)S(1)} %copy-done, bf16[2,1024,128]{2,1,0:T(8,128)(2,1)S(1)} %copy-done.1, bf16[2064,128]{1,0:T(8,128)(2,1)S(1)} %copy-done.2, ...), custom_call_target="tpu_custom_call" | custom-call | flops 3221225472 | bytes 9437184 | tf_op jit(solution)/shard_map/layer1/pallas_call | solution.py:197
  113.1 22.7 %all_to_all.10 = bf16[128,24,128]{2,1,0:T(8,128)(2,1)S(1)} all-to-all(bf16[128,24,128]{2,1,0:T(8,128)(2,1)S(1)} %layer1.1), channel_id=1, replica_groups=mesh['seq'=16,'filt'=8] {'seq','filt'}, dimensions={0} | all-to-all | bytes 1572864 | tf_op jit(solution)/shard_map/all_to_all | solution.py:251
  135.9 0.9 slice.8
  (24 shorter events, 0.1 us)
Async XLA Ops:
  0.6 80.0 %copy-start.1 = (bf16[2,1024,128]{2,1,0:T(8,128)(2,1)S(1)}, bf16[2,1024,128]{2,1,0:T(8,128)(2,1)}, u32[]{:S(2)}) copy-start(bf16[2,1024,128]{2,1,0:T(8,128)(2,1)} %mix_ref.5) | copy-start | bytes 1572868
  5.0 75.7 %copy-start = (bf16[2,3,1024,128]{3,2,1,0:T(8,128)(2,1)S(1)}, bf16[2,3,1024,128]{3,2,1,0:T(8,128)(2,1)}, u32[]{:S(2)}) copy-start(bf16[2,3,1024,128]{3,2,1,0:T(8,128)(2,1)} %conv_ref.5) | copy-start | bytes 4718596
  5.0 75.7 %copy-start.4 = (f32[2,1024]{1,0:T(2,128)S(1)}, f32[2,1024]{1,0:T(2,128)}, u32[]{:S(2)}) copy-start(f32[2,1024]{1,0:T(2,128)} %gain_ref.3) | copy-start | bytes 24580
  5.0 75.7 %copy-start.5 = (s32[10]{0:T(128)S(1)}, s32[10]{0:T(128)}, u32[]{:S(2)}) copy-start(s32[10]{0:T(128)} %stack.43.where_ref) | copy-start | bytes 124
  5.0 48.9 %collective-permute-start.4 = (bf16[4128,128]{1,0:T(8,128)(2,1)}, bf16[4128,128]{1,0:T(8,128)(2,1)S(1)}, u32[]{:S(2)}, u32[]{:S(2)}) collective-permute-start(bf16[4128,128]{1,0:T(8,128)(2,1)} %get-tuple-element.28), channel_id=1, source_target_pairs={{0,4},{1,5},{2,6},{3,7},{4,16},{5,17},{6,18},{7,19},{8,28},{9,29},... | collective-permute-start | bytes 3170312 | tf_op jit(solution)/shard_map/ppermute | solution.py:47
  8.6 45.2 %all-to-all-start = ((bf16[128,24,128]{2,1,0:T(8,128)(2,1)}), bf16[128,24,128]{2,1,0:T(8,128)(2,1)}, u32[]{:S(2)}, u32[]{:S(2)}) async-start(bf16[128,24,128]{2,1,0:T(8,128)(2,1)} %bitcast.12), calls=%async_computation | async-start | bytes 1572864 | tf_op jit(solution)/shard_map/all_to_all | solution.py:233
  18.3 21.8 %collective-permute-start = (bf16[2064,128]{1,0:T(8,128)(2,1)}, bf16[2064,128]{1,0:T(8,128)(2,1)}, u32[]{:S(2)}, u32[]{:S(2)}) collective-permute-start(bf16[2064,128]{1,0:T(8,128)(2,1)} %get-tuple-element.26.rest_0_), channel_id=1, source_target_pairs={{0,1},{1,2},{2,3},{3,0},{4,5},{5,6},{6,7},{7,4},{8,11},{9,8},{10,9... | collective-permute-start | bytes 1585160 | tf_op jit(solution)/shard_map/ppermute | solution.py:47
  21.6 29.8 %collective-permute-start.1 = (bf16[2064,128]{1,0:T(8,128)(2,1)}, bf16[2064,128]{1,0:T(8,128)(2,1)}, u32[]{:S(2)}, u32[]{:S(2)}) collective-permute-start(bf16[2064,128]{1,0:T(8,128)(2,1)} %get-tuple-element.27.rest_0_), channel_id=1, source_target_pairs={{0,1},{1,2},{2,3},{3,0},{4,5},{5,6},{6,7},{7,4},{8,11},{9,8},{10,9... | collective-permute-start | bytes 1585160 | tf_op jit(solution)/shard_map/ppermute | solution.py:47
  21.9 29.4 %collective-permute-start.2 = (bf16[2064,128]{1,0:T(8,128)(2,1)}, bf16[2064,128]{1,0:T(8,128)(2,1)}, u32[]{:S(2)}, u32[]{:S(2)}) collective-permute-start(bf16[2064,128]{1,0:T(8,128)(2,1)} %get-tuple-element.26.rest_0_), channel_id=1, source_target_pairs={{0,3},{1,0},{2,1},{3,2},{4,7},{5,4},{6,5},{7,6},{8,9},{9,10},{10,1... | collective-permute-start | bytes 1585160 | tf_op jit(solution)/shard_map/ppermute | solution.py:47
  23.1 30.8 %collective-permute-start.3 = (bf16[2064,128]{1,0:T(8,128)(2,1)}, bf16[2064,128]{1,0:T(8,128)(2,1)}, u32[]{:S(2)}, u32[]{:S(2)}) collective-permute-start(bf16[2064,128]{1,0:T(8,128)(2,1)} %get-tuple-element.27.rest_0_), channel_id=1, source_target_pairs={{0,3},{1,0},{2,1},{3,2},{4,7},{5,4},{6,5},{7,6},{8,9},{9,10},{10,1... | collective-permute-start | bytes 1585160 | tf_op jit(solution)/shard_map/ppermute | solution.py:47
  53.9 50.7 %copy-start.2 = (bf16[2064,128]{1,0:T(8,128)(2,1)S(1)}, bf16[2064,128]{1,0:T(8,128)(2,1)}, u32[]{:S(2)}) copy-start(bf16[2064,128]{1,0:T(8,128)(2,1)} %get-tuple-element.27.rest_0_) | copy-start | bytes 1585156
  53.9 8.7 %collective-permute-start.5 = (bf16[2064,128]{1,0:T(8,128)(2,1)}, bf16[2064,128]{1,0:T(8,128)(2,1)S(1)}, u32[]{:S(2)}, u32[]{:S(2)}) collective-permute-start(bf16[2064,128]{1,0:T(8,128)(2,1)} %collective-permute-done.rest_1_), channel_id=1, source_target_pairs={{0,4},{1,5},{2,6},{3,7},{4,16},{5,17},{6,18},{7,19},{8,28},{9,29},... | collective-permute-start | bytes 1585160 | tf_op jit(solution)/shard_map/ppermute | solution.py:47
  55.9 8.6 %collective-permute-start.6 = (bf16[2064,128]{1,0:T(8,128)(2,1)}, bf16[2064,128]{1,0:T(8,128)(2,1)S(1)}, u32[]{:S(2)}, u32[]{:S(2)}) collective-permute-start(bf16[2064,128]{1,0:T(8,128)(2,1)} %collective-permute-done.rest_1_), channel_id=1, source_target_pairs={{0,1},{1,2},{2,3},{3,0},{4,5},{5,6},{6,7},{7,4},{8,11},{9,8},{10,9... | collective-permute-start | bytes 1585160 | tf_op jit(solution)/shard_map/ppermute | solution.py:47
  64.4 8.6 %collective-permute-start.7 = (bf16[2064,128]{1,0:T(8,128)(2,1)}, bf16[2064,128]{1,0:T(8,128)(2,1)S(1)}, u32[]{:S(2)}, u32[]{:S(2)}) collective-permute-start(bf16[2064,128]{1,0:T(8,128)(2,1)} %collective-permute-done.2.rest_3_), channel_id=1, source_target_pairs={{0,4},{1,5},{2,6},{3,7},{4,16},{5,17},{6,18},{7,19},{8,28},{9,29},... | collective-permute-start | bytes 1585160 | tf_op jit(solution)/shard_map/ppermute | solution.py:47
  65.7 10.7 %collective-permute-start.8 = (bf16[2064,128]{1,0:T(8,128)(2,1)S(1)}, bf16[2064,128]{1,0:T(8,128)(2,1)S(1)}, u32[]{:S(2)}, u32[]{:S(2)}) collective-permute-start(bf16[2064,128]{1,0:T(8,128)(2,1)S(1)} %collective-permute-done.5.rest_9_), channel_id=1, source_target_pairs={{0,1},{1,2},{2,3},{3,0},{4,5},{5,6},{6,7},{7,4},{8,11},{9,8},{10,9... | collective-permute-start | bytes 1585160 | tf_op jit(solution)/shard_map/ppermute | solution.py:47
  66.8 10.6 %collective-permute-start.12 = (bf16[2064,128]{1,0:T(8,128)(2,1)}, bf16[2064,128]{1,0:T(8,128)(2,1)S(1)}, u32[]{:S(2)}, u32[]{:S(2)}) collective-permute-start(bf16[2064,128]{1,0:T(8,128)(2,1)} %collective-permute-done.rest_1_), channel_id=1, source_target_pairs={{0,8},{1,9},{2,10},{3,11},{4,12},{5,13},{6,14},{7,15},{8,0},{9,1},... | collective-permute-start | bytes 1585160 | tf_op jit(solution)/shard_map/ppermute | solution.py:47
  67.0 13.6 %collective-permute-start.14 = (bf16[4128,128]{1,0:T(8,128)(2,1)S(1)}, bf16[4128,128]{1,0:T(8,128)(2,1)S(1)}, u32[]{:S(2)}, u32[]{:S(2)}) collective-permute-start(bf16[4128,128]{1,0:T(8,128)(2,1)S(1)} %collective-permute-done.4.rest_7_), channel_id=1, source_target_pairs={{0,8},{1,9},{2,10},{3,11},{4,12},{5,13},{6,14},{7,15},{8,0},{9,1},... | collective-permute-start | bytes 3170312 | tf_op jit(solution)/shard_map/ppermute | solution.py:47
  67.3 10.1 %collective-permute-start.11 = (bf16[2064,128]{1,0:T(8,128)(2,1)}, bf16[2064,128]{1,0:T(8,128)(2,1)S(1)}, u32[]{:S(2)}, u32[]{:S(2)}) collective-permute-start(bf16[2064,128]{1,0:T(8,128)(2,1)} %collective-permute-done.2.rest_3_), channel_id=1, source_target_pairs={{0,8},{1,9},{2,10},{3,11},{4,12},{5,13},{6,14},{7,15},{8,0},{9,1},... | collective-permute-start | bytes 1585160 | tf_op jit(solution)/shard_map/ppermute | solution.py:47
  73.0 4.9 %collective-permute-start.13 = (bf16[2064,128]{1,0:T(8,128)(2,1)S(1)}, bf16[2064,128]{1,0:T(8,128)(2,1)S(1)}, u32[]{:S(2)}, u32[]{:S(2)}) collective-permute-start(bf16[2064,128]{1,0:T(8,128)(2,1)S(1)} %collective-permute-done.6.rest_5_), channel_id=1, source_target_pairs={{0,8},{1,9},{2,10},{3,11},{4,12},{5,13},{6,14},{7,15},{8,0},{9,1},... | collective-permute-start | bytes 1585160 | tf_op jit(solution)/shard_map/ppermute | solution.py:47
  76.3 2.7 %collective-permute-start.16 = (bf16[2064,128]{1,0:T(8,128)(2,1)S(1)}, bf16[2064,128]{1,0:T(8,128)(2,1)S(1)}, u32[]{:S(2)}, u32[]{:S(2)}) collective-permute-start(bf16[2064,128]{1,0:T(8,128)(2,1)S(1)} %collective-permute-done.5.rest_9_), channel_id=1, source_target_pairs={{0,8},{1,9},{2,10},{3,11},{4,12},{5,13},{6,14},{7,15},{8,0},{9,1},... | collective-permute-start | bytes 1585160 | tf_op jit(solution)/shard_map/ppermute | solution.py:47
  77.4 3.2 %collective-permute-start.15 = (bf16[2064,128]{1,0:T(8,128)(2,1)S(1)}, bf16[2064,128]{1,0:T(8,128)(2,1)S(1)}, u32[]{:S(2)}, u32[]{:S(2)}) collective-permute-start(bf16[2064,128]{1,0:T(8,128)(2,1)S(1)} %collective-permute-done.7.rest_11_), channel_id=1, source_target_pairs={{0,8},{1,9},{2,10},{3,11},{4,12},{5,13},{6,14},{7,15},{8,0},{9,1},... | collective-permute-start | bytes 1585160 | tf_op jit(solution)/shard_map/ppermute | solution.py:47
  77.4 3.2 %collective-permute-start.17 = (bf16[2064,128]{1,0:T(8,128)(2,1)S(1)}, bf16[2064,128]{1,0:T(8,128)(2,1)S(1)}, u32[]{:S(2)}, u32[]{:S(2)}) collective-permute-start(bf16[2064,128]{1,0:T(8,128)(2,1)S(1)} %collective-permute-done.8.rest_13_), channel_id=1, source_target_pairs={{0,8},{1,9},{2,10},{3,11},{4,12},{5,13},{6,14},{7,15},{8,0},{9,1},... | collective-permute-start | bytes 1585160 | tf_op jit(solution)/shard_map/ppermute | solution.py:47
  77.9 13.0 %collective-permute-start.10 = (bf16[2064,128]{1,0:T(8,128)(2,1)}, bf16[2064,128]{1,0:T(8,128)(2,1)S(1)}, u32[]{:S(2)}, u32[]{:S(2)}) collective-permute-start(bf16[2064,128]{1,0:T(8,128)(2,1)} %collective-permute-done.1.rest_1_), channel_id=1, source_target_pairs={{0,1},{1,2},{2,3},{3,0},{4,5},{5,6},{6,7},{7,4},{8,11},{9,8},{10,9... | collective-permute-start | bytes 1585160 | tf_op jit(solution)/shard_map/ppermute | solution.py:47
  79.0 12.0 %collective-permute-start.9 = (bf16[2064,128]{1,0:T(8,128)(2,1)}, bf16[2064,128]{1,0:T(8,128)(2,1)S(1)}, u32[]{:S(2)}, u32[]{:S(2)}) collective-permute-start(bf16[2064,128]{1,0:T(8,128)(2,1)} %collective-permute-done.1.rest_1_), channel_id=1, source_target_pairs={{0,4},{1,5},{2,6},{3,7},{4,16},{5,17},{6,18},{7,19},{8,28},{9,29},... | collective-permute-start | bytes 1585160 | tf_op jit(solution)/shard_map/ppermute | solution.py:47
  80.6 14.6 %collective-permute-start.19 = (bf16[2064,128]{1,0:T(8,128)(2,1)}, bf16[2064,128]{1,0:T(8,128)(2,1)S(1)}, u32[]{:S(2)}, u32[]{:S(2)}) collective-permute-start(bf16[2064,128]{1,0:T(8,128)(2,1)} %collective-permute-done.1.rest_1_), channel_id=1, source_target_pairs={{0,8},{1,9},{2,10},{3,11},{4,12},{5,13},{6,14},{7,15},{8,0},{9,1},... | collective-permute-start | bytes 1585160 | tf_op jit(solution)/shard_map/ppermute | solution.py:47
  80.7 1.0 copy-start.3
  90.9 8.8 %collective-permute-start.21 = (bf16[2064,128]{1,0:T(8,128)(2,1)}, bf16[2064,128]{1,0:T(8,128)(2,1)S(1)}, u32[]{:S(2)}, u32[]{:S(2)}) collective-permute-start(bf16[2064,128]{1,0:T(8,128)(2,1)} %collective-permute-done.3.rest_3_), channel_id=1, source_target_pairs={{0,4},{1,5},{2,6},{3,7},{4,16},{5,17},{6,18},{7,19},{8,28},{9,29},... | collective-permute-start | bytes 1585160 | tf_op jit(solution)/shard_map/ppermute | solution.py:47
  92.9 9.5 %collective-permute-start.24 = (bf16[2064,128]{1,0:T(8,128)(2,1)S(1)}, bf16[2064,128]{1,0:T(8,128)(2,1)S(1)}, u32[]{:S(2)}, u32[]{:S(2)}) collective-permute-start(bf16[2064,128]{1,0:T(8,128)(2,1)S(1)} %collective-permute-done.9.rest_9_), channel_id=1, source_target_pairs={{0,1},{1,2},{2,3},{3,0},{4,5},{5,6},{6,7},{7,4},{8,11},{9,8},{10,9... | collective-permute-start | bytes 1585160 | tf_op jit(solution)/shard_map/ppermute | solution.py:47
  94.7 8.3 %collective-permute-start.18 = (bf16[2064,128]{1,0:T(8,128)(2,1)}, bf16[2064,128]{1,0:T(8,128)(2,1)S(1)}, u32[]{:S(2)}, u32[]{:S(2)}) collective-permute-start(bf16[2064,128]{1,0:T(8,128)(2,1)} %collective-permute-done.3.rest_3_), channel_id=1, source_target_pairs={{0,8},{1,9},{2,10},{3,11},{4,12},{5,13},{6,14},{7,15},{8,0},{9,1},... | collective-permute-start | bytes 1585160 | tf_op jit(solution)/shard_map/ppermute | solution.py:47
  94.7 8.3 %collective-permute-start.23 = (bf16[2064,128]{1,0:T(8,128)(2,1)S(1)}, bf16[2064,128]{1,0:T(8,128)(2,1)S(1)}, u32[]{:S(2)}, u32[]{:S(2)}) collective-permute-start(bf16[2064,128]{1,0:T(8,128)(2,1)S(1)} %collective-permute-done.9.rest_9_), channel_id=1, source_target_pairs={{0,8},{1,9},{2,10},{3,11},{4,12},{5,13},{6,14},{7,15},{8,0},{9,1},... | collective-permute-start | bytes 1585160 | tf_op jit(solution)/shard_map/ppermute | solution.py:47
  95.2 7.8 %collective-permute-start.20 = (bf16[2064,128]{1,0:T(8,128)(2,1)S(1)}, bf16[2064,128]{1,0:T(8,128)(2,1)S(1)}, u32[]{:S(2)}, u32[]{:S(2)}) collective-permute-start(bf16[2064,128]{1,0:T(8,128)(2,1)S(1)} %collective-permute-done.10.rest_5_), channel_id=1, source_target_pairs={{0,8},{1,9},{2,10},{3,11},{4,12},{5,13},{6,14},{7,15},{8,0},{9,1},... | collective-permute-start | bytes 1585160 | tf_op jit(solution)/shard_map/ppermute | solution.py:47
  99.8 4.1 %collective-permute-start.22 = (bf16[2064,128]{1,0:T(8,128)(2,1)S(1)}, bf16[2064,128]{1,0:T(8,128)(2,1)S(1)}, u32[]{:S(2)}, u32[]{:S(2)}) collective-permute-start(bf16[2064,128]{1,0:T(8,128)(2,1)S(1)} %collective-permute-done.21.rest_11_), channel_id=1, source_target_pairs={{0,8},{1,9},{2,10},{3,11},{4,12},{5,13},{6,14},{7,15},{8,0},{9,1},... | collective-permute-start | bytes 1585160 | tf_op jit(solution)/shard_map/ppermute | solution.py:47
  102.3 2.3 %collective-permute-start.25 = (bf16[2064,128]{1,0:T(8,128)(2,1)S(1)}, bf16[2064,128]{1,0:T(8,128)(2,1)S(1)}, u32[]{:S(2)}, u32[]{:S(2)}) collective-permute-start(bf16[2064,128]{1,0:T(8,128)(2,1)S(1)} %collective-permute-done.24.rest_13_), channel_id=1, source_target_pairs={{0,8},{1,9},{2,10},{3,11},{4,12},{5,13},{6,14},{7,15},{8,0},{9,1},... | collective-permute-start | bytes 1585160 | tf_op jit(solution)/shard_map/ppermute | solution.py:47

commit v5 on v3

--- a/solution.py
+++ b/solution.py
@@ -37,10 +37,19 @@
     return [(i, linear(*step(*coords(i)))) for i in range(128)]
 
 
-Z_AWAY = route(lambda x, y, z, c: (x, y, z + 1 - 2 * c, c))
-Z_BACK = route(lambda x, y, z, c: (x, y, z - 1 + 2 * c, c))
+Z_SIDE = route(lambda x, y, z, c: (x, y, z + 1 - 2 * (c ^ x & 1), c))
 Y_SIDE = route(lambda x, y, z, c: (x, y + 1 - 2 * c, z, c))
+X_SIDE = route(lambda x, y, z, c: (x + 1 - 2 * c, y, z, c))
 SWAP = route(lambda x, y, z, c: (x, y, z, 1 - c))
+
+
+def place():
+    seq, filt = lax.axis_index("seq"), lax.axis_index("filt")
+    core, parity = seq & 1, (seq >> 2) & 1
+    z, yl = filt & 3, filt >> 2
+    side = 2 * (core ^ parity) - 1
+    zs = [z, (z + side) & 3, (z - side) & 3, (z + 2) & 3]
+    return core, [yl * 4 + v for v in zs] + [(1 - yl) * 4 + v for v in zs]
 
 
 def send(block, path):
@@ -54,28 +63,42 @@
     return [hi, mid, lo]
 
 
-def prepare_kernel(where_ref, tokens_ref, conv_ref, mix_ref, conv_bias_ref, mix_bias_ref, padded_ref, own_ref, sems):
+def prepare_kernel(tokens_ref, conv_ref, mix_ref, conv_bias_ref, mix_bias_ref, padded_ref, own_ref, bias_ref, tokens, own, sems, out_sems):
     length = tokens_ref.shape[0]
-    rows = pl.ds(pl.multiple_of(where_ref[0] * HALF, HALF), HALF)
-    moves = []
+    core, _ = place()
+    rows = pl.ds(pl.multiple_of(core * HALF, HALF), HALF)
+    arriving, leaving = [], []
     for layer in range(LAYERS):
         for t in range(4):
             source = conv_ref.at[layer, t, rows] if t < 3 else mix_ref.at[layer, rows]
-            moves.append((source, own_ref.at[pl.ds(layer * PART + t * HALF, HALF)]))
-    moves.append((tokens_ref, padded_ref.at[pl.ds(0, length)]))
-    copies = [pltpu.make_async_copy(a, b, sems.at[i]) for i, (a, b) in enumerate(moves)]
-    for copy in copies:
+            spot = pl.ds(layer * PART + t * HALF, HALF)
+            arriving.append((source, own.at[spot]))
+            leaving.append((own.at[spot], own_ref.at[spot]))
+    arriving.append((tokens_ref, tokens.at[pl.ds(0, length)]))
+    leaving.append((tokens, padded_ref))
+    arriving = [pltpu.make_async_copy(a, b, sems.at[i]) for i, (a, b) in enumerate(arriving)]
+    for copy in arriving:
         copy.start()
-    padded_ref[length:, :] = jnp.zeros((128 * RES - length, LANES), jnp.bfloat16)
+    tokens[length:, :] = jnp.zeros((128 * RES - length, LANES), jnp.bfloat16)
     for layer in range(LAYERS):
         lines = three_parts(conv_bias_ref[layer:layer + 1, :]) + three_parts(mix_bias_ref[layer:layer + 1, :])
         lines.append(jnp.zeros((EXTRA - 6, LANES), jnp.float32))
-        own_ref[layer * PART + 4 * HALF:(layer + 1) * PART, :] = jnp.concatenate(lines, axis=0).astype(jnp.bfloat16)
-    for copy in copies:
+        block = jnp.concatenate(lines, axis=0).astype(jnp.bfloat16)
+        spot = slice(layer * PART + 4 * HALF, (layer + 1) * PART)
+        own[spot, :] = block
+        bias_ref[layer] = block
+        leaving.append((own.at[spot], own_ref.at[spot]))
+    leaving = [pltpu.make_async_copy(a, b, out_sems.at[i]) for i, (a, b) in enumerate(leaving)]
+    for copy in leaving[len(arriving):]:
+        copy.start()
+    for coming, going in zip(arriving, leaving):
+        coming.wait()
+        going.start()
+    for copy in leaving:
         copy.wait()
 
 
-def prepare(where, tokens, conv, mix, conv_bias, mix_bias):
+def prepare(tokens, conv, mix, conv_bias, mix_bias):
     anywhere = pl.BlockSpec(memory_space=pl.ANY)
     vmem = pl.BlockSpec(memory_space=pltpu.VMEM)
     return pl.pallas_call(
@@ -83,26 +106,34 @@
         out_shape=[
             jax.ShapeDtypeStruct((128 * RES, LANES), jnp.bfloat16),
             jax.ShapeDtypeStruct((LAYERS * PART, LANES), jnp.bfloat16),
+            jax.ShapeDtypeStruct((LAYERS, EXTRA, LANES), jnp.bfloat16),
         ],
-        in_specs=[pl.BlockSpec(memory_space=pltpu.SMEM), anywhere, anywhere, anywhere, vmem, vmem],
-        out_specs=[vmem, vmem],
-        scratch_shapes=[pltpu.SemaphoreType.DMA((1 + 4 * LAYERS,))],
+        in_specs=[anywhere, anywhere, anywhere, vmem, vmem],
+        out_specs=[anywhere, anywhere, vmem],
+        scratch_shapes=[
+            pltpu.VMEM((128 * RES, LANES), jnp.bfloat16),
+            pltpu.VMEM((LAYERS * PART, LANES), jnp.bfloat16),
+            pltpu.SemaphoreType.DMA((1 + 4 * LAYERS,)),
+            pltpu.SemaphoreType.DMA((1 + 5 * LAYERS,)),
+        ],
         compiler_params=pltpu.CompilerParams(vmem_limit_bytes=60 * 2**20),
         cost_estimate=pl.CostEstimate(flops=0, bytes_accessed=4 * 2**20, transcendentals=0),
         name="prepare",
-    )(where, tokens, conv, mix, conv_bias, mix_bias)
-
-
-def blocks_kernel(where_ref, x_ref, gain_ref, conv_ref, mix_ref, own_ref, *rest):
+    )(tokens, conv, mix, conv_bias, mix_bias)
+
+
+def blocks_kernel(x_ref, gain_ref, bias_ref, conv_ref, mix_ref, *rest):
     parts = rest[:2 * (SHARDS - 1)]
-    out_ref, w, mine, bias, x, normed, n, act, mixing, sems, mine_sems, bias_sems = rest[2 * (SHARDS - 1):]
+    out_ref, w, mine, x, normed, n, act, mixing, sems, mine_sems = rest[2 * (SHARDS - 1):]
+    core, homes = place()
+    halves = (core, 1 - core)
     width = 2 * LANES
 
     def half(i):
-        return pl.ds(pl.multiple_of(where_ref[i] * HALF, HALF), HALF)
+        return pl.ds(pl.multiple_of(halves[i] * HALF, HALF), HALF)
 
     def home(k):
-        return pl.ds(pl.multiple_of(where_ref[2 + k] * LANES, LANES), LANES)
+        return pl.ds(pl.multiple_of(homes[k] * LANES, LANES), LANES)
 
     arriving = []
     for layer in range(LAYERS):
@@ -112,7 +143,6 @@
                 moves = [
                     (conv_ref.at[layer], mine.at[layer, pl.ds(0, 3)], mine_sems.at[layer, 0]),
                     (mix_ref.at[layer], mine.at[layer, 3], mine_sems.at[layer, 1]),
-                    (own_ref.at[pl.ds(layer * PART + 4 * HALF, EXTRA)], bias.at[layer], bias_sems.at[layer]),
                 ]
             else:
                 moves = []
@@ -154,7 +184,7 @@
             return jnp.concatenate([w[2 * (k - 1) + i, base + 3 * HALF:base + 4 * HALF, :] for i in range(2)], axis=0)
 
         def bias_row(k, start):
-            rows = bias[layer] if k == 0 else w[2 * (k - 1), base + 4 * HALF:base + PART, :]
+            rows = bias_ref[layer] if k == 0 else w[2 * (k - 1), base + 4 * HALF:base + PART, :]
             rows = rows.astype(jnp.float32)
             return rows[start:start + 1] + rows[start + 1:start + 2] + rows[start + 2:start + 3]
 
@@ -180,25 +210,24 @@
             for h, k in enumerate(pair):
                 total = x[:, home(k)] + mixed[:, h * LANES:(h + 1) * LANES]
                 if layer == LAYERS - 1:
-                    f = where_ref[2 + k]
+                    f = homes[k]
                     for b in range(BLOCKS):
                         out_ref[b * SHARDS + f] = total[b * RES:(b + 1) * RES].astype(jnp.bfloat16)
                 else:
                     x[:, home(k)] = total.astype(jnp.bfloat16).astype(jnp.float32)
 
 
-def run_blocks(where, x, gain, conv, mix, own, parts):
+def run_blocks(x, gain, bias, conv, mix, parts):
     vmem = pl.BlockSpec(memory_space=pltpu.VMEM)
     anywhere = pl.BlockSpec(memory_space=pl.ANY)
     return pl.pallas_call(
         blocks_kernel,
         out_shape=jax.ShapeDtypeStruct((BLOCKS * SHARDS, RES, LANES), jnp.bfloat16),
-        in_specs=[pl.BlockSpec(memory_space=pltpu.SMEM), vmem, vmem] + [anywhere] * (3 + len(parts)),
+        in_specs=[vmem, vmem, vmem] + [anywhere] * (2 + len(parts)),
         out_specs=vmem,
         scratch_shapes=[
             pltpu.VMEM((len(parts), LAYERS * PART, LANES), jnp.bfloat16),
             pltpu.VMEM((LAYERS, 4, C, LANES), jnp.bfloat16),
-            pltpu.VMEM((LAYERS, EXTRA, LANES), jnp.bfloat16),
             pltpu.VMEM((ROWS, C), jnp.float32),
             pltpu.VMEM((ROWS, C), jnp.float32),
             pltpu.VMEM((ROWS, 3 * C), jnp.bfloat16),
@@ -206,38 +235,30 @@
             pltpu.VMEM((ROWS, C), jnp.bfloat16),
             pltpu.SemaphoreType.DMA((LAYERS, len(parts))),
             pltpu.SemaphoreType.DMA((LAYERS, 2)),
-            pltpu.SemaphoreType.DMA((LAYERS,)),
         ],
         compiler_params=pltpu.CompilerParams(vmem_limit_bytes=32 * 2**20),
         cost_estimate=pl.CostEstimate(flops=16 * ROWS * C * C, bytes_accessed=18 * 2**20, transcendentals=2 * ROWS * C),
         name="blocks",
-    )(where, x, gain, conv, mix, own, *parts)
+    )(x, gain, bias, conv, mix, *parts)
 
 
 def per_device(tokens, conv_weight, conv_bias, mix_weight, mix_bias, norm_gain):
-    seq, filt = lax.axis_index("seq"), lax.axis_index("filt")
-    core = seq & 1
-    z, yl = filt & 3, filt >> 2
-    zs = [z, (z - 1 + 2 * core) & 3, (z + 1 - 2 * core) & 3, (z + 2) & 3]
-    shards = [yl * 4 + v for v in zs] + [(1 - yl) * 4 + v for v in zs]
-    where = jnp.stack([core, 1 - core] + shards).astype(jnp.int32)
-
-    padded, own = prepare(where, tokens, conv_weight, mix_weight, conv_bias, mix_bias)
-    near, far = send(own, Z_AWAY), send(own, Z_BACK)
-    cross = send(own, Y_SIDE)
+    padded, own, bias = prepare(tokens, conv_weight, mix_weight, conv_bias, mix_bias)
+    a = send(own, Z_SIDE)
+    own_y = send(own, Y_SIDE)
     x = lax.all_to_all(padded.reshape(128, RES, LANES), AXES, split_axis=0, concat_axis=0, tiled=True)
-    near, far, cross, x = lax.optimization_barrier((near, far, cross, x))
-    beyond = send(near, Z_AWAY)
-    cross_near = send(near, Y_SIDE)
-    far, cross_near = lax.optimization_barrier((far, cross_near))
-    cross_far = send(far, Y_SIDE)
-    cross_beyond = send(cross_near, Z_AWAY)
-    mine = [near, far, beyond, cross, cross_near, cross_far, cross_beyond]
+    b = send(a, X_SIDE)
+    e = send(a, Z_SIDE)
+    a_y = send(a, Y_SIDE)
+    a_y, e, b, x = lax.optimization_barrier((a_y, e, b, x))
+    b_y = send(a_y, X_SIDE)
+    e_y = send(e, Y_SIDE)
+    mine = [a, b, e, own_y, a_y, b_y, e_y]
     swapped = [send(v, SWAP) for v in mine]
     parts = []
     for k, i in enumerate([1, 0, 2, 3, 5, 4, 6]):
         parts += [mine[k], swapped[i]]
-    x = run_blocks(where, x, norm_gain, conv_weight, mix_weight, own, parts)
+    x = run_blocks(x, norm_gain, bias, conv_weight, mix_weight, parts)
     y = lax.all_to_all(x, AXES, split_axis=0, concat_axis=0, tiled=True)
     return y.reshape(128 * RES, LANES)[:tokens.shape[0]]
 

time: 123 us -> 112 us (0.911)
  blocking collectives: 55.4 us -> 21 us
  waiting for transfers between devices: 25.6 us -> 42.8 us
  starting transfers between devices: 18.5 us -> 27 us
    all_to_all x1 -> x0, blocking collectives: 33.4 us -> none  [per_device(): lax.all_to_all(padded.reshape(128, RES, LANES), AXES, split_axis=0, conca...]
    all_to_all x0 -> x1, waiting for transfers between devices: none -> 16.5 us  [per_device(): lax.all_to_all(padded.reshape(128, RES, LANES), AXES, split_axis=0, conca...]
    all_to_all x0 -> x1, starting transfers between devices: none -> 7.7 us  [per_device(): lax.all_to_all(padded.reshape(128, RES, LANES), AXES, split_axis=0, conca...]
  transfers between devices with their start and end apart: 14 -> 15, of which waited for: 4 -> 5; matrix products, arithmetic and copies ran while one was open for 0% -> 0% of each run, Pallas kernels for 0% -> 0%
where the time goes in v5:
time: 112 us
  waiting for transfers between devices  42.8 us (38%)
  starting transfers between devices  27 us (24%)
  blocking collectives  21 us (19%)
  Pallas kernels  19.5 us (17%)
  local copies, waits for them, and re-layouts  1.62 us (1%)
    ppermute x14, waiting for transfers between devices, send(): return lax.ppermute(block, AXES, path)  26.4 us
    all_to_all x1, blocking collectives, per_device(): y = lax.all_to_all(x, AXES, split_axis=0, concat_axis=0, tiled=True)  21 us
    ppermute x14, starting transfers between devices, send(): return lax.ppermute(block, AXES, path)  19.3 us
    all_to_all x1, waiting for transfers between devices, per_device(): lax.all_to_all(padded.reshape(128, RES, LANES), AXES, split_axis=0, conca...  16.5 us
    pallas_call x1, Pallas kernels, run_blocks(): pl.pallas_call(blocks_kernel, out_shape=jax.ShapeDtypeStruct((BLOCKS * SH...  15.5 us
    all_to_all x1, starting transfers between devices, per_device(): lax.all_to_all(padded.reshape(128, RES, LANES), AXES, split_axis=0, conca...  7.7 us
    pallas_call x1, Pallas kernels, prepare(): pl.pallas_call(prepare_kernel, out_shape=[jax.ShapeDtypeStruct((128 * RES...  3.96 us
  transfers between devices with their start and end apart: 15, of which 5 were waited for; matrix products, arithmetic and copies ran while one was open for 0% of the time, Pallas kernels for 0%

profile of v5, /device:TPU:1, one launch (start us, length us, event | category | flops | bytes accessed | tf_op | source)
XLA Modules:
  0.0 112.0 jit_solution(15720108956192569303)
XLA Ops:
  0.0 0.0 copy-start.1
  0.0 0.0 copy-start.2
  0.0 4.0 %prepare.1 = (bf16[3072,128]{1,0:T(8,128)(2,1)}, bf16[4128,128]{1,0:T(8,128)(2,1)}, bf16[2,16,128]{2,1,0:T(8,128)(2,1)}) custom-call(bf16[2688,128]{1,0:T(8,128)(2,1)} %tokens_ref.1, bf16[2,3,1024,128]{3,2,1,0:T(8,128)(2,1)} %conv_ref.3, bf16[2,1024,128]{2,1,0:T(8,128)(2,1)} %mix_ref.3, f32[2,128]{1,0:T(2,128)} %conv_bias_ref.1, f32[2,128]{1,0:T(2,128)} %mix_bias_ref.1), custom_call_target="tpu_custom_call" | custom-call | bytes 4194304 | tf_op jit(solution)/shard_map/prepare/pallas_call | solution.py:104
  4.0 0.0 copy-start
  4.0 4.7 %collective-permute-start = (bf16[4128,128]{1,0:T(8,128)(2,1)}, bf16[4128,128]{1,0:T(8,128)(2,1)}, u32[]{:S(2)}, u32[]{:S(2)}) collective-permute-start(bf16[4128,128]{1,0:T(8,128)(2,1)} %get-tuple-element.12), channel_id=1, source_target_pairs={{0,1},{1,2},{2,3},{3,0},{4,5},{5,6},{6,7},{7,4},{8,11},{9,8},{10,9... | collective-permute-start | bytes 3170312 | tf_op jit(solution)/shard_map/ppermute | solution.py:56
  8.6 2.7 %collective-permute-start.7 = (bf16[4128,128]{1,0:T(8,128)(2,1)}, bf16[4128,128]{1,0:T(8,128)(2,1)}, u32[]{:S(2)}, u32[]{:S(2)}) collective-permute-start(bf16[4128,128]{1,0:T(8,128)(2,1)} %get-tuple-element.12), channel_id=1, source_target_pairs={{0,4},{1,5},{2,6},{3,7},{4,16},{5,17},{6,18},{7,19},{8,28},{9,29},... | collective-permute-start | bytes 3170312 | tf_op jit(solution)/shard_map/ppermute | solution.py:56
  11.4 9.4 %collective-permute-done.rest_0_ = bf16[4128,128]{1,0:T(8,128)(2,1)} collective-permute-done((bf16[4128,128]{1,0:T(8,128)(2,1)}, bf16[4128,128]{1,0:T(8,128)(2,1)}, u32[]{:S(2)}, u32[]{:S(2)}) %collective-permute-start) | collective-permute-done | bytes 1056800 | tf_op jit(solution)/shard_map/ppermute | solution.py:56
  20.8 3.2 %collective-permute-start.3 = (bf16[4128,128]{1,0:T(8,128)(2,1)}, bf16[4128,128]{1,0:T(8,128)(2,1)}, u32[]{:S(2)}, u32[]{:S(2)}) collective-permute-start(bf16[4128,128]{1,0:T(8,128)(2,1)} %collective-permute-done.rest_0_), channel_id=1, source_target_pairs={{0,32},{1,33},{2,34},{3,35},{4,36},{5,37},{6,38},{7,39},{8,104},{9... | collective-permute-start | bytes 3170312 | tf_op jit(solution)/shard_map/ppermute | solution.py:56
  24.0 1.5 %collective-permute-start.2 = (bf16[4128,128]{1,0:T(8,128)(2,1)}, bf16[4128,128]{1,0:T(8,128)(2,1)}, u32[]{:S(2)}, u32[]{:S(2)}) collective-permute-start(bf16[4128,128]{1,0:T(8,128)(2,1)} %collective-permute-done.rest_0_), channel_id=1, source_target_pairs={{0,1},{1,2},{2,3},{3,0},{4,5},{5,6},{6,7},{7,4},{8,11},{9,8},{10,9... | collective-permute-start | bytes 3170312 | tf_op jit(solution)/shard_map/ppermute | solution.py:56
  25.5 2.7 %collective-permute-start.1 = (bf16[4128,128]{1,0:T(8,128)(2,1)}, bf16[4128,128]{1,0:T(8,128)(2,1)}, u32[]{:S(2)}, u32[]{:S(2)}) collective-permute-start(bf16[4128,128]{1,0:T(8,128)(2,1)} %collective-permute-done.rest_0_), channel_id=1, source_target_pairs={{0,4},{1,5},{2,6},{3,7},{4,16},{5,17},{6,18},{7,19},{8,28},{9,29},... | collective-permute-start | bytes 3170312 | tf_op jit(solution)/shard_map/ppermute | solution.py:56
  28.2 7.7 %all-to-all-start = ((bf16[128,24,128]{2,1,0:T(8,128)(2,1)}), bf16[128,24,128]{2,1,0:T(8,128)(2,1)S(1)}, u32[]{:S(2)}, u32[]{:S(2)}) async-start(bf16[128,24,128]{2,1,0:T(8,128)(2,1)} %bitcast.2), calls=%async_computation | async-start | bytes 1572864 | tf_op jit(solution)/shard_map/all_to_all | solution.py:249
  35.9 1.1 %collective-permute-start.5 = (bf16[4128,128]{1,0:T(8,128)(2,1)}, bf16[4128,128]{1,0:T(8,128)(2,1)}, u32[]{:S(2)}, u32[]{:S(2)}) collective-permute-start(bf16[4128,128]{1,0:T(8,128)(2,1)} %collective-permute-done.rest_0_), channel_id=1, source_target_pairs={{0,8},{1,9},{2,10},{3,11},{4,12},{5,13},{6,14},{7,15},{8,0},{9,1},... | collective-permute-start | bytes 3170312 | tf_op jit(solution)/shard_map/ppermute | solution.py:56
  37.1 0.0 collective-permute-done.7.rest_6_
  37.1 0.1 collective-permute-start.8
  37.2 16.5 %all-to-all-done.x_ref = bf16[128,24,128]{2,1,0:T(8,128)(2,1)S(1)} async-done(((bf16[128,24,128]{2,1,0:T(8,128)(2,1)}), bf16[128,24,128]{2,1,0:T(8,128)(2,1)S(1)}, u32[]{:S(2)}, u32[]{:S(2)}) %all-to-all-start) | async-done | bytes 786464 | tf_op jit(solution)/shard_map/all_to_all | solution.py:249
  53.6 0.0 collective-permute-done.3.rest_2_
  53.6 0.0 collective-permute-done.2.rest_4_
  53.6 0.0 collective-permute-done.1.rest_8_
  53.6 0.1 collective-permute-start.12
  53.7 0.4 collective-permute-start.9
  54.1 0.0 collective-permute-start.6
  54.1 0.0 collective-permute-done.8.rest_7_
  54.1 0.5 collective-permute-start.11
  54.6 0.0 collective-permute-done.5.rest_3_
  54.6 0.1 collective-permute-start.4
  54.7 13.2 %collective-permute-done.12.rest_12_ = bf16[4128,128]{1,0:T(8,128)(2,1)S(1)} collective-permute-done((bf16[4128,128]{1,0:T(8,128)(2,1)}, bf16[4128,128]{1,0:T(8,128)(2,1)S(1)}, u32[]{:S(2)}, u32[]{:S(2)}) %collective-permute-start.12) | collective-permute-done | bytes 1056800 | tf_op jit(solution)/shard_map/ppermute | solution.py:56
  67.9 2.1 %collective-permute-start.13 = (bf16[4128,128]{1,0:T(8,128)(2,1)S(1)}, bf16[4128,128]{1,0:T(8,128)(2,1)S(1)}, u32[]{:S(2)}, u32[]{:S(2)}) collective-permute-start(bf16[4128,128]{1,0:T(8,128)(2,1)S(1)} %collective-permute-done.12.rest_12_), channel_id=1, source_target_pairs={{0,8},{1,9},{2,10},{3,11},{4,12},{5,13},{6,14},{7,15},{8,0},{9,1},... | collective-permute-start | bytes 3170312 | tf_op jit(solution)/shard_map/ppermute | solution.py:56
  70.0 0.0 collective-permute-done.9.rest_10_
  70.0 0.1 collective-permute-start.10
  70.1 0.0 collective-permute-done.4.rest_1_
  70.1 0.0 collective-permute-done.6.rest_5_
  70.1 0.0 collective-permute-done.11.rest_11_
  70.1 2.2 %collective-permute-done.13.rest_13_ = bf16[4128,128]{1,0:T(8,128)(2,1)S(1)} collective-permute-done((bf16[4128,128]{1,0:T(8,128)(2,1)S(1)}, bf16[4128,128]{1,0:T(8,128)(2,1)S(1)}, u32[]{:S(2)}, u32[]{:S(2)}) %collective-permute-start.13) | collective-permute-done | bytes 1056800 | tf_op jit(solution)/shard_map/ppermute | solution.py:56
  72.3 1.5 %collective-permute-done.10.rest_9_ = bf16[4128,128]{1,0:T(8,128)(2,1)S(1)} collective-permute-done((bf16[4128,128]{1,0:T(8,128)(2,1)S(1)}, bf16[4128,128]{1,0:T(8,128)(2,1)S(1)}, u32[]{:S(2)}, u32[]{:S(2)}) %collective-permute-start.10) | collective-permute-done | bytes 1056800 | tf_op jit(solution)/shard_map/ppermute | solution.py:56
  73.8 0.0 copy-done.1
  73.9 0.0 copy-done.2
  73.9 0.0 copy-done
  73.9 0.0 copy-start.3
  73.9 0.7 copy-done.3
  74.6 15.5 %blocks.1 = bf16[128,24,128]{2,1,0:T(8,128)(2,1)S(1)} custom-call(bf16[128,24,128]{2,1,0:T(8,128)(2,1)S(1)} %all-to-all-done.x_ref, f32[2,1024]{1,0:T(2,128)S(1)} %copy-done.2, bf16[2,16,128]{2,1,0:T(8,128)(2,1)S(1)} %copy-done.3, bf16[2,3,1024,128]{3,2,1,0:T(8,128)(2,1)S(1)} %copy-done, bf16[2,1024,128]{2,1,0:T(8,128)(2,1)S(1)} %copy-done.1, ...), custom_call_target="tpu_custom_call" | custom-call | flops 6442450944 | bytes 18874368 | tf_op jit(solution)/shard_map/blocks/pallas_call | solution.py:223
  90.1 21.0 %all_to_all.10 = bf16[128,24,128]{2,1,0:T(8,128)(2,1)S(1)} all-to-all(bf16[128,24,128]{2,1,0:T(8,128)(2,1)S(1)} %blocks.1), channel_id=1, replica_groups=mesh['seq'=16,'filt'=8] {'seq','filt'}, dimensions={0} | all-to-all | bytes 1572864 | tf_op jit(solution)/shard_map/all_to_all | solution.py:262
  111.1 0.9 slice.8
Async XLA Ops:
  0.0 73.9 %copy-start.1 = (bf16[2,1024,128]{2,1,0:T(8,128)(2,1)S(1)}, bf16[2,1024,128]{2,1,0:T(8,128)(2,1)}, u32[]{:S(2)}) copy-start(bf16[2,1024,128]{2,1,0:T(8,128)(2,1)} %mix_ref.3) | copy-start | bytes 1572868
  0.0 73.9 %copy-start.2 = (f32[2,1024]{1,0:T(2,128)S(1)}, f32[2,1024]{1,0:T(2,128)}, u32[]{:S(2)}) copy-start(f32[2,1024]{1,0:T(2,128)} %gain_ref.1) | copy-start | bytes 24580
  4.0 69.9 %copy-start = (bf16[2,3,1024,128]{3,2,1,0:T(8,128)(2,1)S(1)}, bf16[2,3,1024,128]{3,2,1,0:T(8,128)(2,1)}, u32[]{:S(2)}) copy-start(bf16[2,3,1024,128]{3,2,1,0:T(8,128)(2,1)} %conv_ref.3) | copy-start | bytes 4718596
  4.0 16.8 %collective-permute-start = (bf16[4128,128]{1,0:T(8,128)(2,1)}, bf16[4128,128]{1,0:T(8,128)(2,1)}, u32[]{:S(2)}, u32[]{:S(2)}) collective-permute-start(bf16[4128,128]{1,0:T(8,128)(2,1)} %get-tuple-element.12), channel_id=1, source_target_pairs={{0,1},{1,2},{2,3},{3,0},{4,5},{5,6},{6,7},{7,4},{8,11},{9,8},{10,9... | collective-permute-start | bytes 3170312 | tf_op jit(solution)/shard_map/ppermute | solution.py:56
  8.6 28.4 %collective-permute-start.7 = (bf16[4128,128]{1,0:T(8,128)(2,1)}, bf16[4128,128]{1,0:T(8,128)(2,1)}, u32[]{:S(2)}, u32[]{:S(2)}) collective-permute-start(bf16[4128,128]{1,0:T(8,128)(2,1)} %get-tuple-element.12), channel_id=1, source_target_pairs={{0,4},{1,5},{2,6},{3,7},{4,16},{5,17},{6,18},{7,19},{8,28},{9,29},... | collective-permute-start | bytes 3170312 | tf_op jit(solution)/shard_map/ppermute | solution.py:56
  20.8 32.8 %collective-permute-start.3 = (bf16[4128,128]{1,0:T(8,128)(2,1)}, bf16[4128,128]{1,0:T(8,128)(2,1)}, u32[]{:S(2)}, u32[]{:S(2)}) collective-permute-start(bf16[4128,128]{1,0:T(8,128)(2,1)} %collective-permute-done.rest_0_), channel_id=1, source_target_pairs={{0,32},{1,33},{2,34},{3,35},{4,36},{5,37},{6,38},{7,39},{8,104},{9... | collective-permute-start | bytes 3170312 | tf_op jit(solution)/shard_map/ppermute | solution.py:56
  24.0 29.6 %collective-permute-start.2 = (bf16[4128,128]{1,0:T(8,128)(2,1)}, bf16[4128,128]{1,0:T(8,128)(2,1)}, u32[]{:S(2)}, u32[]{:S(2)}) collective-permute-start(bf16[4128,128]{1,0:T(8,128)(2,1)} %collective-permute-done.rest_0_), channel_id=1, source_target_pairs={{0,1},{1,2},{2,3},{3,0},{4,5},{5,6},{6,7},{7,4},{8,11},{9,8},{10,9... | collective-permute-start | bytes 3170312 | tf_op jit(solution)/shard_map/ppermute | solution.py:56
  25.5 28.2 %collective-permute-start.1 = (bf16[4128,128]{1,0:T(8,128)(2,1)}, bf16[4128,128]{1,0:T(8,128)(2,1)}, u32[]{:S(2)}, u32[]{:S(2)}) collective-permute-start(bf16[4128,128]{1,0:T(8,128)(2,1)} %collective-permute-done.rest_0_), channel_id=1, source_target_pairs={{0,4},{1,5},{2,6},{3,7},{4,16},{5,17},{6,18},{7,19},{8,28},{9,29},... | collective-permute-start | bytes 3170312 | tf_op jit(solution)/shard_map/ppermute | solution.py:56
  28.2 25.4 %all-to-all-start = ((bf16[128,24,128]{2,1,0:T(8,128)(2,1)}), bf16[128,24,128]{2,1,0:T(8,128)(2,1)S(1)}, u32[]{:S(2)}, u32[]{:S(2)}) async-start(bf16[128,24,128]{2,1,0:T(8,128)(2,1)} %bitcast.2), calls=%async_computation | async-start | bytes 1572864 | tf_op jit(solution)/shard_map/all_to_all | solution.py:249
  35.9 18.7 %collective-permute-start.5 = (bf16[4128,128]{1,0:T(8,128)(2,1)}, bf16[4128,128]{1,0:T(8,128)(2,1)}, u32[]{:S(2)}, u32[]{:S(2)}) collective-permute-start(bf16[4128,128]{1,0:T(8,128)(2,1)} %collective-permute-done.rest_0_), channel_id=1, source_target_pairs={{0,8},{1,9},{2,10},{3,11},{4,12},{5,13},{6,14},{7,15},{8,0},{9,1},... | collective-permute-start | bytes 3170312 | tf_op jit(solution)/shard_map/ppermute | solution.py:56
  37.1 17.1 %collective-permute-start.8 = (bf16[4128,128]{1,0:T(8,128)(2,1)}, bf16[4128,128]{1,0:T(8,128)(2,1)}, u32[]{:S(2)}, u32[]{:S(2)}) collective-permute-start(bf16[4128,128]{1,0:T(8,128)(2,1)} %collective-permute-done.7.rest_6_), channel_id=1, source_target_pairs={{0,8},{1,9},{2,10},{3,11},{4,12},{5,13},{6,14},{7,15},{8,0},{9,1},... | collective-permute-start | bytes 3170312 | tf_op jit(solution)/shard_map/ppermute | solution.py:56
  53.6 14.3 %collective-permute-start.12 = (bf16[4128,128]{1,0:T(8,128)(2,1)}, bf16[4128,128]{1,0:T(8,128)(2,1)S(1)}, u32[]{:S(2)}, u32[]{:S(2)}) collective-permute-start(bf16[4128,128]{1,0:T(8,128)(2,1)} %collective-permute-done.2.rest_4_), channel_id=1, source_target_pairs={{0,4},{1,5},{2,6},{3,7},{4,16},{5,17},{6,18},{7,19},{8,28},{9,29},... | collective-permute-start | bytes 3170312 | tf_op jit(solution)/shard_map/ppermute | solution.py:56
  53.7 16.3 %collective-permute-start.9 = (bf16[4128,128]{1,0:T(8,128)(2,1)}, bf16[4128,128]{1,0:T(8,128)(2,1)S(1)}, u32[]{:S(2)}, u32[]{:S(2)}) collective-permute-start(bf16[4128,128]{1,0:T(8,128)(2,1)} %collective-permute-done.1.rest_8_), channel_id=1, source_target_pairs={{0,32},{1,33},{2,34},{3,35},{4,36},{5,37},{6,38},{7,39},{8,104},{9... | collective-permute-start | bytes 3170312 | tf_op jit(solution)/shard_map/ppermute | solution.py:56
  54.1 16.0 %collective-permute-start.6 = (bf16[4128,128]{1,0:T(8,128)(2,1)}, bf16[4128,128]{1,0:T(8,128)(2,1)S(1)}, u32[]{:S(2)}, u32[]{:S(2)}) collective-permute-start(bf16[4128,128]{1,0:T(8,128)(2,1)} %collective-permute-done.2.rest_4_), channel_id=1, source_target_pairs={{0,8},{1,9},{2,10},{3,11},{4,12},{5,13},{6,14},{7,15},{8,0},{9,1},... | collective-permute-start | bytes 3170312 | tf_op jit(solution)/shard_map/ppermute | solution.py:56
  54.1 16.0 %collective-permute-start.11 = (bf16[4128,128]{1,0:T(8,128)(2,1)}, bf16[4128,128]{1,0:T(8,128)(2,1)S(1)}, u32[]{:S(2)}, u32[]{:S(2)}) collective-permute-start(bf16[4128,128]{1,0:T(8,128)(2,1)} %collective-permute-done.1.rest_8_), channel_id=1, source_target_pairs={{0,8},{1,9},{2,10},{3,11},{4,12},{5,13},{6,14},{7,15},{8,0},{9,1},... | collective-permute-start | bytes 3170312 | tf_op jit(solution)/shard_map/ppermute | solution.py:56
  54.6 15.5 %collective-permute-start.4 = (bf16[4128,128]{1,0:T(8,128)(2,1)}, bf16[4128,128]{1,0:T(8,128)(2,1)S(1)}, u32[]{:S(2)}, u32[]{:S(2)}) collective-permute-start(bf16[4128,128]{1,0:T(8,128)(2,1)} %collective-permute-done.3.rest_2_), channel_id=1, source_target_pairs={{0,8},{1,9},{2,10},{3,11},{4,12},{5,13},{6,14},{7,15},{8,0},{9,1},... | collective-permute-start | bytes 3170312 | tf_op jit(solution)/shard_map/ppermute | solution.py:56
  67.9 4.4 %collective-permute-start.13 = (bf16[4128,128]{1,0:T(8,128)(2,1)S(1)}, bf16[4128,128]{1,0:T(8,128)(2,1)S(1)}, u32[]{:S(2)}, u32[]{:S(2)}) collective-permute-start(bf16[4128,128]{1,0:T(8,128)(2,1)S(1)} %collective-permute-done.12.rest_12_), channel_id=1, source_target_pairs={{0,8},{1,9},{2,10},{3,11},{4,12},{5,13},{6,14},{7,15},{8,0},{9,1},... | collective-permute-start | bytes 3170312 | tf_op jit(solution)/shard_map/ppermute | solution.py:56
  70.0 3.8 %collective-permute-start.10 = (bf16[4128,128]{1,0:T(8,128)(2,1)S(1)}, bf16[4128,128]{1,0:T(8,128)(2,1)S(1)}, u32[]{:S(2)}, u32[]{:S(2)}) collective-permute-start(bf16[4128,128]{1,0:T(8,128)(2,1)S(1)} %collective-permute-done.9.rest_10_), channel_id=1, source_target_pairs={{0,8},{1,9},{2,10},{3,11},{4,12},{5,13},{6,14},{7,15},{8,0},{9,1},... | collective-permute-start | bytes 3170312 | tf_op jit(solution)/shard_map/ppermute | solution.py:56
  73.9 0.7 copy-start.3

commit v6 on v5

v6 whole, which is shorter than its diff:
```python
import functools

import jax
import jax.numpy as jnp
from jax import lax
from jax.experimental import pallas as pl
from jax.experimental.pallas import tpu as pltpu
from jax.sharding import PartitionSpec as P

LAYERS = 2
C = 1024
BLOCKS = 16
LANES = 128
SHARDS = 8
RES = 24
ROWS = BLOCKS * RES
EXTRA = 16
HALF = C // 2
PART = 4 * HALF + EXTRA
EARLY = 4
AXES = ("seq", "filt")


def coords(i):
    z, i = i % 4, i // 4
    yl, i = i % 2, i // 2
    c, i = i % 2, i // 2
    yh, x = i % 2, i // 2
    return x, yh * 2 + yl, z, c


def linear(x, y, z, c):
    x, y, z = x % 4, y % 4, z % 4
    return (((x * 2 + y // 2) * 2 + c) * 2 + y % 2) * 4 + z


def route(step):
    return [(i, linear(*step(*coords(i)))) for i in range(128)]


Z_SIDE = route(lambda x, y, z, c: (x, y, z + 1 - 2 * (c ^ x & 1), c))
Y_SIDE = route(lambda x, y, z, c: (x, y + 1 - 2 * c, z, c))
X_SIDE = route(lambda x, y, z, c: (x + 1 - 2 * c, y, z, c))
SWAP = route(lambda x, y, z, c: (x, y, z, 1 - c))


def place():
    seq, filt = lax.axis_index("seq"), lax.axis_index("filt")
    core, parity = seq & 1, (seq >> 2) & 1
    z, yl = filt & 3, filt >> 2
    side = 2 * (core ^ parity) - 1
    zs = [z, (z + side) & 3, (z - side) & 3, (z + 2) & 3]
    return core, [yl * 4 + v for v in zs] + [(1 - yl) * 4 + v for v in zs]


def send(block, path):
    return lax.ppermute(block, AXES, path)


def three_parts(v):
    hi = v.astype(jnp.bfloat16).astype(jnp.float32)
    mid = (v - hi).astype(jnp.bfloat16).astype(jnp.float32)
    lo = v - hi - mid
    return [hi, mid, lo]


def prepare_kernel(conv_ref, mix_ref, conv_bias_ref, mix_bias_ref, own_ref, bias_ref, own, sems, out_sems):
    core, _ = place()
    rows = pl.ds(pl.multiple_of(core * HALF, HALF), HALF)
    arriving, leaving = [], []
    for layer in range(LAYERS):
        for t in range(4):
            source = conv_ref.at[layer, t, rows] if t < 3 else mix_ref.at[layer, rows]
            spot = pl.ds(layer * PART + t * HALF, HALF)
            arriving.append((source, own.at[spot]))
            leaving.append((own.at[spot], own_ref.at[spot]))
    arriving = [pltpu.make_async_copy(a, b, sems.at[i]) for i, (a, b) in enumerate(arriving)]
    for copy in arriving:
        copy.start()
    for layer in range(LAYERS):
        lines = three_parts(conv_bias_ref[layer:layer + 1, :]) + three_parts(mix_bias_ref[layer:layer + 1, :])
        lines.append(jnp.zeros((EXTRA - 6, LANES), jnp.float32))
        block = jnp.concatenate(lines, axis=0).astype(jnp.bfloat16)
        spot = slice(layer * PART + 4 * HALF, (layer + 1) * PART)
        own[spot, :] = block
        bias_ref[layer] = block
        leaving.append((own.at[spot], own_ref.at[spot]))
    leaving = [pltpu.make_async_copy(a, b, out_sems.at[i]) for i, (a, b) in enumerate(leaving)]
    for copy in leaving[len(arriving):]:
        copy.start()
    for coming, going in zip(arriving, leaving):
        coming.wait()
        going.start()
    for copy in leaving:
        copy.wait()


def prepare(conv, mix, conv_bias, mix_bias):
    anywhere = pl.BlockSpec(memory_space=pl.ANY)
    vmem = pl.BlockSpec(memory_space=pltpu.VMEM)
    return pl.pallas_call(
        prepare_kernel,
        out_shape=[
            jax.ShapeDtypeStruct((LAYERS * PART, LANES), jnp.bfloat16),
            jax.ShapeDtypeStruct((LAYERS, EXTRA, LANES), jnp.bfloat16),
        ],
        in_specs=[anywhere, anywhere, vmem, vmem],
        out_specs=[anywhere, vmem],
        scratch_shapes=[
            pltpu.VMEM((LAYERS * PART, LANES), jnp.bfloat16),
            pltpu.SemaphoreType.DMA((4 * LAYERS,)),
            pltpu.SemaphoreType.DMA((5 * LAYERS,)),
        ],
        compiler_params=pltpu.CompilerParams(vmem_limit_bytes=60 * 2**20),
        cost_estimate=pl.CostEstimate(flops=0, bytes_accessed=4 * 2**20, transcendentals=0),
        name="prepare",
    )(conv, mix, conv_bias, mix_bias)


def sides(core):
    halves = (core, 1 - core)
    return [pl.ds(pl.multiple_of(v * HALF, HALF), HALF) for v in halves]


def home(shard):
    return pl.ds(pl.multiple_of(shard * LANES, LANES), LANES)


def normalize(layer, x, gain_ref, normed, n, halves):
    wide = x[...]
    scale = lax.rsqrt(jnp.mean(wide * wide, axis=-1, keepdims=True) + 1e-06)
    normed[...] = wide * scale * gain_ref[layer:layer + 1, :]
    shift = RES * 2**layer
    edge = jnp.zeros((shift, HALF), jnp.float32)
    for i in range(2):
        here = normed[:, halves[i]]
        earlier = jnp.concatenate([edge, here[:ROWS - shift]], axis=0)
        later = jnp.concatenate([here[shift:], edge], axis=0)
        for t, rows in enumerate((earlier, here, later)):
            start = (3 * i + t) * HALF
            n[:, start:start + HALF] = rows.astype(jnp.bfloat16)


def bias_row(rows, start):
    rows = rows.astype(jnp.float32)
    return rows[start:start + 1] + rows[start + 1:start + 2] + rows[start + 2:start + 3]


def convolve(n, columns, biases, act, homes):
    hidden = jnp.dot(n[...], jnp.concatenate(columns, axis=1), preferred_element_type=jnp.float32)
    hidden = hidden + jnp.concatenate([bias_row(v, 0) for v in biases], axis=1)
    done = (hidden * (1.0 + lax.erf(hidden * 0.7071067811865476)) * 0.5).astype(jnp.bfloat16)
    for h in range(2):
        act[:, home(homes[h])] = done[:, h * LANES:(h + 1) * LANES]


def head_kernel(x_ref, gain_ref, bias_ref, conv_ref, *rest):
    parts = rest[:2 * (EARLY - 1)]
    x, n, act, w, mine, normed, sems, mine_sem = rest[2 * (EARLY - 1):]
    core, homes = place()
    halves = sides(core)
    arriving = [[pltpu.make_async_copy(conv_ref.at[0], mine, mine_sem.at[0])]]
    for k in range(1, EARLY):
        copies = []
        for p in (2 * k - 2, 2 * k - 1):
            copies.append(pltpu.make_async_copy(parts[p].at[pl.ds(0, PART)], w.at[p], sems.at[p]))
        arriving.append(copies)
    for copies in arriving:
        for copy in copies:
            copy.start()
    for b in range(BLOCKS):
        for f in range(SHARDS):
            x[b * RES:(b + 1) * RES, f * LANES:(f + 1) * LANES] = x_ref[b * SHARDS + f].astype(jnp.float32)
    normalize(0, x, gain_ref, normed, n, halves)

    def column(k):
        if k == 0:
            return jnp.concatenate([mine[t, halves[i], :] for i in range(2) for t in range(3)], axis=0)
        return jnp.concatenate([w[2 * k - 2 + i, :3 * HALF, :] for i in range(2)], axis=0)

    for k in range(0, EARLY, 2):
        for copy in arriving[k] + arriving[k + 1]:
            copy.wait()
        biases = [bias_ref[0] if k == 0 else w[2 * k - 2, 4 * HALF:, :], w[2 * k, 4 * HALF:, :]]
        convolve(n, [column(k), column(k + 1)], biases, act, homes[k:k + 2])
    for k in range(EARLY, SHARDS):
        act[:, home(homes[k])] = jnp.zeros((ROWS, LANES), jnp.bfloat16)


def run_head(x, gain, bias, conv, parts):
    vmem = pl.BlockSpec(memory_space=pltpu.VMEM)
    anywhere = pl.BlockSpec(memory_space=pl.ANY)
    return pl.pallas_call(
        head_kernel,
        out_shape=[
            jax.ShapeDtypeStruct((ROWS, C), jnp.float32),
            jax.ShapeDtypeStruct((ROWS, 3 * C), jnp.bfloat16),
            jax.ShapeDtypeStruct((ROWS, C), jnp.bfloat16),
        ],
        in_specs=[vmem, vmem, vmem] + [anywhere] * (1 + len(parts)),
        out_specs=[vmem] * 3,
        scratch_shapes=[
            pltpu.VMEM((len(parts), PART, LANES), jnp.bfloat16),
            pltpu.VMEM((3, C, LANES), jnp.bfloat16),
            pltpu.VMEM((ROWS, C), jnp.float32),
            pltpu.SemaphoreType.DMA((len(parts),)),
            pltpu.SemaphoreType.DMA((1,)),
        ],
        compiler_params=pltpu.CompilerParams(vmem_limit_bytes=20 * 2**20),
        cost_estimate=pl.CostEstimate(flops=4 * ROWS * C * C, bytes_accessed=9 * 2**20, transcendentals=ROWS * C),
        name="head",
    )(x, gain, bias, conv, *parts)


def tail_kernel(x_ref, n_ref, act_ref, gain_ref, bias_ref, conv_ref, mix_ref, *rest):
    parts = rest[:2 * (SHARDS - 1)]
    out_ref, w, mine, x, normed, n, act, mixing, sems, late_sems, mine_sems = rest[2 * (SHARDS - 1):]
    core, homes = place()
    halves = sides(core)
    order = list(range(EARLY, SHARDS)) + list(range(EARLY))
    coming = {}
    for layer in range(LAYERS):
        for k in order if layer == 0 else range(SHARDS):
            if k == 0:
                copies = [pltpu.make_async_copy(mix_ref.at[layer], mine.at[layer, 3], mine_sems.at[layer, 1])]
                if layer > 0:
                    copies.append(pltpu.make_async_copy(conv_ref.at[layer], mine.at[layer, pl.ds(0, 3)], mine_sems.at[layer, 0]))
            else:
                rows = pl.ds(layer * PART, PART) if layer > 0 or k >= EARLY else pl.ds(3 * HALF, HALF + EXTRA)
                copies = []
                for p in (2 * k - 2, 2 * k - 1):
                    sem = (late_sems if layer > 0 else sems).at[p]
                    copies.append(pltpu.make_async_copy(parts[p].at[rows], w.at[p, rows], sem))
            for copy in copies:
                copy.start()
            coming[layer, k] = copies

    def arrived(layer, pair):
        for k in pair:
            for copy in coming.pop((layer, k), []):
                copy.wait()

    x[...] = x_ref[...]
    act[...] = act_ref[...]
    for layer in range(LAYERS):
        base = layer * PART

        def column(k, start, stop):
            if k == 0:
                return jnp.concatenate([mine[layer, t, halves[i], :] for i in range(2) for t in range(start, stop)], axis=0)
            spot = slice(base + start * HALF, base + stop * HALF)
            return jnp.concatenate([w[2 * k - 2 + i, spot, :] for i in range(2)], axis=0)

        def lines(k):
            return bias_ref[layer] if k == 0 else w[2 * k - 2, base + 4 * HALF:base + PART, :]

        if layer > 0:
            normalize(layer, x, gain_ref, normed, n, halves)
        for k in range(EARLY if layer == 0 else 0, SHARDS, 2):
            pair = (k, k + 1)
            arrived(layer, pair)
            convolve(n_ref if layer == 0 else n, [column(v, 0, 3) for v in pair], [lines(v) for v in pair], act, homes[k:k + 2])
        for i in range(2):
            mixing[:, i * HALF:(i + 1) * HALF] = act[:, halves[i]]
        for k in range(0, SHARDS, 2):
            pair = (k, k + 1)
            arrived(layer, pair)
            mixed = jnp.dot(mixing[...], jnp.concatenate([column(v, 3, 4) for v in pair], axis=1), preferred_element_type=jnp.float32)
            mixed = mixed + jnp.concatenate([bias_row(lines(v), 3) for v in pair], axis=1)
            for h, v in enumerate(pair):
                total = x[:, home(homes[v])] + mixed[:, h * LANES:(h + 1) * LANES]
                if layer == LAYERS - 1:
                    for b in range(BLOCKS):
                        out_ref[b * SHARDS + homes[v]] = total[b * RES:(b + 1) * RES].astype(jnp.bfloat16)
                else:
                    x[:, home(homes[v])] = total.astype(jnp.bfloat16).astype(jnp.float32)


def run_tail(x, n, act, gain, bias, conv, mix, parts):
    vmem = pl.BlockSpec(memory_space=pltpu.VMEM)
    anywhere = pl.BlockSpec(memory_space=pl.ANY)
    return pl.pallas_call(
        tail_kernel,
        out_shape=jax.ShapeDtypeStruct((BLOCKS * SHARDS, RES, LANES), jnp.bfloat16),
        in_specs=[vmem] * 5 + [anywhere] * (2 + len(parts)),
        out_specs=vmem,
        scratch_shapes=[
            pltpu.VMEM((len(parts), LAYERS * PART, LANES), jnp.bfloat16),
            pltpu.VMEM((LAYERS, 4, C, LANES), jnp.bfloat16),
            pltpu.VMEM((ROWS, C), jnp.float32),
            pltpu.VMEM((ROWS, C), jnp.float32),
            pltpu.VMEM((ROWS, 3 * C), jnp.bfloat16),
            pltpu.VMEM((ROWS, C), jnp.bfloat16),
            pltpu.VMEM((ROWS, C), jnp.bfloat16),
            pltpu.SemaphoreType.DMA((len(parts),)),
            pltpu.SemaphoreType.DMA((len(parts),)),
            pltpu.SemaphoreType.DMA((LAYERS, 2)),
        ],
        compiler_params=pltpu.CompilerParams(vmem_limit_bytes=30 * 2**20),
        cost_estimate=pl.CostEstimate(flops=12 * ROWS * C * C, bytes_accessed=14 * 2**20, transcendentals=ROWS * C),
        name="tail",
    )(x, n, act, gain, bias, conv, mix, *parts)


def per_device(tokens, conv_weight, conv_bias, mix_weight, mix_bias, norm_gain):
    own, bias = prepare(conv_weight, mix_weight, conv_bias, mix_bias)
    a = send(own, Z_SIDE)
    own_y = send(own, Y_SIDE)
    padded = jnp.pad(tokens, ((0, 128 * RES - tokens.shape[0]), (0, 0)))
    a, own_y, padded = lax.optimization_barrier((a, own_y, padded))
    x = lax.all_to_all(padded.reshape(128, RES, LANES), AXES, split_axis=0, concat_axis=0, tiled=True)
    b = send(a, X_SIDE)
    e = send(a, Z_SIDE)
    a_y = send(a, Y_SIDE)
    a_y, e, b, x = lax.optimization_barrier((a_y, e, b, x))
    b_y = send(a_y, X_SIDE)
    e_y = send(e, Y_SIDE)
    swapped = [send(v, SWAP) for v in (b, a, e)]
    early = [v for pair in zip((a, b, e), swapped) for v in pair]
    x, n, act = run_head(x, norm_gain, bias, conv_weight, early)
    b_y, e_y, act = lax.optimization_barrier((b_y, e_y, act))
    late = (own_y, a_y, b_y, e_y)
    swapped = [send(v, SWAP) for v in (own_y, b_y, a_y, e_y)]
    parts = early + [v for pair in zip(late, swapped) for v in pair]
    x = run_tail(x, n, act, norm_gain, bias, conv_weight, mix_weight, parts)
    y = lax.all_to_all(x, AXES, split_axis=0, concat_axis=0, tiled=True)
    return y.reshape(128 * RES, LANES)[:tokens.shape[0]]


def solution(mesh):
    in_specs = (
        P("seq", "filt"),
        P(None, None, None, "filt"),
        P(None, "filt"),
        P(None, None, "filt"),
        P(None, "filt"),
        P(),
    )
    out_specs = P("seq", "filt")
    return jax.shard_map(
        per_device, mesh=mesh, in_specs=in_specs, out_specs=out_specs, check_vma=False
    )
```

time: 112 us -> 111 us (level)
  waiting for transfers between devices: 42.8 us -> 40.8 us
  starting transfers between devices: 27 us -> 25.4 us
  Pallas kernels: 19.5 us -> 20.8 us
    ppermute x14, waiting for transfers between devices: 26.4 us -> 24.5 us  [send(): return lax.ppermute(block, AXES, path)]
    pallas_call x2 -> x3, Pallas kernels: 19.5 us -> 20.8 us  [the longest x1 13.6 us: run_tail(): pl.pallas_call(tail_kernel, out_shape=jax.ShapeDtypeStruct((BLOCKS * SHAR...]
  transfers between devices with their start and end apart: 15 -> 15, of which waited for: 5 -> 9; matrix products, arithmetic and copies ran while one was open for 0% -> 1% of each run, Pallas kernels for 0% -> 3%
where the time goes in v6:
time: 111 us
  waiting for transfers between devices  40.8 us (37%)
  starting transfers between devices  25.4 us (23%)
  blocking collectives  22 us (20%)
  Pallas kernels  20.8 us (19%)
  local copies, waits for them, and re-layouts  1.9 us (2%)
    ppermute x14, waiting for transfers between devices, send(): return lax.ppermute(block, AXES, path)  24.5 us
    all_to_all x1, blocking collectives, per_device(): y = lax.all_to_all(x, AXES, split_axis=0, concat_axis=0, tiled=True)  22 us
    ppermute x14, starting transfers between devices, send(): return lax.ppermute(block, AXES, path)  18.6 us
    all_to_all x1, waiting for transfers between devices, per_device(): lax.all_to_all(padded.reshape(128, RES, LANES), AXES, split_axis=0, conca...  16.3 us
    pallas_call x1, Pallas kernels, run_tail(): pl.pallas_call(tail_kernel, out_shape=jax.ShapeDtypeStruct((BLOCKS * SHAR...  13.6 us
    all_to_all x1, starting transfers between devices, per_device(): lax.all_to_all(padded.reshape(128, RES, LANES), AXES, split_axis=0, conca...  6.82 us
    pallas_call x1, Pallas kernels, run_head(): pl.pallas_call(head_kernel, out_shape=[jax.ShapeDtypeStruct((ROWS, C), jn...  3.71 us
    pallas_call x1, Pallas kernels, prepare(): pl.pallas_call(prepare_kernel, out_shape=[jax.ShapeDtypeStruct((LAYERS *...  3.5 us
  transfers between devices with their start and end apart: 15, of which 9 were waited for; matrix products, arithmetic and copies ran while one was open for 1% of the time, Pallas kernels for 3%

profile of v6, /device:TPU:1, one launch (start us, length us, event | category | flops | bytes accessed | tf_op | source)
XLA Modules:
  0.0 110.9 jit_solution(11907475843834890778)
XLA Ops:
  0.0 0.0 copy-start.6
  0.0 3.5 %prepare.1 = (bf16[4128,128]{1,0:T(8,128)(2,1)}, bf16[2,16,128]{2,1,0:T(8,128)(2,1)}) custom-call(bf16[2,3,1024,128]{3,2,1,0:T(8,128)(2,1)} %conv_ref.5, bf16[2,1024,128]{2,1,0:T(8,128)(2,1)} %mix_ref.3, f32[2,128]{1,0:T(2,128)} %conv_bias_ref.1, f32[2,128]{1,0:T(2,128)} %mix_bias_ref.1), custom_call_target="tpu_custom_call" | custom-call | bytes 4194304 | tf_op jit(solution)/shard_map/prepare/pallas_call | solution.py:101
  3.5 3.6 %collective-permute-start.1 = (bf16[4128,128]{1,0:T(8,128)(2,1)}, bf16[4128,128]{1,0:T(8,128)(2,1)S(1)}, u32[]{:S(2)}, u32[]{:S(2)}) collective-permute-start(bf16[4128,128]{1,0:T(8,128)(2,1)} %get-tuple-element.20), channel_id=1, source_target_pairs={{0,4},{1,5},{2,6},{3,7},{4,16},{5,17},{6,18},{7,19},{8,28},{9,29},... | collective-permute-start | bytes 3170312 | tf_op jit(solution)/shard_map/ppermute | solution.py:57
  7.1 3.8 %collective-permute-start = (bf16[4128,128]{1,0:T(8,128)(2,1)}, bf16[4128,128]{1,0:T(8,128)(2,1)S(1)}, u32[]{:S(2)}, u32[]{:S(2)}) collective-permute-start(bf16[4128,128]{1,0:T(8,128)(2,1)} %get-tuple-element.20), channel_id=1, source_target_pairs={{0,1},{1,2},{2,3},{3,0},{4,5},{5,6},{6,7},{7,4},{8,11},{9,8},{10,9... | collective-permute-start | bytes 3170312 | tf_op jit(solution)/shard_map/ppermute | solution.py:57
  10.9 0.0 copy-done.6
  10.9 0.0 copy-start.5
  10.9 1.0 pad.4
  11.9 0.0 copy-start
  11.9 7.4 %collective-permute-done.1.rest_6_ = bf16[4128,128]{1,0:T(8,128)(2,1)S(1)} collective-permute-done((bf16[4128,128]{1,0:T(8,128)(2,1)}, bf16[4128,128]{1,0:T(8,128)(2,1)S(1)}, u32[]{:S(2)}, u32[]{:S(2)}) %collective-permute-start.1) | collective-permute-done | bytes 1056800 | tf_op jit(solution)/shard_map/ppermute | solution.py:57
  19.3 3.8 %collective-permute-done.rest_0_ = bf16[4128,128]{1,0:T(8,128)(2,1)S(1)} collective-permute-done((bf16[4128,128]{1,0:T(8,128)(2,1)}, bf16[4128,128]{1,0:T(8,128)(2,1)S(1)}, u32[]{:S(2)}, u32[]{:S(2)}) %collective-permute-start) | collective-permute-done | bytes 1056800 | tf_op jit(solution)/shard_map/ppermute | solution.py:57
  23.0 2.8 %collective-permute-start.4 = (bf16[4128,128]{1,0:T(8,128)(2,1)S(1)}, bf16[4128,128]{1,0:T(8,128)(2,1)}, u32[]{:S(2)}, u32[]{:S(2)}) collective-permute-start(bf16[4128,128]{1,0:T(8,128)(2,1)S(1)} %collective-permute-done.rest_0_), channel_id=1, source_target_pairs={{0,32},{1,33},{2,34},{3,35},{4,36},{5,37},{6,38},{7,39},{8,104},{9... | collective-permute-start | bytes 3170312 | tf_op jit(solution)/shard_map/ppermute | solution.py:57
  25.9 0.0 copy-done.2
  25.9 1.7 %collective-permute-start.3 = (bf16[4128,128]{1,0:T(8,128)(2,1)S(1)}, bf16[4128,128]{1,0:T(8,128)(2,1)}, u32[]{:S(2)}, u32[]{:S(2)}) collective-permute-start(bf16[4128,128]{1,0:T(8,128)(2,1)S(1)} %collective-permute-done.rest_0_), channel_id=1, source_target_pairs={{0,1},{1,2},{2,3},{3,0},{4,5},{5,6},{6,7},{7,4},{8,11},{9,8},{10,9... | collective-permute-start | bytes 3170312 | tf_op jit(solution)/shard_map/ppermute | solution.py:57
  27.6 1.2 %collective-permute-start.2 = (bf16[4128,128]{1,0:T(8,128)(2,1)S(1)}, bf16[4128,128]{1,0:T(8,128)(2,1)}, u32[]{:S(2)}, u32[]{:S(2)}) collective-permute-start(bf16[4128,128]{1,0:T(8,128)(2,1)S(1)} %collective-permute-done.rest_0_), channel_id=1, source_target_pairs={{0,4},{1,5},{2,6},{3,7},{4,16},{5,17},{6,18},{7,19},{8,28},{9,29},... | collective-permute-start | bytes 3170312 | tf_op jit(solution)/shard_map/ppermute | solution.py:57
  28.8 6.8 %all-to-all-start = ((bf16[128,24,128]{2,1,0:T(8,128)(2,1)}), bf16[128,24,128]{2,1,0:T(8,128)(2,1)S(1)}, u32[]{:S(2)}, u32[]{:S(2)}) async-start(bf16[128,24,128]{2,1,0:T(8,128)(2,1)} %bitcast.2), calls=%async_computation | async-start | bytes 1572864 | tf_op jit(solution)/shard_map/all_to_all | solution.py:311
  35.7 1.1 %collective-permute-start.6 = (bf16[4128,128]{1,0:T(8,128)(2,1)S(1)}, bf16[4128,128]{1,0:T(8,128)(2,1)}, u32[]{:S(2)}, u32[]{:S(2)}) collective-permute-start(bf16[4128,128]{1,0:T(8,128)(2,1)S(1)} %collective-permute-done.rest_0_), channel_id=1, source_target_pairs={{0,8},{1,9},{2,10},{3,11},{4,12},{5,13},{6,14},{7,15},{8,0},{9,1},... | collective-permute-start | bytes 3170312 | tf_op jit(solution)/shard_map/ppermute | solution.py:57
  36.8 16.3 %all-to-all-done.x_ref = bf16[128,24,128]{2,1,0:T(8,128)(2,1)S(1)} async-done(((bf16[128,24,128]{2,1,0:T(8,128)(2,1)}), bf16[128,24,128]{2,1,0:T(8,128)(2,1)S(1)}, u32[]{:S(2)}, u32[]{:S(2)}) %all-to-all-start) | async-done | bytes 786464 | tf_op jit(solution)/shard_map/all_to_all | solution.py:311
  53.1 0.0 collective-permute-done.4.rest_2_
  53.1 0.0 collective-permute-done.3.rest_4_
  53.1 0.0 collective-permute-done.2.rest_8_
  53.1 0.3 collective-permute-start.5
  53.4 0.3 collective-permute-start.7
  53.7 0.5 collective-permute-start.8
  54.2 0.8 collective-permute-start.9
  55.0 0.0 collective-permute-done.6.rest_3_
  55.0 0.0 collective-permute-start.10
  55.0 1.1 collective-permute-done.5.rest_1_
  56.1 0.2 collective-permute-start.12
  56.3 1.3 %collective-permute-done.7.rest_5_ = bf16[4128,128]{1,0:T(8,128)(2,1)S(1)} collective-permute-done((bf16[4128,128]{1,0:T(8,128)(2,1)}, bf16[4128,128]{1,0:T(8,128)(2,1)S(1)}, u32[]{:S(2)}, u32[]{:S(2)}) %collective-permute-start.7) | collective-permute-done | bytes 1056800 | tf_op jit(solution)/shard_map/ppermute | solution.py:57
  57.6 0.0 copy-done.4
  57.6 0.0 copy-done.5
  57.6 0.0 copy-done
  57.6 0.0 copy-start.1
  57.6 0.0 copy-start.3
  57.6 3.7 %head.1 = (f32[384,1024]{1,0:T(8,128)S(1)}, bf16[384,3072]{1,0:T(8,128)(2,1)S(1)}, bf16[384,1024]{1,0:T(8,128)(2,1)S(1)}) custom-call(bf16[128,24,128]{2,1,0:T(8,128)(2,1)S(1)} %all-to-all-done.x_ref, f32[2,1024]{1,0:T(2,128)S(1)} %copy-done.4, bf16[2,16,128]{2,1,0:T(8,128)(2,1)S(1)} %copy-done.5, bf16[2,3,1024,128]{3,2,1,0:T(8,128)(2,1)S(1)} %copy-done, ...), custom_call_target="tpu_custom_call" | custom-call | flops 1610612736 | bytes 9437184 | tf_op jit(solution)/shard_map/head/pallas_call | solution.py:193
  61.3 6.6 %collective-permute-done.8.rest_10_ = bf16[4128,128]{1,0:T(8,128)(2,1)S(1)} collective-permute-done((bf16[4128,128]{1,0:T(8,128)(2,1)}, bf16[4128,128]{1,0:T(8,128)(2,1)S(1)}, u32[]{:S(2)}, u32[]{:S(2)}) %collective-permute-start.8) | collective-permute-done | bytes 1056800 | tf_op jit(solution)/shard_map/ppermute | solution.py:57
  67.9 0.5 collective-permute-done.9.rest_12_
  68.4 2.2 %collective-permute-start.11 = (bf16[4128,128]{1,0:T(8,128)(2,1)S(1)}, bf16[4128,128]{1,0:T(8,128)(2,1)S(1)}, u32[]{:S(2)}, u32[]{:S(2)}) collective-permute-start(bf16[4128,128]{1,0:T(8,128)(2,1)S(1)} %collective-permute-done.8.rest_10_), channel_id=1, source_target_pairs={{0,8},{1,9},{2,10},{3,11},{4,12},{5,13},{6,14},{7,15},{8,0},{9,1},... | collective-permute-start | bytes 3170312 | tf_op jit(solution)/shard_map/ppermute | solution.py:57
  70.6 0.0 collective-permute-start.13
  70.6 0.0 collective-permute-done.10.rest_7_
  70.6 0.0 collective-permute-done.12.rest_11_
  70.6 2.3 %collective-permute-done.11.rest_9_ = bf16[4128,128]{1,0:T(8,128)(2,1)S(1)} collective-permute-done((bf16[4128,128]{1,0:T(8,128)(2,1)S(1)}, bf16[4128,128]{1,0:T(8,128)(2,1)S(1)}, u32[]{:S(2)}, u32[]{:S(2)}) %collective-permute-start.11) | collective-permute-done | bytes 1056800 | tf_op jit(solution)/shard_map/ppermute | solution.py:57
  72.9 1.5 %collective-permute-done.13.rest_13_ = bf16[4128,128]{1,0:T(8,128)(2,1)S(1)} collective-permute-done((bf16[4128,128]{1,0:T(8,128)(2,1)S(1)}, bf16[4128,128]{1,0:T(8,128)(2,1)S(1)}, u32[]{:S(2)}, u32[]{:S(2)}) %collective-permute-start.13) | collective-permute-done | bytes 1056800 | tf_op jit(solution)/shard_map/ppermute | solution.py:57
  74.4 0.0 copy-done.1
  74.4 0.0 copy-done.3
  74.4 13.6 %tail.1 = bf16[128,24,128]{2,1,0:T(8,128)(2,1)S(1)} custom-call(f32[384,1024]{1,0:T(8,128)S(1)} %get-tuple-element.27.x_ref, bf16[384,3072]{1,0:T(8,128)(2,1)S(1)} %get-tuple-element.28.n_ref, bf16[384,1024]{1,0:T(8,128)(2,1)S(1)} %get-tuple-element.31.act_ref, f32[2,1024]{1,0:T(2,128)S(1)} %copy-done.4, bf16[2,16,128]{2,1,0:T(8,128)(2,1)S(1)} %copy-done.5, ...), custom_call_target="tpu_custom_call" | custom-call | flops 4831838208 | bytes 14680064 | tf_op jit(solution)/shard_map/tail/pallas_call | solution.py:282
  88.0 22.0 %all_to_all.10 = bf16[128,24,128]{2,1,0:T(8,128)(2,1)S(1)} all-to-all(bf16[128,24,128]{2,1,0:T(8,128)(2,1)S(1)} %tail.1), channel_id=1, replica_groups=mesh['seq'=16,'filt'=8] {'seq','filt'}, dimensions={0} | all-to-all | bytes 1572864 | tf_op jit(solution)/shard_map/all_to_all | solution.py:326
  110.0 0.9 slice.8
  (2 shorter events, 0.0 us)
Async XLA Ops:
  0.0 10.9 %copy-start.6 = (bf16[2688,128]{1,0:T(8,128)(2,1)S(1)}, bf16[2688,128]{1,0:T(8,128)(2,1)}, u32[]{:S(2)}) copy-start(bf16[2688,128]{1,0:T(8,128)(2,1)} %param.6) | copy-start | bytes 2064388
  3.5 15.8 %collective-permute-start.1 = (bf16[4128,128]{1,0:T(8,128)(2,1)}, bf16[4128,128]{1,0:T(8,128)(2,1)S(1)}, u32[]{:S(2)}, u32[]{:S(2)}) collective-permute-start(bf16[4128,128]{1,0:T(8,128)(2,1)} %get-tuple-element.20), channel_id=1, source_target_pairs={{0,4},{1,5},{2,6},{3,7},{4,16},{5,17},{6,18},{7,19},{8,28},{9,29},... | collective-permute-start | bytes 3170312 | tf_op jit(solution)/shard_map/ppermute | solution.py:57
  7.1 15.9 %collective-permute-start = (bf16[4128,128]{1,0:T(8,128)(2,1)}, bf16[4128,128]{1,0:T(8,128)(2,1)S(1)}, u32[]{:S(2)}, u32[]{:S(2)}) collective-permute-start(bf16[4128,128]{1,0:T(8,128)(2,1)} %get-tuple-element.20), channel_id=1, source_target_pairs={{0,1},{1,2},{2,3},{3,0},{4,5},{5,6},{6,7},{7,4},{8,11},{9,8},{10,9... | collective-permute-start | bytes 3170312 | tf_op jit(solution)/shard_map/ppermute | solution.py:57
  10.9 46.7 %copy-start.4 = (f32[2,1024]{1,0:T(2,128)S(1)}, f32[2,1024]{1,0:T(2,128)}, u32[]{:S(2)}) copy-start(f32[2,1024]{1,0:T(2,128)} %gain_ref.3) | copy-start | bytes 24580
  10.9 46.7 %copy-start.5 = (bf16[2,16,128]{2,1,0:T(8,128)(2,1)S(1)}, bf16[2,16,128]{2,1,0:T(8,128)(2,1)}, u32[]{:S(2)}) copy-start(bf16[2,16,128]{2,1,0:T(8,128)(2,1)} %get-tuple-element.24.bias_ref) | copy-start | bytes 24580
  11.9 45.7 %copy-start = (bf16[2,3,1024,128]{3,2,1,0:T(8,128)(2,1)S(1)}, bf16[2,3,1024,128]{3,2,1,0:T(8,128)(2,1)}, u32[]{:S(2)}) copy-start(bf16[2,3,1024,128]{3,2,1,0:T(8,128)(2,1)} %conv_ref.5) | copy-start | bytes 4718596
  19.3 6.6 %copy-start.2 = (bf16[4128,128]{1,0:T(8,128)(2,1)}, bf16[4128,128]{1,0:T(8,128)(2,1)S(1)}, u32[]{:S(2)}) copy-start(bf16[4128,128]{1,0:T(8,128)(2,1)S(1)} %collective-permute-done.1.rest_6_) | copy-start | bytes 3170308
  23.0 30.1 %collective-permute-start.4 = (bf16[4128,128]{1,0:T(8,128)(2,1)S(1)}, bf16[4128,128]{1,0:T(8,128)(2,1)}, u32[]{:S(2)}, u32[]{:S(2)}) collective-permute-start(bf16[4128,128]{1,0:T(8,128)(2,1)S(1)} %collective-permute-done.rest_0_), channel_id=1, source_target_pairs={{0,32},{1,33},{2,34},{3,35},{4,36},{5,37},{6,38},{7,39},{8,104},{9... | collective-permute-start | bytes 3170312 | tf_op jit(solution)/shard_map/ppermute | solution.py:57
  25.9 27.2 %collective-permute-start.3 = (bf16[4128,128]{1,0:T(8,128)(2,1)S(1)}, bf16[4128,128]{1,0:T(8,128)(2,1)}, u32[]{:S(2)}, u32[]{:S(2)}) collective-permute-start(bf16[4128,128]{1,0:T(8,128)(2,1)S(1)} %collective-permute-done.rest_0_), channel_id=1, source_target_pairs={{0,1},{1,2},{2,3},{3,0},{4,5},{5,6},{6,7},{7,4},{8,11},{9,8},{10,9... | collective-permute-start | bytes 3170312 | tf_op jit(solution)/shard_map/ppermute | solution.py:57
  27.6 25.5 %collective-permute-start.2 = (bf16[4128,128]{1,0:T(8,128)(2,1)S(1)}, bf16[4128,128]{1,0:T(8,128)(2,1)}, u32[]{:S(2)}, u32[]{:S(2)}) collective-permute-start(bf16[4128,128]{1,0:T(8,128)(2,1)S(1)} %collective-permute-done.rest_0_), channel_id=1, source_target_pairs={{0,4},{1,5},{2,6},{3,7},{4,16},{5,17},{6,18},{7,19},{8,28},{9,29},... | collective-permute-start | bytes 3170312 | tf_op jit(solution)/shard_map/ppermute | solution.py:57
  28.8 24.3 %all-to-all-start = ((bf16[128,24,128]{2,1,0:T(8,128)(2,1)}), bf16[128,24,128]{2,1,0:T(8,128)(2,1)S(1)}, u32[]{:S(2)}, u32[]{:S(2)}) async-start(bf16[128,24,128]{2,1,0:T(8,128)(2,1)} %bitcast.2), calls=%async_computation | async-start | bytes 1572864 | tf_op jit(solution)/shard_map/all_to_all | solution.py:311
  35.7 19.3 %collective-permute-start.6 = (bf16[4128,128]{1,0:T(8,128)(2,1)S(1)}, bf16[4128,128]{1,0:T(8,128)(2,1)}, u32[]{:S(2)}, u32[]{:S(2)}) collective-permute-start(bf16[4128,128]{1,0:T(8,128)(2,1)S(1)} %collective-permute-done.rest_0_), channel_id=1, source_target_pairs={{0,8},{1,9},{2,10},{3,11},{4,12},{5,13},{6,14},{7,15},{8,0},{9,1},... | collective-permute-start | bytes 3170312 | tf_op jit(solution)/shard_map/ppermute | solution.py:57
  53.1 3.0 %collective-permute-start.5 = (bf16[4128,128]{1,0:T(8,128)(2,1)}, bf16[4128,128]{1,0:T(8,128)(2,1)S(1)}, u32[]{:S(2)}, u32[]{:S(2)}) collective-permute-start(bf16[4128,128]{1,0:T(8,128)(2,1)} %collective-permute-done.4.rest_2_), channel_id=1, source_target_pairs={{0,8},{1,9},{2,10},{3,11},{4,12},{5,13},{6,14},{7,15},{8,0},{9,1},... | collective-permute-start | bytes 3170312 | tf_op jit(solution)/shard_map/ppermute | solution.py:57
  53.4 4.2 %collective-permute-start.7 = (bf16[4128,128]{1,0:T(8,128)(2,1)}, bf16[4128,128]{1,0:T(8,128)(2,1)S(1)}, u32[]{:S(2)}, u32[]{:S(2)}) collective-permute-start(bf16[4128,128]{1,0:T(8,128)(2,1)} %collective-permute-done.3.rest_4_), channel_id=1, source_target_pairs={{0,8},{1,9},{2,10},{3,11},{4,12},{5,13},{6,14},{7,15},{8,0},{9,1},... | collective-permute-start | bytes 3170312 | tf_op jit(solution)/shard_map/ppermute | solution.py:57
  53.7 14.2 %collective-permute-start.8 = (bf16[4128,128]{1,0:T(8,128)(2,1)}, bf16[4128,128]{1,0:T(8,128)(2,1)S(1)}, u32[]{:S(2)}, u32[]{:S(2)}) collective-permute-start(bf16[4128,128]{1,0:T(8,128)(2,1)} %collective-permute-done.2.rest_8_), channel_id=1, source_target_pairs={{0,32},{1,33},{2,34},{3,35},{4,36},{5,37},{6,38},{7,39},{8,104},{9... | collective-permute-start | bytes 3170312 | tf_op jit(solution)/shard_map/ppermute | solution.py:57
  54.2 14.2 %collective-permute-start.9 = (bf16[4128,128]{1,0:T(8,128)(2,1)}, bf16[4128,128]{1,0:T(8,128)(2,1)S(1)}, u32[]{:S(2)}, u32[]{:S(2)}) collective-permute-start(bf16[4128,128]{1,0:T(8,128)(2,1)} %collective-permute-done.3.rest_4_), channel_id=1, source_target_pairs={{0,4},{1,5},{2,6},{3,7},{4,16},{5,17},{6,18},{7,19},{8,28},{9,29},... | collective-permute-start | bytes 3170312 | tf_op jit(solution)/shard_map/ppermute | solution.py:57
  55.0 15.7 %collective-permute-start.10 = (bf16[4128,128]{1,0:T(8,128)(2,1)}, bf16[4128,128]{1,0:T(8,128)(2,1)S(1)}, u32[]{:S(2)}, u32[]{:S(2)}) collective-permute-start(bf16[4128,128]{1,0:T(8,128)(2,1)} %copy-done.2), channel_id=1, source_target_pairs={{0,8},{1,9},{2,10},{3,11},{4,12},{5,13},{6,14},{7,15},{8,0},{9,1},... | collective-permute-start | bytes 3170312 | tf_op jit(solution)/shard_map/ppermute | solution.py:57
  56.1 14.6 %collective-permute-start.12 = (bf16[4128,128]{1,0:T(8,128)(2,1)}, bf16[4128,128]{1,0:T(8,128)(2,1)S(1)}, u32[]{:S(2)}, u32[]{:S(2)}) collective-permute-start(bf16[4128,128]{1,0:T(8,128)(2,1)} %collective-permute-done.2.rest_8_), channel_id=1, source_target_pairs={{0,8},{1,9},{2,10},{3,11},{4,12},{5,13},{6,14},{7,15},{8,0},{9,1},... | collective-permute-start | bytes 3170312 | tf_op jit(solution)/shard_map/ppermute | solution.py:57
  57.6 16.8 %copy-start.1 = (bf16[2,1024,128]{2,1,0:T(8,128)(2,1)S(1)}, bf16[2,1024,128]{2,1,0:T(8,128)(2,1)}, u32[]{:S(2)}) copy-start(bf16[2,1024,128]{2,1,0:T(8,128)(2,1)} %mix_ref.3) | copy-start | bytes 1572868
  57.6 16.8 %copy-start.3 = (bf16[4128,128]{1,0:T(8,128)(2,1)S(1)}, bf16[4128,128]{1,0:T(8,128)(2,1)}, u32[]{:S(2)}) copy-start(bf16[4128,128]{1,0:T(8,128)(2,1)} %copy-done.2) | copy-start | bytes 3170308
  68.4 4.5 %collective-permute-start.11 = (bf16[4128,128]{1,0:T(8,128)(2,1)S(1)}, bf16[4128,128]{1,0:T(8,128)(2,1)S(1)}, u32[]{:S(2)}, u32[]{:S(2)}) collective-permute-start(bf16[4128,128]{1,0:T(8,128)(2,1)S(1)} %collective-permute-done.8.rest_10_), channel_id=1, source_target_pairs={{0,8},{1,9},{2,10},{3,11},{4,12},{5,13},{6,14},{7,15},{8,0},{9,1},... | collective-permute-start | bytes 3170312 | tf_op jit(solution)/shard_map/ppermute | solution.py:57
  70.6 3.8 %collective-permute-start.13 = (bf16[4128,128]{1,0:T(8,128)(2,1)S(1)}, bf16[4128,128]{1,0:T(8,128)(2,1)S(1)}, u32[]{:S(2)}, u32[]{:S(2)}) collective-permute-start(bf16[4128,128]{1,0:T(8,128)(2,1)S(1)} %collective-permute-done.9.rest_12_), channel_id=1, source_target_pairs={{0,8},{1,9},{2,10},{3,11},{4,12},{5,13},{6,14},{7,15},{8,0},{9,1},... | collective-permute-start | bytes 3170312 | tf_op jit(solution)/shard_map/ppermute | solution.py:57

commit v7 on v6

--- a/solution.py
+++ b/solution.py
@@ -156,16 +156,18 @@
 
 def head_kernel(x_ref, gain_ref, bias_ref, conv_ref, *rest):
     parts = rest[:2 * (EARLY - 1)]
-    x, n, act, w, mine, normed, sems, mine_sem = rest[2 * (EARLY - 1):]
+    x, n, act, w, mine, normed, sems, later_sems, mine_sem = rest[2 * (EARLY - 1):]
     core, homes = place()
     halves = sides(core)
     arriving = [[pltpu.make_async_copy(conv_ref.at[0], mine, mine_sem.at[0])]]
     for k in range(1, EARLY):
         copies = []
         for p in (2 * k - 2, 2 * k - 1):
-            copies.append(pltpu.make_async_copy(parts[p].at[pl.ds(0, PART)], w.at[p], sems.at[p]))
+            copies.append(pltpu.make_async_copy(parts[p].at[pl.ds(0, PART)], w.at[p, pl.ds(0, PART)], sems.at[p]))
         arriving.append(copies)
-    for copies in arriving:
+    rows = pl.ds(PART, (LAYERS - 1) * PART)
+    later = [pltpu.make_async_copy(part.at[rows], w.at[p, rows], later_sems.at[p]) for p, part in enumerate(parts)]
+    for copies in arriving + [later]:
         for copy in copies:
             copy.start()
     for b in range(BLOCKS):
@@ -181,10 +183,12 @@
     for k in range(0, EARLY, 2):
         for copy in arriving[k] + arriving[k + 1]:
             copy.wait()
-        biases = [bias_ref[0] if k == 0 else w[2 * k - 2, 4 * HALF:, :], w[2 * k, 4 * HALF:, :]]
+        biases = [bias_ref[0] if k == 0 else w[2 * k - 2, 4 * HALF:PART, :], w[2 * k, 4 * HALF:PART, :]]
         convolve(n, [column(k), column(k + 1)], biases, act, homes[k:k + 2])
     for k in range(EARLY, SHARDS):
         act[:, home(homes[k])] = jnp.zeros((ROWS, LANES), jnp.bfloat16)
+    for copy in later:
+        copy.wait()
 
 
 def run_head(x, gain, bias, conv, parts):
@@ -196,13 +200,14 @@
             jax.ShapeDtypeStruct((ROWS, C), jnp.float32),
             jax.ShapeDtypeStruct((ROWS, 3 * C), jnp.bfloat16),
             jax.ShapeDtypeStruct((ROWS, C), jnp.bfloat16),
+            jax.ShapeDtypeStruct((len(parts), LAYERS * PART, LANES), jnp.bfloat16),
         ],
         in_specs=[vmem, vmem, vmem] + [anywhere] * (1 + len(parts)),
-        out_specs=[vmem] * 3,
+        out_specs=[vmem] * 4,
         scratch_shapes=[
-            pltpu.VMEM((len(parts), PART, LANES), jnp.bfloat16),
             pltpu.VMEM((3, C, LANES), jnp.bfloat16),
             pltpu.VMEM((ROWS, C), jnp.float32),
+            pltpu.SemaphoreType.DMA((len(parts),)),
             pltpu.SemaphoreType.DMA((len(parts),)),
             pltpu.SemaphoreType.DMA((1,)),
         ],
@@ -212,9 +217,9 @@
     )(x, gain, bias, conv, *parts)
 
 
-def tail_kernel(x_ref, n_ref, act_ref, gain_ref, bias_ref, conv_ref, mix_ref, *rest):
-    parts = rest[:2 * (SHARDS - 1)]
-    out_ref, w, mine, x, normed, n, act, mixing, sems, late_sems, mine_sems = rest[2 * (SHARDS - 1):]
+def tail_kernel(x_ref, n_ref, act_ref, early_ref, gain_ref, bias_ref, conv_ref, mix_ref, *rest):
+    parts = rest[:2 * (SHARDS - EARLY)]
+    out_ref, w, mine, x, normed, n, act, mixing, sems, late_sems, mine_sems = rest[2 * (SHARDS - EARLY):]
     core, homes = place()
     halves = sides(core)
     order = list(range(EARLY, SHARDS)) + list(range(EARLY))
@@ -225,10 +230,12 @@
                 copies = [pltpu.make_async_copy(mix_ref.at[layer], mine.at[layer, 3], mine_sems.at[layer, 1])]
                 if layer > 0:
                     copies.append(pltpu.make_async_copy(conv_ref.at[layer], mine.at[layer, pl.ds(0, 3)], mine_sems.at[layer, 0]))
+            elif k < EARLY:
+                continue
             else:
-                rows = pl.ds(layer * PART, PART) if layer > 0 or k >= EARLY else pl.ds(3 * HALF, HALF + EXTRA)
+                rows = pl.ds(layer * PART, PART)
                 copies = []
-                for p in (2 * k - 2, 2 * k - 1):
+                for p in (2 * (k - EARLY), 2 * (k - EARLY) + 1):
                     sem = (late_sems if layer > 0 else sems).at[p]
                     copies.append(pltpu.make_async_copy(parts[p].at[rows], w.at[p, rows], sem))
             for copy in copies:
@@ -240,6 +247,9 @@
             for copy in coming.pop((layer, k), []):
                 copy.wait()
 
+    def block(k, i, spot):
+        return early_ref[2 * k - 2 + i, spot, :] if k < EARLY else w[2 * (k - EARLY) + i, spot, :]
+
     x[...] = x_ref[...]
     act[...] = act_ref[...]
     for layer in range(LAYERS):
@@ -249,10 +259,10 @@
             if k == 0:
                 return jnp.concatenate([mine[layer, t, halves[i], :] for i in range(2) for t in range(start, stop)], axis=0)
             spot = slice(base + start * HALF, base + stop * HALF)
-            return jnp.concatenate([w[2 * k - 2 + i, spot, :] for i in range(2)], axis=0)
+            return jnp.concatenate([block(k, i, spot) for i in range(2)], axis=0)
 
         def lines(k):
-            return bias_ref[layer] if k == 0 else w[2 * k - 2, base + 4 * HALF:base + PART, :]
+            return bias_ref[layer] if k == 0 else block(k, 0, slice(base + 4 * HALF, base + PART))
 
         if layer > 0:
             normalize(layer, x, gain_ref, normed, n, halves)
@@ -276,13 +286,13 @@
                     x[:, home(homes[v])] = total.astype(jnp.bfloat16).astype(jnp.float32)
 
 
-def run_tail(x, n, act, gain, bias, conv, mix, parts):
+def run_tail(x, n, act, early, gain, bias, conv, mix, parts):
     vmem = pl.BlockSpec(memory_space=pltpu.VMEM)
     anywhere = pl.BlockSpec(memory_space=pl.ANY)
     return pl.pallas_call(
         tail_kernel,
         out_shape=jax.ShapeDtypeStruct((BLOCKS * SHARDS, RES, LANES), jnp.bfloat16),
-        in_specs=[vmem] * 5 + [anywhere] * (2 + len(parts)),
+        in_specs=[vmem] * 6 + [anywhere] * (2 + len(parts)),
         out_specs=vmem,
         scratch_shapes=[
             pltpu.VMEM((len(parts), LAYERS * PART, LANES), jnp.bfloat16),
@@ -296,10 +306,10 @@
             pltpu.SemaphoreType.DMA((len(parts),)),
             pltpu.SemaphoreType.DMA((LAYERS, 2)),
         ],
-        compiler_params=pltpu.CompilerParams(vmem_limit_bytes=30 * 2**20),
+        compiler_params=pltpu.CompilerParams(vmem_limit_bytes=24 * 2**20),
         cost_estimate=pl.CostEstimate(flops=12 * ROWS * C * C, bytes_accessed=14 * 2**20, transcendentals=ROWS * C),
         name="tail",
-    )(x, n, act, gain, bias, conv, mix, *parts)
+    )(x, n, act, early, gain, bias, conv, mix, *parts)
 
 
 def per_device(tokens, conv_weight, conv_bias, mix_weight, mix_bias, norm_gain):
@@ -317,12 +327,12 @@
     e_y = send(e, Y_SIDE)
     swapped = [send(v, SWAP) for v in (b, a, e)]
     early = [v for pair in zip((a, b, e), swapped) for v in pair]
-    x, n, act = run_head(x, norm_gain, bias, conv_weight, early)
+    x, n, act, kept = run_head(x, norm_gain, bias, conv_weight, early)
     b_y, e_y, act = lax.optimization_barrier((b_y, e_y, act))
     late = (own_y, a_y, b_y, e_y)
     swapped = [send(v, SWAP) for v in (own_y, b_y, a_y, e_y)]
-    parts = early + [v for pair in zip(late, swapped) for v in pair]
-    x = run_tail(x, n, act, norm_gain, bias, conv_weight, mix_weight, parts)
+    parts = [v for pair in zip(late, swapped) for v in pair]
+    x = run_tail(x, n, act, kept, norm_gain, bias, conv_weight, mix_weight, parts)
     y = lax.all_to_all(x, AXES, split_axis=0, concat_axis=0, tiled=True)
     return y.reshape(128 * RES, LANES)[:tokens.shape[0]]
 

time: 111 us -> 111 us (level)
  Pallas kernels: 20.8 us -> 19 us
  blocking collectives: 22 us -> 23.3 us
    pallas_call x1, Pallas kernels: 13.6 us -> 11.3 us  [run_tail(): pl.pallas_call(tail_kernel, out_shape=jax.ShapeDtypeStruct((BLOCKS * SHAR...]
    all_to_all x1, blocking collectives: 22 us -> 23.3 us  [per_device(): y = lax.all_to_all(x, AXES, split_axis=0, concat_axis=0, tiled=True)]
    all_to_all x1, waiting for transfers between devices: 16.3 us -> 17.5 us  [per_device(): lax.all_to_all(padded.reshape(128, RES, LANES), AXES, split_axis=0, conca...]
  transfers between devices with their start and end apart: 15 -> 15, of which waited for: 9 -> 8; matrix products, arithmetic and copies ran while one was open for 1% -> 1% of each run, Pallas kernels for 3% -> 4%
where the time goes in v7:
time: 111 us; the launch traced here: 110 us
  waiting for transfers between devices  41.1 us (37%)
  starting transfers between devices  25.2 us (23%)
  blocking collectives  23.3 us (21%)
  Pallas kernels  19 us (17%)
  local copies, waits for them, and re-layouts  1.89 us (2%)
    ppermute x14, waiting for transfers between devices, send(): return lax.ppermute(block, AXES, path)  23.6 us
    all_to_all x1, blocking collectives, per_device(): y = lax.all_to_all(x, AXES, split_axis=0, concat_axis=0, tiled=True)  23.3 us
    ppermute x14, starting transfers between devices, send(): return lax.ppermute(block, AXES, path)  18.6 us
    all_to_all x1, waiting for transfers between devices, per_device(): lax.all_to_all(padded.reshape(128, RES, LANES), AXES, split_axis=0, conca...  17.5 us
    pallas_call x1, Pallas kernels, run_tail(): pl.pallas_call(tail_kernel, out_shape=jax.ShapeDtypeStruct((BLOCKS * SHAR...  11.3 us
    all_to_all x1, starting transfers between devices, per_device(): lax.all_to_all(padded.reshape(128, RES, LANES), AXES, split_axis=0, conca...  6.62 us
    pallas_call x1, Pallas kernels, run_head(): pl.pallas_call(head_kernel, out_shape=[jax.ShapeDtypeStruct((ROWS, C), jn...  4.18 us
    pallas_call x1, Pallas kernels, prepare(): pl.pallas_call(prepare_kernel, out_shape=[jax.ShapeDtypeStruct((LAYERS *...  3.5 us
  transfers between devices with their start and end apart: 15, of which 8 were waited for; matrix products, arithmetic and copies ran while one was open for 1% of the time, Pallas kernels for 4%

profile of v7, /device:TPU:1, one launch (start us, length us, event | category | flops | bytes accessed | tf_op | source)
XLA Modules:
  0.0 110.5 jit_solution(13942497059128232987)
XLA Ops:
  0.0 0.0 copy-start.4
  0.0 3.5 %prepare.1 = (bf16[4128,128]{1,0:T(8,128)(2,1)}, bf16[2,16,128]{2,1,0:T(8,128)(2,1)}) custom-call(bf16[2,3,1024,128]{3,2,1,0:T(8,128)(2,1)} %conv_ref.5, bf16[2,1024,128]{2,1,0:T(8,128)(2,1)} %mix_ref.3, f32[2,128]{1,0:T(2,128)} %conv_bias_ref.1, f32[2,128]{1,0:T(2,128)} %mix_bias_ref.1), custom_call_target="tpu_custom_call" | custom-call | bytes 4194304 | tf_op jit(solution)/shard_map/prepare/pallas_call | solution.py:101
  3.5 4.7 %collective-permute-start = (bf16[4128,128]{1,0:T(8,128)(2,1)}, bf16[4128,128]{1,0:T(8,128)(2,1)}, u32[]{:S(2)}, u32[]{:S(2)}) collective-permute-start(bf16[4128,128]{1,0:T(8,128)(2,1)} %get-tuple-element.21), channel_id=1, source_target_pairs={{0,1},{1,2},{2,3},{3,0},{4,5},{5,6},{6,7},{7,4},{8,11},{9,8},{10,9... | collective-permute-start | bytes 3170312 | tf_op jit(solution)/shard_map/ppermute | solution.py:57
  8.2 2.7 %collective-permute-start.1 = (bf16[4128,128]{1,0:T(8,128)(2,1)}, bf16[4128,128]{1,0:T(8,128)(2,1)S(1)}, u32[]{:S(2)}, u32[]{:S(2)}) collective-permute-start(bf16[4128,128]{1,0:T(8,128)(2,1)} %get-tuple-element.21), channel_id=1, source_target_pairs={{0,4},{1,5},{2,6},{3,7},{4,16},{5,17},{6,18},{7,19},{8,28},{9,29},... | collective-permute-start | bytes 3170312 | tf_op jit(solution)/shard_map/ppermute | solution.py:57
  10.9 0.0 copy-done.4
  10.9 0.0 copy-start.2
  10.9 0.0 copy-start.3
  10.9 0.9 pad.4
  11.9 0.0 copy-start
  11.9 8.5 %collective-permute-done.rest_0_ = bf16[4128,128]{1,0:T(8,128)(2,1)} collective-permute-done((bf16[4128,128]{1,0:T(8,128)(2,1)}, bf16[4128,128]{1,0:T(8,128)(2,1)}, u32[]{:S(2)}, u32[]{:S(2)}) %collective-permute-start) | collective-permute-done | bytes 1056800 | tf_op jit(solution)/shard_map/ppermute | solution.py:57
  20.3 2.7 %collective-permute-done.1.rest_0_ = bf16[4128,128]{1,0:T(8,128)(2,1)S(1)} collective-permute-done((bf16[4128,128]{1,0:T(8,128)(2,1)}, bf16[4128,128]{1,0:T(8,128)(2,1)S(1)}, u32[]{:S(2)}, u32[]{:S(2)}) %collective-permute-start.1) | collective-permute-done | bytes 1056800 | tf_op jit(solution)/shard_map/ppermute | solution.py:57
  23.0 3.0 %collective-permute-start.2 = (bf16[4128,128]{1,0:T(8,128)(2,1)}, bf16[4128,128]{1,0:T(8,128)(2,1)}, u32[]{:S(2)}, u32[]{:S(2)}) collective-permute-start(bf16[4128,128]{1,0:T(8,128)(2,1)} %collective-permute-done.rest_0_), channel_id=1, source_target_pairs={{0,4},{1,5},{2,6},{3,7},{4,16},{5,17},{6,18},{7,19},{8,28},{9,29},... | collective-permute-start | bytes 3170312 | tf_op jit(solution)/shard_map/ppermute | solution.py:57
  26.1 0.1 collective-permute-start.3
  26.2 1.9 %collective-permute-start.4 = (bf16[4128,128]{1,0:T(8,128)(2,1)}, bf16[4128,128]{1,0:T(8,128)(2,1)}, u32[]{:S(2)}, u32[]{:S(2)}) collective-permute-start(bf16[4128,128]{1,0:T(8,128)(2,1)} %collective-permute-done.rest_0_), channel_id=1, source_target_pairs={{0,32},{1,33},{2,34},{3,35},{4,36},{5,37},{6,38},{7,39},{8,104},{9... | collective-permute-start | bytes 3170312 | tf_op jit(solution)/shard_map/ppermute | solution.py:57
  28.1 6.6 %all-to-all-start = ((bf16[128,24,128]{2,1,0:T(8,128)(2,1)}), bf16[128,24,128]{2,1,0:T(8,128)(2,1)S(1)}, u32[]{:S(2)}, u32[]{:S(2)}) async-start(bf16[128,24,128]{2,1,0:T(8,128)(2,1)} %bitcast.2), calls=%async_computation | async-start | bytes 1572864 | tf_op jit(solution)/shard_map/all_to_all | solution.py:321
  34.7 1.1 %collective-permute-start.6 = (bf16[4128,128]{1,0:T(8,128)(2,1)}, bf16[4128,128]{1,0:T(8,128)(2,1)}, u32[]{:S(2)}, u32[]{:S(2)}) collective-permute-start(bf16[4128,128]{1,0:T(8,128)(2,1)} %collective-permute-done.rest_0_), channel_id=1, source_target_pairs={{0,8},{1,9},{2,10},{3,11},{4,12},{5,13},{6,14},{7,15},{8,0},{9,1},... | collective-permute-start | bytes 3170312 | tf_op jit(solution)/shard_map/ppermute | solution.py:57
  35.8 17.5 %all-to-all-done.x_ref = bf16[128,24,128]{2,1,0:T(8,128)(2,1)S(1)} async-done(((bf16[128,24,128]{2,1,0:T(8,128)(2,1)}), bf16[128,24,128]{2,1,0:T(8,128)(2,1)S(1)}, u32[]{:S(2)}, u32[]{:S(2)}) %all-to-all-start) | async-done | bytes 786464 | tf_op jit(solution)/shard_map/all_to_all | solution.py:321
  53.3 0.0 collective-permute-done.2.rest_2_
  53.3 0.0 collective-permute-done.3.rest_4_
  53.3 0.0 collective-permute-done.4.rest_2_
  53.4 0.4 collective-permute-start.7
  53.7 0.2 collective-permute-start.5
  53.9 1.5 %collective-permute-start.8 = (bf16[4128,128]{1,0:T(8,128)(2,1)}, bf16[4128,128]{1,0:T(8,128)(2,1)S(1)}, u32[]{:S(2)}, u32[]{:S(2)}) collective-permute-start(bf16[4128,128]{1,0:T(8,128)(2,1)} %collective-permute-done.2.rest_2_), channel_id=1, source_target_pairs={{0,32},{1,33},{2,34},{3,35},{4,36},{5,37},{6,38},{7,39},{8,104},{9... | collective-permute-start | bytes 3170312 | tf_op jit(solution)/shard_map/ppermute | solution.py:57
  55.4 0.9 collective-permute-start.9
  56.4 0.0 collective-permute-done.6.rest_3_
  56.4 0.0 collective-permute-start.10
  56.4 0.0 collective-permute-done.7.rest_5_
  56.4 0.5 collective-permute-start.12
  56.9 0.9 collective-permute-done.5.rest_1_
  57.8 0.0 copy-done.2
  57.8 0.0 copy-done.3
  57.8 0.0 copy-done
  57.8 0.0 copy-start.1
  57.9 4.2 %head.1 = (f32[384,1024]{1,0:T(8,128)S(1)}, bf16[384,3072]{1,0:T(8,128)(2,1)S(1)}, bf16[384,1024]{1,0:T(8,128)(2,1)S(1)}, bf16[6,4128,128]{2,1,0:T(8,128)(2,1)S(1)}) custom-call(bf16[128,24,128]{2,1,0:T(8,128)(2,1)S(1)} %all-to-all-done.x_ref, f32[2,1024]{1,0:T(2,128)S(1)} %copy-done.2, bf16[2,16,128]{2,1,0:T(8,128)(2,1)S(1)} %copy-done.3, ...), custom_call_target="tpu_custom_call" | custom-call | flops 1610612736 | bytes 9437184 | tf_op jit(solution)/shard_map/head/pallas_call | solution.py:197
  62.0 6.1 %collective-permute-done.8.rest_4_ = bf16[4128,128]{1,0:T(8,128)(2,1)S(1)} collective-permute-done((bf16[4128,128]{1,0:T(8,128)(2,1)}, bf16[4128,128]{1,0:T(8,128)(2,1)S(1)}, u32[]{:S(2)}, u32[]{:S(2)}) %collective-permute-start.8) | collective-permute-done | bytes 1056800 | tf_op jit(solution)/shard_map/ppermute | solution.py:57
  68.2 1.5 %collective-permute-done.9.rest_6_ = bf16[4128,128]{1,0:T(8,128)(2,1)S(1)} collective-permute-done((bf16[4128,128]{1,0:T(8,128)(2,1)}, bf16[4128,128]{1,0:T(8,128)(2,1)S(1)}, u32[]{:S(2)}, u32[]{:S(2)}) %collective-permute-start.9) | collective-permute-done | bytes 1056800 | tf_op jit(solution)/shard_map/ppermute | solution.py:57
  69.7 1.5 %collective-permute-start.11 = (bf16[4128,128]{1,0:T(8,128)(2,1)S(1)}, bf16[4128,128]{1,0:T(8,128)(2,1)S(1)}, u32[]{:S(2)}, u32[]{:S(2)}) collective-permute-start(bf16[4128,128]{1,0:T(8,128)(2,1)S(1)} %collective-permute-done.8.rest_4_), channel_id=1, source_target_pairs={{0,8},{1,9},{2,10},{3,11},{4,12},{5,13},{6,14},{7,15},{8,0},{9,1},... | collective-permute-start | bytes 3170312 | tf_op jit(solution)/shard_map/ppermute | solution.py:57
  71.2 0.0 collective-permute-start.13
  71.2 0.0 collective-permute-done.10.rest_1_
  71.2 0.0 collective-permute-done.12.rest_5_
  71.2 2.3 %collective-permute-done.11.rest_3_ = bf16[4128,128]{1,0:T(8,128)(2,1)S(1)} collective-permute-done((bf16[4128,128]{1,0:T(8,128)(2,1)S(1)}, bf16[4128,128]{1,0:T(8,128)(2,1)S(1)}, u32[]{:S(2)}, u32[]{:S(2)}) %collective-permute-start.11) | collective-permute-done | bytes 1056800 | tf_op jit(solution)/shard_map/ppermute | solution.py:57
  73.5 1.5 %collective-permute-done.13.rest_7_ = bf16[4128,128]{1,0:T(8,128)(2,1)S(1)} collective-permute-done((bf16[4128,128]{1,0:T(8,128)(2,1)S(1)}, bf16[4128,128]{1,0:T(8,128)(2,1)S(1)}, u32[]{:S(2)}, u32[]{:S(2)}) %collective-permute-start.13) | collective-permute-done | bytes 1056800 | tf_op jit(solution)/shard_map/ppermute | solution.py:57
  75.0 0.0 copy-done.1
  75.0 11.3 %tail.1 = bf16[128,24,128]{2,1,0:T(8,128)(2,1)S(1)} custom-call(f32[384,1024]{1,0:T(8,128)S(1)} %get-tuple-element.28.x_ref, bf16[384,3072]{1,0:T(8,128)(2,1)S(1)} %get-tuple-element.29.n_ref, bf16[384,1024]{1,0:T(8,128)(2,1)S(1)} %get-tuple-element.32.act_ref, bf16[6,4128,128]{2,1,0:T(8,128)(2,1)S(1)} %get-tuple-element.33.early_ref, ...), custom_call_target="tpu_custom_call" | custom-call | flops 4831838208 | bytes 14680064 | tf_op jit(solution)/shard_map/tail/pallas_call | solution.py:292
  86.3 23.3 %all_to_all.10 = bf16[128,24,128]{2,1,0:T(8,128)(2,1)S(1)} all-to-all(bf16[128,24,128]{2,1,0:T(8,128)(2,1)S(1)} %tail.1), channel_id=1, replica_groups=mesh['seq'=16,'filt'=8] {'seq','filt'}, dimensions={0} | all-to-all | bytes 1572864 | tf_op jit(solution)/shard_map/all_to_all | solution.py:336
  109.6 0.9 slice.8
Async XLA Ops:
  0.0 10.9 %copy-start.4 = (bf16[2688,128]{1,0:T(8,128)(2,1)S(1)}, bf16[2688,128]{1,0:T(8,128)(2,1)}, u32[]{:S(2)}) copy-start(bf16[2688,128]{1,0:T(8,128)(2,1)} %param.6) | copy-start | bytes 2064388
  3.5 16.8 %collective-permute-start = (bf16[4128,128]{1,0:T(8,128)(2,1)}, bf16[4128,128]{1,0:T(8,128)(2,1)}, u32[]{:S(2)}, u32[]{:S(2)}) collective-permute-start(bf16[4128,128]{1,0:T(8,128)(2,1)} %get-tuple-element.21), channel_id=1, source_target_pairs={{0,1},{1,2},{2,3},{3,0},{4,5},{5,6},{6,7},{7,4},{8,11},{9,8},{10,9... | collective-permute-start | bytes 3170312 | tf_op jit(solution)/shard_map/ppermute | solution.py:57
  8.2 14.9 %collective-permute-start.1 = (bf16[4128,128]{1,0:T(8,128)(2,1)}, bf16[4128,128]{1,0:T(8,128)(2,1)S(1)}, u32[]{:S(2)}, u32[]{:S(2)}) collective-permute-start(bf16[4128,128]{1,0:T(8,128)(2,1)} %get-tuple-element.21), channel_id=1, source_target_pairs={{0,4},{1,5},{2,6},{3,7},{4,16},{5,17},{6,18},{7,19},{8,28},{9,29},... | collective-permute-start | bytes 3170312 | tf_op jit(solution)/shard_map/ppermute | solution.py:57
  10.9 46.9 %copy-start.2 = (f32[2,1024]{1,0:T(2,128)S(1)}, f32[2,1024]{1,0:T(2,128)}, u32[]{:S(2)}) copy-start(f32[2,1024]{1,0:T(2,128)} %gain_ref.3) | copy-start | bytes 24580
  10.9 46.9 %copy-start.3 = (bf16[2,16,128]{2,1,0:T(8,128)(2,1)S(1)}, bf16[2,16,128]{2,1,0:T(8,128)(2,1)}, u32[]{:S(2)}) copy-start(bf16[2,16,128]{2,1,0:T(8,128)(2,1)} %get-tuple-element.25.bias_ref) | copy-start | bytes 24580
  11.9 46.0 %copy-start = (bf16[2,3,1024,128]{3,2,1,0:T(8,128)(2,1)S(1)}, bf16[2,3,1024,128]{3,2,1,0:T(8,128)(2,1)}, u32[]{:S(2)}) copy-start(bf16[2,3,1024,128]{3,2,1,0:T(8,128)(2,1)} %conv_ref.5) | copy-start | bytes 4718596
  23.0 30.3 %collective-permute-start.2 = (bf16[4128,128]{1,0:T(8,128)(2,1)}, bf16[4128,128]{1,0:T(8,128)(2,1)}, u32[]{:S(2)}, u32[]{:S(2)}) collective-permute-start(bf16[4128,128]{1,0:T(8,128)(2,1)} %collective-permute-done.rest_0_), channel_id=1, source_target_pairs={{0,4},{1,5},{2,6},{3,7},{4,16},{5,17},{6,18},{7,19},{8,28},{9,29},... | collective-permute-start | bytes 3170312 | tf_op jit(solution)/shard_map/ppermute | solution.py:57
  26.1 27.3 %collective-permute-start.3 = (bf16[4128,128]{1,0:T(8,128)(2,1)}, bf16[4128,128]{1,0:T(8,128)(2,1)}, u32[]{:S(2)}, u32[]{:S(2)}) collective-permute-start(bf16[4128,128]{1,0:T(8,128)(2,1)} %collective-permute-done.rest_0_), channel_id=1, source_target_pairs={{0,1},{1,2},{2,3},{3,0},{4,5},{5,6},{6,7},{7,4},{8,11},{9,8},{10,9... | collective-permute-start | bytes 3170312 | tf_op jit(solution)/shard_map/ppermute | solution.py:57
  26.2 27.2 %collective-permute-start.4 = (bf16[4128,128]{1,0:T(8,128)(2,1)}, bf16[4128,128]{1,0:T(8,128)(2,1)}, u32[]{:S(2)}, u32[]{:S(2)}) collective-permute-start(bf16[4128,128]{1,0:T(8,128)(2,1)} %collective-permute-done.rest_0_), channel_id=1, source_target_pairs={{0,32},{1,33},{2,34},{3,35},{4,36},{5,37},{6,38},{7,39},{8,104},{9... | collective-permute-start | bytes 3170312 | tf_op jit(solution)/shard_map/ppermute | solution.py:57
  28.1 25.3 %all-to-all-start = ((bf16[128,24,128]{2,1,0:T(8,128)(2,1)}), bf16[128,24,128]{2,1,0:T(8,128)(2,1)S(1)}, u32[]{:S(2)}, u32[]{:S(2)}) async-start(bf16[128,24,128]{2,1,0:T(8,128)(2,1)} %bitcast.2), calls=%async_computation | async-start | bytes 1572864 | tf_op jit(solution)/shard_map/all_to_all | solution.py:321
  34.7 21.7 %collective-permute-start.6 = (bf16[4128,128]{1,0:T(8,128)(2,1)}, bf16[4128,128]{1,0:T(8,128)(2,1)}, u32[]{:S(2)}, u32[]{:S(2)}) collective-permute-start(bf16[4128,128]{1,0:T(8,128)(2,1)} %collective-permute-done.rest_0_), channel_id=1, source_target_pairs={{0,8},{1,9},{2,10},{3,11},{4,12},{5,13},{6,14},{7,15},{8,0},{9,1},... | collective-permute-start | bytes 3170312 | tf_op jit(solution)/shard_map/ppermute | solution.py:57
  53.4 3.0 %collective-permute-start.7 = (bf16[4128,128]{1,0:T(8,128)(2,1)}, bf16[4128,128]{1,0:T(8,128)(2,1)S(1)}, u32[]{:S(2)}, u32[]{:S(2)}) collective-permute-start(bf16[4128,128]{1,0:T(8,128)(2,1)} %collective-permute-done.3.rest_4_), channel_id=1, source_target_pairs={{0,8},{1,9},{2,10},{3,11},{4,12},{5,13},{6,14},{7,15},{8,0},{9,1},... | collective-permute-start | bytes 3170312 | tf_op jit(solution)/shard_map/ppermute | solution.py:57
  53.7 4.1 %collective-permute-start.5 = (bf16[4128,128]{1,0:T(8,128)(2,1)}, bf16[4128,128]{1,0:T(8,128)(2,1)S(1)}, u32[]{:S(2)}, u32[]{:S(2)}) collective-permute-start(bf16[4128,128]{1,0:T(8,128)(2,1)} %collective-permute-done.4.rest_2_), channel_id=1, source_target_pairs={{0,8},{1,9},{2,10},{3,11},{4,12},{5,13},{6,14},{7,15},{8,0},{9,1},... | collective-permute-start | bytes 3170312 | tf_op jit(solution)/shard_map/ppermute | solution.py:57
  53.9 14.2 %collective-permute-start.8 = (bf16[4128,128]{1,0:T(8,128)(2,1)}, bf16[4128,128]{1,0:T(8,128)(2,1)S(1)}, u32[]{:S(2)}, u32[]{:S(2)}) collective-permute-start(bf16[4128,128]{1,0:T(8,128)(2,1)} %collective-permute-done.2.rest_2_), channel_id=1, source_target_pairs={{0,32},{1,33},{2,34},{3,35},{4,36},{5,37},{6,38},{7,39},{8,104},{9... | collective-permute-start | bytes 3170312 | tf_op jit(solution)/shard_map/ppermute | solution.py:57
  55.4 14.2 %collective-permute-start.9 = (bf16[4128,128]{1,0:T(8,128)(2,1)}, bf16[4128,128]{1,0:T(8,128)(2,1)S(1)}, u32[]{:S(2)}, u32[]{:S(2)}) collective-permute-start(bf16[4128,128]{1,0:T(8,128)(2,1)} %collective-permute-done.3.rest_4_), channel_id=1, source_target_pairs={{0,4},{1,5},{2,6},{3,7},{4,16},{5,17},{6,18},{7,19},{8,28},{9,29},... | collective-permute-start | bytes 3170312 | tf_op jit(solution)/shard_map/ppermute | solution.py:57
  56.4 14.8 %collective-permute-start.10 = (bf16[4128,128]{1,0:T(8,128)(2,1)S(1)}, bf16[4128,128]{1,0:T(8,128)(2,1)S(1)}, u32[]{:S(2)}, u32[]{:S(2)}) collective-permute-start(bf16[4128,128]{1,0:T(8,128)(2,1)S(1)} %collective-permute-done.1.rest_0_), channel_id=1, source_target_pairs={{0,8},{1,9},{2,10},{3,11},{4,12},{5,13},{6,14},{7,15},{8,0},{9,1},... | collective-permute-start | bytes 3170312 | tf_op jit(solution)/shard_map/ppermute | solution.py:57
  56.4 14.8 %collective-permute-start.12 = (bf16[4128,128]{1,0:T(8,128)(2,1)}, bf16[4128,128]{1,0:T(8,128)(2,1)S(1)}, u32[]{:S(2)}, u32[]{:S(2)}) collective-permute-start(bf16[4128,128]{1,0:T(8,128)(2,1)} %collective-permute-done.2.rest_2_), channel_id=1, source_target_pairs={{0,8},{1,9},{2,10},{3,11},{4,12},{5,13},{6,14},{7,15},{8,0},{9,1},... | collective-permute-start | bytes 3170312 | tf_op jit(solution)/shard_map/ppermute | solution.py:57
  57.8 17.2 %copy-start.1 = (bf16[2,1024,128]{2,1,0:T(8,128)(2,1)S(1)}, bf16[2,1024,128]{2,1,0:T(8,128)(2,1)}, u32[]{:S(2)}) copy-start(bf16[2,1024,128]{2,1,0:T(8,128)(2,1)} %mix_ref.3) | copy-start | bytes 1572868
  69.7 3.8 %collective-permute-start.11 = (bf16[4128,128]{1,0:T(8,128)(2,1)S(1)}, bf16[4128,128]{1,0:T(8,128)(2,1)S(1)}, u32[]{:S(2)}, u32[]{:S(2)}) collective-permute-start(bf16[4128,128]{1,0:T(8,128)(2,1)S(1)} %collective-permute-done.8.rest_4_), channel_id=1, source_target_pairs={{0,8},{1,9},{2,10},{3,11},{4,12},{5,13},{6,14},{7,15},{8,0},{9,1},... | collective-permute-start | bytes 3170312 | tf_op jit(solution)/shard_map/ppermute | solution.py:57
  71.2 3.8 %collective-permute-start.13 = (bf16[4128,128]{1,0:T(8,128)(2,1)S(1)}, bf16[4128,128]{1,0:T(8,128)(2,1)S(1)}, u32[]{:S(2)}, u32[]{:S(2)}) collective-permute-start(bf16[4128,128]{1,0:T(8,128)(2,1)S(1)} %collective-permute-done.9.rest_6_), channel_id=1, source_target_pairs={{0,8},{1,9},{2,10},{3,11},{4,12},{5,13},{6,14},{7,15},{8,0},{9,1},... | collective-permute-start | bytes 3170312 | tf_op jit(solution)/shard_map/ppermute | solution.py:57

commit v8 on v7

--- a/solution.py
+++ b/solution.py
@@ -317,12 +317,12 @@
     a = send(own, Z_SIDE)
     own_y = send(own, Y_SIDE)
     padded = jnp.pad(tokens, ((0, 128 * RES - tokens.shape[0]), (0, 0)))
-    a, own_y, padded = lax.optimization_barrier((a, own_y, padded))
     x = lax.all_to_all(padded.reshape(128, RES, LANES), AXES, split_axis=0, concat_axis=0, tiled=True)
+    a, own_y, x = lax.optimization_barrier((a, own_y, x))
     b = send(a, X_SIDE)
     e = send(a, Z_SIDE)
     a_y = send(a, Y_SIDE)
-    a_y, e, b, x = lax.optimization_barrier((a_y, e, b, x))
+    a_y, e, b = lax.optimization_barrier((a_y, e, b))
     b_y = send(a_y, X_SIDE)
     e_y = send(e, Y_SIDE)
     swapped = [send(v, SWAP) for v in (b, a, e)]

time: 111 us -> 109 us (0.982)
  blocking collectives: 23.3 us -> 46.8 us
  waiting for transfers between devices: 41.1 us -> 22.5 us
  starting transfers between devices: 25.2 us -> 19.9 us
    all_to_all x0 -> x1, blocking collectives: none -> 24.3 us  [per_device(): lax.all_to_all(padded.reshape(128, RES, LANES), AXES, split_axis=0, conca...]
    all_to_all x1 -> x0, waiting for transfers between devices: 17.5 us -> none  [per_device(): lax.all_to_all(padded.reshape(128, RES, LANES), AXES, split_axis=0, conca...]
    all_to_all x1 -> x0, starting transfers between devices: 6.62 us -> none  [per_device(): lax.all_to_all(padded.reshape(128, RES, LANES), AXES, split_axis=0, conca...]
    ppermute x14, starting transfers between devices: 18.6 us -> 19.9 us  [send(): return lax.ppermute(block, AXES, path)]
    ppermute x14, waiting for transfers between devices: 23.6 us -> 22.5 us  [send(): return lax.ppermute(block, AXES, path)]
  transfers between devices with their start and end apart: 15 -> 14, of which waited for: 8 -> 7; matrix products, arithmetic and copies ran while one was open for 1% -> 0% of each run, Pallas kernels for 4% -> 4%
where the time goes in v8:
time: 109 us
  blocking collectives  46.8 us (43%)
  waiting for transfers between devices  22.5 us (21%)
  starting transfers between devices  19.9 us (18%)
  Pallas kernels  18.7 us (17%)
    all_to_all x1, blocking collectives, per_device(): lax.all_to_all(padded.reshape(128, RES, LANES), AXES, split_axis=0, conca...  24.3 us
    all_to_all x1, blocking collectives, per_device(): y = lax.all_to_all(x, AXES, split_axis=0, concat_axis=0, tiled=True)  22.5 us
    ppermute x14, waiting for transfers between devices, send(): return lax.ppermute(block, AXES, path)  22.5 us
    ppermute x14, starting transfers between devices, send(): return lax.ppermute(block, AXES, path)  19.9 us
    pallas_call x1, Pallas kernels, run_tail(): pl.pallas_call(tail_kernel, out_shape=jax.ShapeDtypeStruct((BLOCKS * SHAR...  11.1 us
    pallas_call x1, Pallas kernels, run_head(): pl.pallas_call(head_kernel, out_shape=[jax.ShapeDtypeStruct((ROWS, C), jn...  4.12 us
    pallas_call x1, Pallas kernels, prepare(): pl.pallas_call(prepare_kernel, out_shape=[jax.ShapeDtypeStruct((LAYERS *...  3.49 us
  transfers between devices with their start and end apart: 14, of which 7 were waited for; matrix products, arithmetic and copies ran while one was open for 0% of the time, Pallas kernels for 4%

profile of v8, /device:TPU:1, one launch (start us, length us, event | category | flops | bytes accessed | tf_op | source)
XLA Modules:
  0.0 109.0 jit_solution(17121796079187659719)
XLA Ops:
  0.0 0.0 copy-start.4
  0.0 3.5 %prepare.1 = (bf16[4128,128]{1,0:T(8,128)(2,1)}, bf16[2,16,128]{2,1,0:T(8,128)(2,1)}) custom-call(bf16[2,3,1024,128]{3,2,1,0:T(8,128)(2,1)} %conv_ref.5, bf16[2,1024,128]{2,1,0:T(8,128)(2,1)} %mix_ref.3, f32[2,128]{1,0:T(2,128)} %conv_bias_ref.1, f32[2,128]{1,0:T(2,128)} %mix_bias_ref.1), custom_call_target="tpu_custom_call" | custom-call | bytes 4194304 | tf_op jit(solution)/shard_map/prepare/pallas_call | solution.py:101
  3.5 4.7 %collective-permute-start = (bf16[4128,128]{1,0:T(8,128)(2,1)}, bf16[4128,128]{1,0:T(8,128)(2,1)S(1)}, u32[]{:S(2)}, u32[]{:S(2)}) collective-permute-start(bf16[4128,128]{1,0:T(8,128)(2,1)} %get-tuple-element.20), channel_id=1, source_target_pairs={{0,1},{1,2},{2,3},{3,0},{4,5},{5,6},{6,7},{7,4},{8,11},{9,8},{10,9... | collective-permute-start | bytes 3170312 | tf_op jit(solution)/shard_map/ppermute | solution.py:57
  8.2 2.7 %collective-permute-start.1 = (bf16[4128,128]{1,0:T(8,128)(2,1)}, bf16[4128,128]{1,0:T(8,128)(2,1)S(1)}, u32[]{:S(2)}, u32[]{:S(2)}) collective-permute-start(bf16[4128,128]{1,0:T(8,128)(2,1)} %get-tuple-element.20), channel_id=1, source_target_pairs={{0,4},{1,5},{2,6},{3,7},{4,16},{5,17},{6,18},{7,19},{8,28},{9,29},... | collective-permute-start | bytes 3170312 | tf_op jit(solution)/shard_map/ppermute | solution.py:57
  10.9 0.0 copy-done.4
  10.9 0.0 copy-start.2
  10.9 0.0 copy-start.3
  10.9 0.1 pad.4
  11.0 0.0 copy-start
  11.0 24.3 %all_to_all.10.x_ref = bf16[128,24,128]{2,1,0:T(8,128)(2,1)S(1)} all-to-all(bf16[128,24,128]{2,1,0:T(8,128)(2,1)S(1)} %bitcast.2), channel_id=1, replica_groups=mesh['seq'=16,'filt'=8] {'seq','filt'}, dimensions={0} | all-to-all | bytes 1572864 | tf_op jit(solution)/shard_map/all_to_all | solution.py:320
  35.2 0.0 collective-permute-done.rest_0_
  35.2 0.0 collective-permute-done.1.rest_0_
  35.2 0.0 collective-permute-start.2
  35.2 1.4 %collective-permute-start.3 = (bf16[4128,128]{1,0:T(8,128)(2,1)S(1)}, bf16[4128,128]{1,0:T(8,128)(2,1)S(1)}, u32[]{:S(2)}, u32[]{:S(2)}) collective-permute-start(bf16[4128,128]{1,0:T(8,128)(2,1)S(1)} %collective-permute-done.rest_0_), channel_id=1, source_target_pairs={{0,1},{1,2},{2,3},{3,0},{4,5},{5,6},{6,7},{7,4},{8,11},{9,8},{10,9... | collective-permute-start | bytes 3170312 | tf_op jit(solution)/shard_map/ppermute | solution.py:57
  36.6 1.5 %collective-permute-start.4 = (bf16[4128,128]{1,0:T(8,128)(2,1)S(1)}, bf16[4128,128]{1,0:T(8,128)(2,1)S(1)}, u32[]{:S(2)}, u32[]{:S(2)}) collective-permute-start(bf16[4128,128]{1,0:T(8,128)(2,1)S(1)} %collective-permute-done.rest_0_), channel_id=1, source_target_pairs={{0,32},{1,33},{2,34},{3,35},{4,36},{5,37},{6,38},{7,39},{8,104},{9... | collective-permute-start | bytes 3170312 | tf_op jit(solution)/shard_map/ppermute | solution.py:57
  38.1 1.1 collective-permute-start.6
  39.1 10.1 %collective-permute-done.2.rest_2_ = bf16[4128,128]{1,0:T(8,128)(2,1)S(1)} collective-permute-done((bf16[4128,128]{1,0:T(8,128)(2,1)S(1)}, bf16[4128,128]{1,0:T(8,128)(2,1)S(1)}, u32[]{:S(2)}, u32[]{:S(2)}) %collective-permute-start.2) | collective-permute-done | bytes 1056800 | tf_op jit(solution)/shard_map/ppermute | solution.py:57
  49.3 0.1 collective-permute-done.3.rest_4_
  49.4 1.3 %collective-permute-done.4.rest_2_ = bf16[4128,128]{1,0:T(8,128)(2,1)S(1)} collective-permute-done((bf16[4128,128]{1,0:T(8,128)(2,1)S(1)}, bf16[4128,128]{1,0:T(8,128)(2,1)S(1)}, u32[]{:S(2)}, u32[]{:S(2)}) %collective-permute-start.4) | collective-permute-done | bytes 1056800 | tf_op jit(solution)/shard_map/ppermute | solution.py:57
  50.7 2.6 %collective-permute-start.7 = (bf16[4128,128]{1,0:T(8,128)(2,1)S(1)}, bf16[4128,128]{1,0:T(8,128)(2,1)S(1)}, u32[]{:S(2)}, u32[]{:S(2)}) collective-permute-start(bf16[4128,128]{1,0:T(8,128)(2,1)S(1)} %collective-permute-done.3.rest_4_), channel_id=1, source_target_pairs={{0,8},{1,9},{2,10},{3,11},{4,12},{5,13},{6,14},{7,15},{8,0},{9,1},... | collective-permute-start | bytes 3170312 | tf_op jit(solution)/shard_map/ppermute | solution.py:57
  53.3 0.0 collective-permute-start.5
  53.3 1.7 %collective-permute-start.8 = (bf16[4128,128]{1,0:T(8,128)(2,1)S(1)}, bf16[4128,128]{1,0:T(8,128)(2,1)S(1)}, u32[]{:S(2)}, u32[]{:S(2)}) collective-permute-start(bf16[4128,128]{1,0:T(8,128)(2,1)S(1)} %collective-permute-done.2.rest_2_), channel_id=1, source_target_pairs={{0,32},{1,33},{2,34},{3,35},{4,36},{5,37},{6,38},{7,39},{8,104},{9... | collective-permute-start | bytes 3170312 | tf_op jit(solution)/shard_map/ppermute | solution.py:57
  55.0 2.9 %collective-permute-start.9 = (bf16[4128,128]{1,0:T(8,128)(2,1)S(1)}, bf16[4128,128]{1,0:T(8,128)(2,1)S(1)}, u32[]{:S(2)}, u32[]{:S(2)}) collective-permute-start(bf16[4128,128]{1,0:T(8,128)(2,1)S(1)} %collective-permute-done.3.rest_4_), channel_id=1, source_target_pairs={{0,4},{1,5},{2,6},{3,7},{4,16},{5,17},{6,18},{7,19},{8,28},{9,29},... | collective-permute-start | bytes 3170312 | tf_op jit(solution)/shard_map/ppermute | solution.py:57
  57.9 0.0 collective-permute-done.6.rest_3_
  57.9 0.0 collective-permute-start.10
  57.9 0.0 collective-permute-done.7.rest_5_
  57.9 0.5 collective-permute-start.12
  58.4 0.0 collective-permute-done.5.rest_1_
  58.4 0.0 copy-done.2
  58.4 0.0 copy-done.3
  58.4 0.0 copy-done
  58.4 0.0 copy-start.1
  58.5 4.1 %head.1 = (f32[384,1024]{1,0:T(8,128)S(1)}, bf16[384,3072]{1,0:T(8,128)(2,1)S(1)}, bf16[384,1024]{1,0:T(8,128)(2,1)S(1)}, bf16[6,4128,128]{2,1,0:T(8,128)(2,1)S(1)}) custom-call(bf16[128,24,128]{2,1,0:T(8,128)(2,1)S(1)} %all_to_all.10.x_ref, f32[2,1024]{1,0:T(2,128)S(1)} %copy-done.2, bf16[2,16,128]{2,1,0:T(8,128)(2,1)S(1)} %copy-done.3, ...), custom_call_target="tpu_custom_call" | custom-call | flops 1610612736 | bytes 9437184 | tf_op jit(solution)/shard_map/head/pallas_call | solution.py:197
  62.6 4.7 %collective-permute-done.8.rest_4_ = bf16[4128,128]{1,0:T(8,128)(2,1)S(1)} collective-permute-done((bf16[4128,128]{1,0:T(8,128)(2,1)S(1)}, bf16[4128,128]{1,0:T(8,128)(2,1)S(1)}, u32[]{:S(2)}, u32[]{:S(2)}) %collective-permute-start.8) | collective-permute-done | bytes 1056800 | tf_op jit(solution)/shard_map/ppermute | solution.py:57
  67.3 2.4 %collective-permute-done.9.rest_6_ = bf16[4128,128]{1,0:T(8,128)(2,1)S(1)} collective-permute-done((bf16[4128,128]{1,0:T(8,128)(2,1)S(1)}, bf16[4128,128]{1,0:T(8,128)(2,1)S(1)}, u32[]{:S(2)}, u32[]{:S(2)}) %collective-permute-start.9) | collective-permute-done | bytes 1056800 | tf_op jit(solution)/shard_map/ppermute | solution.py:57
  69.7 0.9 collective-permute-start.11
  70.6 0.0 collective-permute-start.13
  70.6 0.0 collective-permute-done.10.rest_1_
  70.6 0.0 collective-permute-done.12.rest_5_
  70.7 2.3 %collective-permute-done.11.rest_3_ = bf16[4128,128]{1,0:T(8,128)(2,1)S(1)} collective-permute-done((bf16[4128,128]{1,0:T(8,128)(2,1)S(1)}, bf16[4128,128]{1,0:T(8,128)(2,1)S(1)}, u32[]{:S(2)}, u32[]{:S(2)}) %collective-permute-start.11) | collective-permute-done | bytes 1056800 | tf_op jit(solution)/shard_map/ppermute | solution.py:57
  72.9 1.5 %collective-permute-done.13.rest_7_ = bf16[4128,128]{1,0:T(8,128)(2,1)S(1)} collective-permute-done((bf16[4128,128]{1,0:T(8,128)(2,1)S(1)}, bf16[4128,128]{1,0:T(8,128)(2,1)S(1)}, u32[]{:S(2)}, u32[]{:S(2)}) %collective-permute-start.13) | collective-permute-done | bytes 1056800 | tf_op jit(solution)/shard_map/ppermute | solution.py:57
  74.4 0.0 copy-done.1
  74.5 11.1 %tail.1 = bf16[128,24,128]{2,1,0:T(8,128)(2,1)S(1)} custom-call(f32[384,1024]{1,0:T(8,128)S(1)} %get-tuple-element.26.x_ref, bf16[384,3072]{1,0:T(8,128)(2,1)S(1)} %get-tuple-element.27.n_ref, bf16[384,1024]{1,0:T(8,128)(2,1)S(1)} %get-tuple-element.30.act_ref, bf16[6,4128,128]{2,1,0:T(8,128)(2,1)S(1)} %get-tuple-element.31.early_ref, ...), custom_call_target="tpu_custom_call" | custom-call | flops 4831838208 | bytes 14680064 | tf_op jit(solution)/shard_map/tail/pallas_call | solution.py:292
  85.5 22.5 %all_to_all.11 = bf16[128,24,128]{2,1,0:T(8,128)(2,1)S(1)} all-to-all(bf16[128,24,128]{2,1,0:T(8,128)(2,1)S(1)} %tail.1), channel_id=1, replica_groups=mesh['seq'=16,'filt'=8] {'seq','filt'}, dimensions={0} | all-to-all | bytes 1572864 | tf_op jit(solution)/shard_map/all_to_all | solution.py:336
  108.1 0.9 slice.8
Async XLA Ops:
  0.0 10.9 %copy-start.4 = (bf16[2688,128]{1,0:T(8,128)(2,1)S(1)}, bf16[2688,128]{1,0:T(8,128)(2,1)}, u32[]{:S(2)}) copy-start(bf16[2688,128]{1,0:T(8,128)(2,1)} %param.6) | copy-start | bytes 2064388
  3.5 31.7 %collective-permute-start = (bf16[4128,128]{1,0:T(8,128)(2,1)}, bf16[4128,128]{1,0:T(8,128)(2,1)S(1)}, u32[]{:S(2)}, u32[]{:S(2)}) collective-permute-start(bf16[4128,128]{1,0:T(8,128)(2,1)} %get-tuple-element.20), channel_id=1, source_target_pairs={{0,1},{1,2},{2,3},{3,0},{4,5},{5,6},{6,7},{7,4},{8,11},{9,8},{10,9... | collective-permute-start | bytes 3170312 | tf_op jit(solution)/shard_map/ppermute | solution.py:57
  8.2 27.1 %collective-permute-start.1 = (bf16[4128,128]{1,0:T(8,128)(2,1)}, bf16[4128,128]{1,0:T(8,128)(2,1)S(1)}, u32[]{:S(2)}, u32[]{:S(2)}) collective-permute-start(bf16[4128,128]{1,0:T(8,128)(2,1)} %get-tuple-element.20), channel_id=1, source_target_pairs={{0,4},{1,5},{2,6},{3,7},{4,16},{5,17},{6,18},{7,19},{8,28},{9,29},... | collective-permute-start | bytes 3170312 | tf_op jit(solution)/shard_map/ppermute | solution.py:57
  10.9 47.5 %copy-start.2 = (f32[2,1024]{1,0:T(2,128)S(1)}, f32[2,1024]{1,0:T(2,128)}, u32[]{:S(2)}) copy-start(f32[2,1024]{1,0:T(2,128)} %gain_ref.3) | copy-start | bytes 24580
  10.9 47.5 %copy-start.3 = (bf16[2,16,128]{2,1,0:T(8,128)(2,1)S(1)}, bf16[2,16,128]{2,1,0:T(8,128)(2,1)}, u32[]{:S(2)}) copy-start(bf16[2,16,128]{2,1,0:T(8,128)(2,1)} %get-tuple-element.22.bias_ref) | copy-start | bytes 24580
  11.0 47.5 %copy-start = (bf16[2,3,1024,128]{3,2,1,0:T(8,128)(2,1)S(1)}, bf16[2,3,1024,128]{3,2,1,0:T(8,128)(2,1)}, u32[]{:S(2)}) copy-start(bf16[2,3,1024,128]{3,2,1,0:T(8,128)(2,1)} %conv_ref.5) | copy-start | bytes 4718596
  35.2 14.0 %collective-permute-start.2 = (bf16[4128,128]{1,0:T(8,128)(2,1)S(1)}, bf16[4128,128]{1,0:T(8,128)(2,1)S(1)}, u32[]{:S(2)}, u32[]{:S(2)}) collective-permute-start(bf16[4128,128]{1,0:T(8,128)(2,1)S(1)} %collective-permute-done.rest_0_), channel_id=1, source_target_pairs={{0,4},{1,5},{2,6},{3,7},{4,16},{5,17},{6,18},{7,19},{8,28},{9,29},... | collective-permute-start | bytes 3170312 | tf_op jit(solution)/shard_map/ppermute | solution.py:57
  35.2 14.1 %collective-permute-start.3 = (bf16[4128,128]{1,0:T(8,128)(2,1)S(1)}, bf16[4128,128]{1,0:T(8,128)(2,1)S(1)}, u32[]{:S(2)}, u32[]{:S(2)}) collective-permute-start(bf16[4128,128]{1,0:T(8,128)(2,1)S(1)} %collective-permute-done.rest_0_), channel_id=1, source_target_pairs={{0,1},{1,2},{2,3},{3,0},{4,5},{5,6},{6,7},{7,4},{8,11},{9,8},{10,9... | collective-permute-start | bytes 3170312 | tf_op jit(solution)/shard_map/ppermute | solution.py:57
  36.6 14.0 %collective-permute-start.4 = (bf16[4128,128]{1,0:T(8,128)(2,1)S(1)}, bf16[4128,128]{1,0:T(8,128)(2,1)S(1)}, u32[]{:S(2)}, u32[]{:S(2)}) collective-permute-start(bf16[4128,128]{1,0:T(8,128)(2,1)S(1)} %collective-permute-done.rest_0_), channel_id=1, source_target_pairs={{0,32},{1,33},{2,34},{3,35},{4,36},{5,37},{6,38},{7,39},{8,104},{9... | collective-permute-start | bytes 3170312 | tf_op jit(solution)/shard_map/ppermute | solution.py:57
  38.1 19.8 %collective-permute-start.6 = (bf16[4128,128]{1,0:T(8,128)(2,1)S(1)}, bf16[4128,128]{1,0:T(8,128)(2,1)S(1)}, u32[]{:S(2)}, u32[]{:S(2)}) collective-permute-start(bf16[4128,128]{1,0:T(8,128)(2,1)S(1)} %collective-permute-done.rest_0_), channel_id=1, source_target_pairs={{0,8},{1,9},{2,10},{3,11},{4,12},{5,13},{6,14},{7,15},{8,0},{9,1},... | collective-permute-start | bytes 3170312 | tf_op jit(solution)/shard_map/ppermute | solution.py:57
  50.7 7.3 %collective-permute-start.7 = (bf16[4128,128]{1,0:T(8,128)(2,1)S(1)}, bf16[4128,128]{1,0:T(8,128)(2,1)S(1)}, u32[]{:S(2)}, u32[]{:S(2)}) collective-permute-start(bf16[4128,128]{1,0:T(8,128)(2,1)S(1)} %collective-permute-done.3.rest_4_), channel_id=1, source_target_pairs={{0,8},{1,9},{2,10},{3,11},{4,12},{5,13},{6,14},{7,15},{8,0},{9,1},... | collective-permute-start | bytes 3170312 | tf_op jit(solution)/shard_map/ppermute | solution.py:57
  53.3 5.2 %collective-permute-start.5 = (bf16[4128,128]{1,0:T(8,128)(2,1)S(1)}, bf16[4128,128]{1,0:T(8,128)(2,1)S(1)}, u32[]{:S(2)}, u32[]{:S(2)}) collective-permute-start(bf16[4128,128]{1,0:T(8,128)(2,1)S(1)} %collective-permute-done.4.rest_2_), channel_id=1, source_target_pairs={{0,8},{1,9},{2,10},{3,11},{4,12},{5,13},{6,14},{7,15},{8,0},{9,1},... | collective-permute-start | bytes 3170312 | tf_op jit(solution)/shard_map/ppermute | solution.py:57
  53.3 14.0 %collective-permute-start.8 = (bf16[4128,128]{1,0:T(8,128)(2,1)S(1)}, bf16[4128,128]{1,0:T(8,128)(2,1)S(1)}, u32[]{:S(2)}, u32[]{:S(2)}) collective-permute-start(bf16[4128,128]{1,0:T(8,128)(2,1)S(1)} %collective-permute-done.2.rest_2_), channel_id=1, source_target_pairs={{0,32},{1,33},{2,34},{3,35},{4,36},{5,37},{6,38},{7,39},{8,104},{9... | collective-permute-start | bytes 3170312 | tf_op jit(solution)/shard_map/ppermute | solution.py:57
  55.0 14.7 %collective-permute-start.9 = (bf16[4128,128]{1,0:T(8,128)(2,1)S(1)}, bf16[4128,128]{1,0:T(8,128)(2,1)S(1)}, u32[]{:S(2)}, u32[]{:S(2)}) collective-permute-start(bf16[4128,128]{1,0:T(8,128)(2,1)S(1)} %collective-permute-done.3.rest_4_), channel_id=1, source_target_pairs={{0,4},{1,5},{2,6},{3,7},{4,16},{5,17},{6,18},{7,19},{8,28},{9,29},... | collective-permute-start | bytes 3170312 | tf_op jit(solution)/shard_map/ppermute | solution.py:57
  57.9 12.7 %collective-permute-start.10 = (bf16[4128,128]{1,0:T(8,128)(2,1)S(1)}, bf16[4128,128]{1,0:T(8,128)(2,1)S(1)}, u32[]{:S(2)}, u32[]{:S(2)}) collective-permute-start(bf16[4128,128]{1,0:T(8,128)(2,1)S(1)} %collective-permute-done.1.rest_0_), channel_id=1, source_target_pairs={{0,8},{1,9},{2,10},{3,11},{4,12},{5,13},{6,14},{7,15},{8,0},{9,1},... | collective-permute-start | bytes 3170312 | tf_op jit(solution)/shard_map/ppermute | solution.py:57
  57.9 12.7 %collective-permute-start.12 = (bf16[4128,128]{1,0:T(8,128)(2,1)S(1)}, bf16[4128,128]{1,0:T(8,128)(2,1)S(1)}, u32[]{:S(2)}, u32[]{:S(2)}) collective-permute-start(bf16[4128,128]{1,0:T(8,128)(2,1)S(1)} %collective-permute-done.2.rest_2_), channel_id=1, source_target_pairs={{0,8},{1,9},{2,10},{3,11},{4,12},{5,13},{6,14},{7,15},{8,0},{9,1},... | collective-permute-start | bytes 3170312 | tf_op jit(solution)/shard_map/ppermute | solution.py:57
  58.4 16.0 %copy-start.1 = (bf16[2,1024,128]{2,1,0:T(8,128)(2,1)S(1)}, bf16[2,1024,128]{2,1,0:T(8,128)(2,1)}, u32[]{:S(2)}) copy-start(bf16[2,1024,128]{2,1,0:T(8,128)(2,1)} %mix_ref.3) | copy-start | bytes 1572868
  69.7 3.2 %collective-permute-start.11 = (bf16[4128,128]{1,0:T(8,128)(2,1)S(1)}, bf16[4128,128]{1,0:T(8,128)(2,1)S(1)}, u32[]{:S(2)}, u32[]{:S(2)}) collective-permute-start(bf16[4128,128]{1,0:T(8,128)(2,1)S(1)} %collective-permute-done.8.rest_4_), channel_id=1, source_target_pairs={{0,8},{1,9},{2,10},{3,11},{4,12},{5,13},{6,14},{7,15},{8,0},{9,1},... | collective-permute-start | bytes 3170312 | tf_op jit(solution)/shard_map/ppermute | solution.py:57
  70.6 3.8 %collective-permute-start.13 = (bf16[4128,128]{1,0:T(8,128)(2,1)S(1)}, bf16[4128,128]{1,0:T(8,128)(2,1)S(1)}, u32[]{:S(2)}, u32[]{:S(2)}) collective-permute-start(bf16[4128,128]{1,0:T(8,128)(2,1)S(1)} %collective-permute-done.9.rest_6_), channel_id=1, source_target_pairs={{0,8},{1,9},{2,10},{3,11},{4,12},{5,13},{6,14},{7,15},{8,0},{9,1},... | collective-permute-start | bytes 3170312 | tf_op jit(solution)/shard_map/ppermute | solution.py:57
